TPU v7x, 32 devices: a whole 2x2x4 slice. The times are simulated.
32 devices in a mesh: batch: 8 (over y, x, core), grp: 4 (over z).
Axes of the slice: x: 2, y: 2, z: 4, core: 2. Of those that a mesh axis runs over, the one named last changes fastest.
Arguments:
- latents: bfloat16 [16, 32, 32, 768], P('batch', 'grp'), may hold values from -6 to 6
- cotangent: bfloat16 [16, 32, 32, 768], P('batch', 'grp'), may hold values from -6 to 6
- timesteps: int32 [16], P('batch'), may hold values from 0 to 999, as said below
- labels: int32 [16], P('batch'), may hold values from 0 to 999
- time_weight: bfloat16 [256, 768], replicated, may hold values from -0.375 to 0.375
- time_bias: bfloat16 [1, 768], replicated, may hold values from -3 to 3
- label_table: bfloat16 [1000, 768], replicated, may hold values from -6 to 6
- ada_weight: bfloat16 [768, 4608], replicated, may hold values from -0.21875 to 0.21875
- ada_bias: bfloat16 [1, 4608], replicated, may hold values from -3 to 3
- conv_a: bfloat16 [9, 768], replicated, may hold values from -2 to 2
- conv_a_bias: bfloat16 [1, 768], replicated, may hold values from -3 to 3
- qkv_weight: bfloat16 [768, 2304], replicated, may hold values from -0.21875 to 0.21875
- qv_bias: bfloat16 [2, 768], replicated, may hold values from -3 to 3
- proj_weight: bfloat16 [768, 768], replicated, may hold values from -0.875 to 0.875
- proj_bias: bfloat16 [1, 768], replicated, may hold values from -3 to 3
- fc1_weight: bfloat16 [768, 3072], replicated, may hold values from -0.21875 to 0.21875
- fc1_bias: bfloat16 [1, 3072], replicated, may hold values from -3 to 3
- conv_f: bfloat16 [9, 3072], replicated, may hold values from -2 to 2
- conv_f_bias: bfloat16 [1, 3072], replicated, may hold values from -3 to 3
- fc2_weight: bfloat16 [3072, 768], replicated, may hold values from -0.109375 to 0.109375
- fc2_bias: bfloat16 [1, 768], replicated, may hold values from -3 to 3
Outputs:
- output: bfloat16 [16, 32, 32, 768], P('batch', 'grp')
- latents_grad: bfloat16 [16, 32, 32, 768], P('batch', 'grp')
- time_weight_grad: float32 [256, 768], P(None, ('batch', 'grp'))
- time_bias_grad: float32 [1, 768], P(None, ('batch', 'grp'))
- label_table_grad: float32 [1000, 768], P(None, ('batch', 'grp'))
- ada_weight_grad: float32 [768, 4608], P(None, ('batch', 'grp'))
- ada_bias_grad: float32 [1, 4608], P(None, ('batch', 'grp'))
- conv_a_grad: float32 [9, 768], P(None, ('batch', 'grp'))
- conv_a_bias_grad: float32 [1, 768], P(None, ('batch', 'grp'))
- qkv_weight_grad: float32 [768, 2304], P(None, ('batch', 'grp'))
- qv_bias_grad: float32 [2, 768], P(None, ('batch', 'grp'))
- proj_weight_grad: float32 [768, 768], P(None, ('batch', 'grp'))
- proj_bias_grad: float32 [1, 768], P(None, ('batch', 'grp'))
- fc1_weight_grad: float32 [768, 3072], P(None, ('batch', 'grp'))
- fc1_bias_grad: float32 [1, 3072], P(None, ('batch', 'grp'))
- conv_f_grad: float32 [9, 3072], P(None, ('batch', 'grp'))
- conv_f_bias_grad: float32 [1, 3072], P(None, ('batch', 'grp'))
- fc2_weight_grad: float32 [3072, 768], P(None, ('batch', 'grp'))
- fc2_bias_grad: float32 [1, 768], P(None, ('batch', 'grp'))
Inputs may be any that keep to these rules, and one draw needn't show every extreme that they name: `timesteps`: diffusion timestep of each latent, more often low than high; some latent has timestep 999 and some has 0.
All inputs are finite; a program needn't handle non-finite values.
Results may differ from a plain program's by a relative error of at most 0.018.
The roundings to bfloat16 on the way count: a program that leaves them out, or rounds other values in their place, can miss the bound.
Values may be sent and summed in bfloat16 or wider, within the bound.
No kernel may reach another device: no remote copies, remote signals or barrier semaphores. Data moves between devices by JAX's collectives and lax.ppermute only.
A program may use at most 192 MiB of HBM per device.

v0:
```python
import math

import jax
import jax.numpy as jnp
from jax import lax
from jax.experimental import pallas as pl
from jax.experimental.pallas import tpu as pltpu
from jax.sharding import PartitionSpec as P


HEAD = 64
BATCH, GRP = "batch", "grp"
HIGHEST = lax.Precision.HIGHEST
F32 = jnp.float32
BF16 = jnp.bfloat16
GELU_C = math.sqrt(2.0 / math.pi)


def swap_bit(value, axis, bit):
    count = lax.axis_size(axis)
    return lax.ppermute(value, axis, [(i, i ^ (1 << bit)) for i in range(count)])


def to_pairs(block):
    strip = lax.axis_index(GRP)
    odd = strip & 1
    arrived = []
    for k in range(2):
        piece = lax.dynamic_slice_in_dim(block, k ^ odd, 1, axis=0)
        arrived.append(lax.ppermute(piece, (BATCH, GRP), pair_moves(k)))
    swapped = odd == 1
    upper = jnp.where(swapped, arrived[1], arrived[0])
    lower = jnp.where(swapped, arrived[0], arrived[1])
    return jnp.concatenate([upper, lower], axis=1)


def pair_moves(k, back=False):
    strips = lax.axis_size(GRP)
    moves = []
    for b in range(lax.axis_size(BATCH)):
        for z in range(strips):
            to = (2 * (b // 2) + (z >> 1)) * strips + 2 * (b & 1) + (k ^ (z & 1))
            moves.append((to, b * strips + z) if back else (b * strips + z, to))
    return moves


def from_pairs(block):
    rows = block.shape[1] // 2
    odd = lax.axis_index(GRP) & 1
    arrived = []
    for k in range(2):
        piece = lax.dynamic_slice_in_dim(block, (k ^ odd) * rows, rows, axis=1)
        arrived.append(lax.ppermute(piece, (BATCH, GRP), pair_moves(k, True)))
    swapped = odd == 1
    first = jnp.where(swapped, arrived[1], arrived[0])
    second = jnp.where(swapped, arrived[0], arrived[1])
    return jnp.concatenate([first, second], axis=0)


def with_edges(block, width):
    rows = block.shape[1]
    lower = (lax.axis_index(BATCH) & 1) == 1
    edge = jnp.where(lower, block[:, :width], block[:, rows - width :])
    other = swap_bit(edge, BATCH, 0)
    zero = jnp.zeros_like(other)
    return jnp.concatenate([jnp.where(lower, other, zero), block, jnp.where(lower, zero, other)], axis=1)


def halve(here, away, axis, bit):
    arrived = swap_bit(away, axis, bit)
    return here.astype(F32) + arrived.astype(F32)


def halve_dim(block, place, axis, bit):
    mine = (lax.axis_index(axis) >> bit) & 1
    away = lax.dynamic_index_in_dim(block, 1 - mine, place, keepdims=False)
    here = lax.dynamic_index_in_dim(block, mine, place, keepdims=False)
    return halve(here, away, axis, bit)


def scatter_rest(block, swapped):
    high = list(range(1, lax.axis_size(BATCH).bit_length() - 1))
    left = high[::-1]
    _, rows, width = block.shape
    block = block.reshape((2,) * len(high) + (rows, width))
    for bit in high[::-1] if swapped else high:
        block = halve_dim(block.astype(BF16), left.index(bit), BATCH, bit)
        left.remove(bit)
    bits = lax.axis_size(GRP).bit_length() - 1
    block = block.reshape((2,) * bits + (-1, width))
    for bit in range(bits):
        block = halve_dim(block.astype(BF16), bits - 1 - bit, GRP, bit)
    return block


def scatter_sum(block, swapped):
    pairs = lax.axis_size(BATCH) // 2
    width = block.shape[-1]
    block = halve_dim(block.reshape(pairs, 2, -1, width), 1, BATCH, 0)
    return scatter_rest(block, swapped)


def gather_sum(rows, pair_rows, summed):
    bits = [(BATCH, bit) for bit in range(1, lax.axis_size(BATCH).bit_length() - 1)]
    bits += [(GRP, bit) for bit in range(lax.axis_size(GRP).bit_length() - 1)]
    length = pair_rows.shape[0]
    both = jnp.concatenate([pair_rows, summed], axis=0)
    other = swap_bit(both, BATCH, 0)
    both = both + other
    rows = jnp.concatenate([both[:length], rows], axis=0)
    summed = both[length:]
    for axis, bit in bits:
        sent = jnp.concatenate([summed, rows], axis=0)
        other = swap_bit(sent, axis, bit)
        summed = summed + other[: len(summed)]
        rows = jnp.concatenate([rows, other[len(summed) :]], axis=0)
    return rows, summed


def exact_dot(left, right):
    high = lax.reduce_precision(left, 8, 7)
    rest = left - high
    middle = lax.reduce_precision(rest, 8, 7)
    low = rest - middle
    rows = jnp.concatenate([high, middle, low], axis=0).astype(BF16)
    out = jnp.dot(rows, right, preferred_element_type=F32)
    count = left.shape[0]
    return out[:count] + (out[count : 2 * count] + out[2 * count :])


def sinusoid(timestep, length):
    halfway = length // 2
    frequency = jnp.exp(-math.log(10000.0) * jnp.arange(halfway, dtype=F32) / halfway)
    angles = timestep.astype(F32)[:, None] * frequency[None, :]
    return jnp.concatenate([jnp.cos(angles), jnp.sin(angles)], axis=1)


def unit_pull(unit, inverse, grad):
    first = jnp.mean(grad, axis=-1, keepdims=True)
    second = jnp.mean(grad * unit, axis=-1, keepdims=True)
    return inverse * (grad - first - unit * second)


def row_shift(values, step):
    cols = values.shape[0]
    place = lax.broadcasted_iota(jnp.int32, values.shape, 0)
    rolled = pltpu.roll(values, step % cols, 0)
    return jnp.where(place == (0 if step == 1 else cols - 1), 0.0, rolled)


def fold_rows(values):
    total = values[0:8]
    for start in range(8, values.shape[0], 8):
        total = total + values[start : start + 8]
    return total


def feed_forward_body(
    place, normed, upstream, fc1, fc1_bias, taps, conv_bias, fc2,
    branch_out, normed_grad_out, fc1_here, fc1_away, fc2_here, fc2_away, small_out,
    hidden, lifted, activated, convolved_grad, hidden_grad, fc1_grad, fc2_grad,
):
    count, rim_rows, cols, width = normed.shape
    rows = rim_rows - 4
    tile = fc1.shape[1]
    lanes = 128
    raw = jnp.dot(
        normed[...].reshape(count * rim_rows * cols, width), fc1[...], preferred_element_type=F32
    ) + fc1_bias[...].astype(F32)
    hidden[...] = raw.astype(BF16).astype(F32).reshape(count, rim_rows, cols, tile)
    hidden[:, 0:2] = hidden[:, 0:2] * place[1].astype(F32)
    hidden[:, rows + 2 :] = hidden[:, rows + 2 :] * place[2].astype(F32)
    lifted[...] = lax.dot_general(
        upstream[...].reshape(count * (rows + 2) * cols, width),
        fc2[...],
        (((1,), (1,)), ((), ())),
        preferred_element_type=F32,
    ).reshape(count, rows + 2, cols, tile)
    for start in range(0, tile, lanes):
        here = slice(start, start + lanes)
        tap = [taps[k : k + 1, here].astype(F32) for k in range(9)]
        bias = conv_bias[:, here].astype(F32)

        def forward_row(l, r, sums):
            near = [hidden[l, r + a, :, here] for a in range(3)]
            parts = [sum(tap[3 * a + e] * near[a] for a in range(3)) for e in range(3)]
            value = row_shift(parts[0], 1) + parts[1] + row_shift(parts[2], -1) + bias
            square = value * value
            bent = jnp.tanh(value * (GELU_C + GELU_C * 0.044715 * square))
            half = 0.5 * (1.0 + bent)
            activated[l, r, :, here] = (value * half).astype(BF16)
            slope = half + value * half * (1.0 - bent) * (GELU_C + 3.0 * 0.044715 * GELU_C * square)
            grad = (lifted[l, r, :, here] * slope).astype(BF16).astype(F32)
            convolved_grad[l, r, :, here] = grad
            if sums is None:
                return None
            moved = [row_shift(grad, -1), grad, row_shift(grad, 1)]
            added = [sums[3 * a + e] + fold_rows(near[a] * moved[e]) for a in range(3) for e in range(3)]
            return tuple(added) + (sums[9] + fold_rows(grad),)

        sums = tuple(jnp.zeros((8, lanes), F32) for _ in range(10))
        bias_sum = jnp.zeros((8, lanes), F32)
        for l in range(count):
            forward_row(l, 0, None)
            forward_row(l, rows + 1, None)
            sums = lax.fori_loop(1, rows + 1, lambda r, sums, l=l: forward_row(l, r, sums), sums)

            def backward_row(r, bias_sum, l=l):
                near = [convolved_grad[l, r + 2 - a, :, here] for a in range(3)]
                parts = [sum(tap[3 * a + e] * near[a] for a in range(3)) for e in range(3)]
                value = row_shift(parts[0], -1) + parts[1] + row_shift(parts[2], 1)
                rounded = value.astype(BF16)
                hidden_grad[l, r, :, here] = rounded
                return bias_sum + fold_rows(rounded.astype(F32))

            bias_sum = lax.fori_loop(0, rows, backward_row, bias_sum)
        for k in range(10):
            small_out[k : k + 1, here] = jnp.sum(sums[k], axis=0, keepdims=True)
        small_out[10:11, here] = jnp.sum(bias_sum, axis=0, keepdims=True)
    tokens = count * rows * cols
    active = activated[:, 1 : rows + 1].reshape(tokens, tile)
    back = hidden_grad[...].reshape(tokens, tile)
    inner = normed[:, 2 : rows + 2].reshape(tokens, width)
    above = upstream[:, 1 : rows + 1].reshape(tokens, width)

    @pl.when(pl.program_id(0) == 0)
    def _():
        branch_out[...] = jnp.zeros_like(branch_out)
        normed_grad_out[...] = jnp.zeros_like(normed_grad_out)

    branch_out[...] += jnp.dot(active, fc2[...], preferred_element_type=F32)
    normed_grad_out[...] += lax.dot_general(
        back, fc1[...], (((1,), (1,)), ((), ())), preferred_element_type=F32
    )
    me = place[0]
    fc1_grad[...] = lax.dot_general(
        back, inner, (((0,), (0,)), ((), ())), preferred_element_type=F32
    ).astype(BF16).reshape(fc1_grad.shape)
    for j in range(fc1_grad.shape[0]):
        fc1_here[0, j] = fc1_grad[j, me]
        fc1_away[0, j] = fc1_grad[j, 1 - me]
    fc2_grad[...] = lax.dot_general(
        above, active, (((0,), (0,)), ((), ())), preferred_element_type=F32
    ).reshape(fc2_grad.shape)
    for j in range(fc2_grad.shape[0]):
        fc2_here[j] = fc2_grad[j, me].astype(BF16)
        fc2_away[j] = fc2_grad[j, 1 - me].astype(BF16)


def feed_forward(place, normed, upstream, fc1, fc1_bias, taps, conv_bias, fc2):
    count, rim_rows, cols, width = normed.shape
    rows = rim_rows - 4
    tokens = count * rows * cols
    units = fc1.shape[1]
    tile = 768
    steps = units // tile
    batch = lax.axis_size(BATCH)
    fc1_block = (1, batch // 2 // steps, units // batch, width)
    fc2_block = (batch // 2, width // batch, tile)
    return pl.pallas_call(
        feed_forward_body,
        grid=(steps,),
        in_specs=[
            pl.BlockSpec(memory_space=pltpu.SMEM),
            pl.BlockSpec(normed.shape, lambda i: (0, 0, 0, 0)),
            pl.BlockSpec(upstream.shape, lambda i: (0, 0, 0, 0)),
            pl.BlockSpec((width, tile), lambda i: (0, i)),
            pl.BlockSpec((1, tile), lambda i: (0, i)),
            pl.BlockSpec((9, tile), lambda i: (0, i)),
            pl.BlockSpec((1, tile), lambda i: (0, i)),
            pl.BlockSpec((tile, width), lambda i: (i, 0)),
        ],
        out_specs=[
            pl.BlockSpec((tokens, width), lambda i: (0, 0)),
            pl.BlockSpec((tokens, width), lambda i: (0, 0)),
            pl.BlockSpec(fc1_block, lambda i: (i, 0, 0, 0)),
            pl.BlockSpec(fc1_block, lambda i: (i, 0, 0, 0)),
            pl.BlockSpec(fc2_block, lambda i: (0, 0, i)),
            pl.BlockSpec(fc2_block, lambda i: (0, 0, i)),
            pl.BlockSpec((16, tile), lambda i: (0, i)),
        ],
        out_shape=[
            jax.ShapeDtypeStruct((tokens, width), F32),
            jax.ShapeDtypeStruct((tokens, width), F32),
            jax.ShapeDtypeStruct((steps,) + fc1_block[1:], BF16),
            jax.ShapeDtypeStruct((steps,) + fc1_block[1:], BF16),
            jax.ShapeDtypeStruct(fc2_block[:2] + (units,), BF16),
            jax.ShapeDtypeStruct(fc2_block[:2] + (units,), BF16),
            jax.ShapeDtypeStruct((16, units), F32),
        ],
        scratch_shapes=[
            pltpu.VMEM((count, rim_rows, cols, tile), F32),
            pltpu.VMEM((count, rows + 2, cols, tile), F32),
            pltpu.VMEM((count, rows + 2, cols, tile), BF16),
            pltpu.VMEM((count, rows + 2, cols, tile), F32),
            pltpu.VMEM((count, rows, cols, tile), BF16),
            pltpu.VMEM((fc1_block[1], 2) + fc1_block[2:], BF16),
            pltpu.VMEM((batch // 2, 2, width // batch, tile), F32),
        ],
        compiler_params=pltpu.CompilerParams(
            dimension_semantics=("arbitrary",), vmem_limit_bytes=48 * 1024 * 1024
        ),
        name="feed_forward",
    )(place, normed, upstream, fc1, fc1_bias, taps, conv_bias, fc2)


def layer_unit(values):
    centre = jnp.mean(values, axis=-1, keepdims=True)
    centred = values - centre
    inverse = lax.rsqrt(jnp.mean(centred * centred, axis=-1, keepdims=True) + 1e-06)
    return centred * inverse, inverse


def chunked(count, rows, cols, width):
    return (count, rows, width // 128, cols, 128)


def half_rows(start):
    return pl.ds(start, 16, stride=2)


def pack_strips(values, outs, me):
    _, rows, chunks, _, lanes = values.shape

    def one(i, carry):
        for s, out in enumerate(outs):
            row = 2 * i + (me ^ s)
            for q in range(2):
                for c in range(chunks):
                    out[q, i, :, c * lanes : (c + 1) * lanes] = values[0, row, c, half_rows(q), :].astype(BF16)
        return carry

    lax.fori_loop(0, rows // 2, one, 0)


def unpack_strips(parts, values, me, first):
    halves = parts[0].shape[1]
    chunks, _, lanes = values.shape[2:]

    def one(i, carry):
        for s, part in enumerate(parts):
            row = 2 * i + (me ^ s ^ first)
            for q in range(2):
                full = part[q, i].astype(F32)
                for c in range(chunks):
                    values[0, row, c, half_rows(q), :] = full[:, c * lanes : (c + 1) * lanes]
        return carry

    lax.fori_loop(0, halves, one, 0)


def stem_body(place, latents, modulation, taps, conv_bias, out0, out1, normed, mixed):
    count, rim_rows, cols, width = normed.shape
    rows = rim_rows - 2
    lanes = 128
    for l in range(count):
        offset = modulation[l : l + 1, 0:width]
        scaling = 1.0 + modulation[l : l + 1, width : 2 * width]

        def norm_row(r, carry, l=l, offset=offset, scaling=scaling):
            for h in range(0, cols, 16):
                unit, _ = layer_unit(latents[l, r + 1, h : h + 16].astype(F32))
                normed[l, r, h : h + 16] = (unit * scaling + offset).astype(BF16).astype(F32)
            return carry

        lax.fori_loop(0, rim_rows, norm_row, 0)
        normed[l, 0] = normed[l, 0] * place[1].astype(F32)
        normed[l, rows + 1] = normed[l, rows + 1] * place[2].astype(F32)
    for start in range(0, width, lanes):
        here = slice(start, start + lanes)
        tap = [taps[k : k + 1, here].astype(F32) for k in range(9)]
        bias = conv_bias[:, here].astype(F32)
        for l in range(count):

            def conv_row(r, carry, l=l, here=here, tap=tap, bias=bias):
                near = [normed[l, r + a, :, here] for a in range(3)]
                parts = [sum(tap[3 * a + e] * near[a] for a in range(3)) for e in range(3)]
                total = row_shift(parts[0], 1) + parts[1] + row_shift(parts[2], -1) + bias
                mixed[l, r, here.start // lanes] = total
                return carry

            lax.fori_loop(0, rows, conv_row, 0)
    pack_strips(mixed, (out0, out1), place[0])


WHOLE = pl.BlockSpec(memory_space=pltpu.VMEM)
SCALARS = pl.BlockSpec(memory_space=pltpu.SMEM)


def call_whole(body, inputs, outputs, scratch):
    return pl.pallas_call(
        body,
        in_specs=[SCALARS] + [WHOLE] * (len(inputs) - 1),
        out_specs=[WHOLE] * len(outputs),
        out_shape=[jax.ShapeDtypeStruct(shape, kind) for shape, kind in outputs],
        scratch_shapes=[pltpu.VMEM(shape, kind) for shape, kind in scratch],
        compiler_params=pltpu.CompilerParams(vmem_limit_bytes=56 * 1024 * 1024),
    )(*inputs)


def stem(place, latents_rim, modulation, taps, conv_bias):
    count, rim_rows, cols, width = latents_rim.shape
    rows = rim_rows - 4
    return call_whole(
        stem_body,
        (place, latents_rim, modulation, taps, conv_bias),
        [((2, rows // 2, cols // 2, width), BF16)] * 2,
        [((count, rows + 2, cols, width), F32), (chunked(count, rows, cols, width), F32)],
    )


def head_mask(lanes, h):
    lane = lax.broadcasted_iota(jnp.int32, (1, lanes), 1)
    return (lane >= h * HEAD) & (lane < (h + 1) * HEAD)


def attend_body(place, part0, part1, weight, bias, out0, out1, projected, log_totals, gathered, attended):
    parts = (part0, part1)
    count, halves, cols, width = part0.shape
    block = halves * cols
    tokens = len(parts) * block
    me = place[0]
    for l in range(count):
        for s, part in enumerate(parts):
            gathered[l, s * block : (s + 1) * block] = part[l].reshape(block, width)
    raw = jnp.dot(gathered[...].reshape(count * tokens, width), weight[...], preferred_element_type=F32)
    projected[...] = (raw + bias[...].astype(F32)).astype(BF16).reshape(count, tokens, 3 * width)
    log_totals[...] = jnp.zeros_like(log_totals)
    lanes = 2 * HEAD
    lane = lax.broadcasted_iota(jnp.int32, (1, lanes), 1)
    for l in range(count):

        def pair(n, carry, l=l):
            start = pl.multiple_of(n * lanes, lanes)
            query = projected[l, :, pl.ds(start, lanes)].astype(F32) * HEAD ** (-0.5)
            key = projected[l, :, pl.ds(pl.multiple_of(width + n * lanes, lanes), lanes)]
            value = projected[l, :, pl.ds(pl.multiple_of(2 * width + n * lanes, lanes), lanes)]
            total_rows = log_totals[l]
            mixed = []
            for h in range(2):
                masked = jnp.where(head_mask(lanes, h), query, 0.0).astype(BF16)
                scores = lax.dot_general(masked, key, (((1,), (1,)), ((), ())), preferred_element_type=F32)
                highest = jnp.max(scores, axis=-1, keepdims=True)
                raised = jnp.exp(scores - highest)
                totals = jnp.sum(raised, axis=-1, keepdims=True)
                weights = (raised * (1.0 / totals)).astype(BF16)
                mixed.append(jnp.dot(weights, value, preferred_element_type=F32))
                total_rows = jnp.where(lane == 2 * n + h, highest + jnp.log(totals), total_rows)
            log_totals[l] = total_rows
            both = jnp.where(head_mask(lanes, 0), mixed[0], mixed[1]).astype(BF16)
            attended[l, :, :, pl.ds(start, lanes)] = both.reshape(len(parts) * halves, cols, lanes)
            return carry

        lax.fori_loop(0, width // lanes, pair, 0)
    send_rows(attended, (out0, out1), me, halves, 1, 0)


def send_rows(values, outs, me, halves, before, shift):
    count, total = values.shape[:2]
    for s, out in enumerate(outs):
        strip = me ^ s
        for k in range(out.shape[1]):
            row = strip * halves - before + shift + k
            inside = ((row >= 0) & (row < total)).astype(F32)
            kept = jnp.clip(row, 0, total - 1)
            source = (me ^ (kept // halves)) * halves + kept % halves
            for l in range(count):
                out[l, k] = (values[l, source].astype(F32) * inside).astype(BF16)


def attend(place, parts, weight, bias):
    count, halves, cols, width = parts[0].shape
    tokens = len(parts) * halves * cols
    return call_whole(
        attend_body,
        (place, *parts, weight, bias),
        [((count, halves + 2, cols, width), BF16)] * 2
        + [((count, tokens, 3 * width), BF16), ((count, tokens, 2 * HEAD), F32)],
        [((count, tokens, width), BF16), ((count, len(parts) * halves, cols, width), BF16)],
    )


def middle_body(place, part0, part1, latents, modulation, weight, bias, normed, attended, branch, spread, rimmed, raw):
    count, rim_rows, cols, width = latents.shape
    rows = rim_rows - 4
    unpack_strips((part0, part1), spread, place[0], 0)
    for c in range(width // 128):
        rimmed[:, :, :, c * 128 : (c + 1) * 128] = spread[:, :, c].astype(BF16)
    attended[...] = rimmed[:, 2 : rows + 2]
    every = rimmed[...].reshape(count * rim_rows * cols, width)
    dotted = jnp.dot(every, weight[...], preferred_element_type=F32) + bias[...].astype(F32)
    raw[...] = dotted.reshape(count, rim_rows, cols, width)
    branch[...] = raw[:, 2 : rows + 2]
    for l in range(count):
        gate = modulation[l : l + 1, 2 * width : 3 * width]
        offset = modulation[l : l + 1, 3 * width : 4 * width]
        scaling = 1.0 + modulation[l : l + 1, 4 * width : 5 * width]

        def norm_row(r, carry, l=l, gate=gate, offset=offset, scaling=scaling):
            for h in range(0, cols, 16):
                middle = latents[l, r, h : h + 16].astype(F32) + gate * raw[l, r, h : h + 16]
                unit, _ = layer_unit(middle)
                normed[l, r, h : h + 16] = (unit * scaling + offset).astype(BF16)
            return carry

        lax.fori_loop(0, rim_rows, norm_row, 0)


def middle_part(place, parts, latents_rim, modulation, weight, bias):
    count, rim_rows, cols, width = latents_rim.shape
    rows = rim_rows - 4
    return call_whole(
        middle_body,
        (place, *parts, latents_rim, modulation, weight, bias),
        [
            (latents_rim.shape, BF16),
            ((count, rows, cols, width), BF16),
            ((count, rows, cols, width), F32),
        ],
        [(chunked(*latents_rim.shape), F32), (latents_rim.shape, BF16), (latents_rim.shape, F32)],
    )


def turn_body(
    place, branch_two, normed_grad, branch_one, attended, latents, cotangent, modulation, fc2_bias, weight,
    output, middle_grad, weight_grad, sums, bias_sums, out0, out1, branch_grad, spread,
):
    count, rows, cols, width = cotangent.shape
    bias_sums[...] = jnp.zeros_like(bias_sums)
    sums[...] = jnp.zeros_like(sums)
    for l in range(count):
        gate_one, _, scaling, gate_two = (
            modulation[l : l + 1, k * width : (k + 1) * width] for k in range(2, 6)
        )
        scaling = 1.0 + scaling

        def one_row(r, carry, l=l, gate_one=gate_one, scaling=scaling, gate_two=gate_two):
            for h in range(0, cols, 16):
                here = slice(h, h + 16)
                first = branch_one[l, r, here]
                second = branch_two[l, r, here] + fc2_bias[...].astype(F32)
                upstream = cotangent[l, r, here].astype(F32)
                middle = latents[l, r + 2, here].astype(F32) + gate_one * first
                output[l, r, here] = (middle + gate_two * second).astype(BF16)
                unit, inverse = layer_unit(middle)
                grad = normed_grad[l, r, here]
                pulled = upstream + unit_pull(unit, inverse, grad * scaling)
                middle_grad[l, r, here] = pulled
                rounded = (gate_one * pulled).astype(BF16)
                branch_grad[l, r, here] = rounded
                sums[l, 0] += fold_rows(pulled * first)
                sums[l, 1] += fold_rows(grad)
                sums[l, 2] += fold_rows(grad * unit)
                sums[l, 3] += fold_rows(upstream * second)
                bias_sums[0] += fold_rows(rounded.astype(F32))
                bias_sums[1] += fold_rows((gate_two * upstream).astype(BF16).astype(F32))
            return carry

        lax.fori_loop(0, rows, one_row, 0)
    tokens = count * rows * cols
    back = branch_grad[...].reshape(tokens, width)
    weight_grad[...] = lax.dot_general(
        back, attended[...].reshape(tokens, width), (((0,), (0,)), ((), ())), preferred_element_type=F32
    ).astype(BF16)
    raw = lax.dot_general(back, weight[...], (((1,), (1,)), ((), ())), preferred_element_type=F32)
    for c in range(width // 128):
        spread[:, :, c] = raw[:, c * 128 : (c + 1) * 128].reshape(count, rows, cols, 128)
    pack_strips(spread, (out0, out1), place[0])


def turn(place, branch_two, normed_grad, branch_one, attended, latents_rim, cotangent, modulation, fc2_bias, weight):
    count, rows, cols, width = cotangent.shape
    return call_whole(
        turn_body,
        (place, branch_two, normed_grad, branch_one, attended, latents_rim, cotangent, modulation, fc2_bias, weight),
        [
            (cotangent.shape, BF16),
            (cotangent.shape, F32),
            ((width, width), BF16),
            ((count, 4, 8, width), F32),
            ((2, 8, width), F32),
        ]
        + [((2, rows // 2, cols // 2, width), BF16)] * 2,
        [(cotangent.shape, BF16), (chunked(*cotangent.shape), F32)],
    )


def attend_back_body(
    place, up0, up1, part0, part1, projected, log_totals, weight,
    weight_grad, bias_sums, out0, out1, gathered, upstream, grads, spread,
):
    parts = (part0, part1)
    count, halves, cols, width = part0.shape
    block = halves * cols
    tokens = len(parts) * block
    me = place[0]
    for l in range(count):
        for s, (part, up) in enumerate(zip(parts, (up0, up1))):
            gathered[l, s * block : (s + 1) * block] = part[l].reshape(block, width)
            upstream[l, s * block : (s + 1) * block] = up[l].reshape(block, width)
    bias_sums[...] = jnp.zeros_like(bias_sums)
    lanes = 2 * HEAD
    lane = lax.broadcasted_iota(jnp.int32, (1, lanes), 1)
    turned = (((0,), (0,)), ((), ()))
    inner = (((1,), (1,)), ((), ()))
    for l in range(count):

        def pair(n, carry, l=l):
            here = [pl.ds(pl.multiple_of(k * width + n * lanes, lanes), lanes) for k in range(3)]
            query = projected[l, :, here[0]]
            key = projected[l, :, here[1]]
            value = projected[l, :, here[2]]
            up = upstream[l, :, here[0]]
            query_full = query.astype(F32) * HEAD ** (-0.5)
            up_full = up.astype(F32)
            found = []
            for h in range(2):
                mask = head_mask(lanes, h)
                total = jnp.sum(jnp.where(lane == 2 * n + h, log_totals[l], 0.0), axis=-1, keepdims=True)
                masked = jnp.where(mask, query_full, 0.0).astype(BF16)
                scores = lax.dot_general(masked, key, inner, preferred_element_type=F32)
                weights = jnp.exp(scores - total)
                value_grad = lax.dot_general(weights.astype(BF16), up, turned, preferred_element_type=F32)
                weight_side = lax.dot_general(
                    jnp.where(mask, up_full, 0.0).astype(BF16), value, inner, preferred_element_type=F32
                )
                weighted = jnp.sum(weights * weight_side, axis=-1, keepdims=True)
                score_grad = (weights * (weight_side - weighted)).astype(BF16)
                query_grad = jnp.dot(score_grad, key, preferred_element_type=F32) * HEAD ** (-0.5)
                key_grad = lax.dot_general(score_grad, query, turned, preferred_element_type=F32) * HEAD ** (-0.5)
                found.append((query_grad, key_grad, value_grad))
            mask = head_mask(lanes, 0)
            for k in range(3):
                both = jnp.where(mask, found[0][k], found[1][k]).astype(BF16)
                grads[l, :, here[k]] = both
                if k != 1:
                    bias_sums[k // 2, :, here[0]] += fold_rows(both.astype(F32))
            return carry

        lax.fori_loop(0, width // lanes, pair, 0)
    every = grads[...].reshape(count * tokens, 3 * width)
    weight_grad[...] = lax.dot_general(
        every, gathered[...].reshape(count * tokens, width), turned, preferred_element_type=F32
    ).astype(BF16)
    raw = lax.dot_general(every, weight[...], inner, preferred_element_type=F32)
    spread[...] = raw.astype(BF16).reshape(count, len(parts) * halves, cols, width)
    send_rows(spread, (out0, out1), me, halves, me, 0)


def attend_back(place, ups, parts, projected, log_totals, weight):
    count, halves, cols, width = parts[0].shape
    tokens = len(parts) * halves * cols
    return call_whole(
        attend_back_body,
        (place, *ups, *parts, projected, log_totals, weight),
        [((3 * width, width), BF16), ((2, 8, width), F32)] + [((count, halves + 1, cols, width), BF16)] * 2,
        [
            ((count, tokens, width), BF16),
            ((count, tokens, width), BF16),
            ((count, tokens, 3 * width), BF16),
            ((count, len(parts) * halves, cols, width), BF16),
        ],
    )


def finish_body(
    place, part0, part1, latents, modulation, taps, middle_grad, latents_grad, sums, small,
    rimmed, normed, normed_grad,
):
    count, rows, cols, width = middle_grad.shape
    lanes = 128
    unpack_strips((part0, part1), rimmed, place[0], 1)
    for l in range(count):
        offset = modulation[l : l + 1, 0:width]
        scaling = 1.0 + modulation[l : l + 1, width : 2 * width]

        def norm_row(r, carry, l=l, offset=offset, scaling=scaling):
            for h in range(0, cols, 16):
                unit, _ = layer_unit(latents[l, r + 2, h : h + 16].astype(F32))
                normed[l, r, h : h + 16] = (unit * scaling + offset).astype(BF16).astype(F32)
            return carry

        lax.fori_loop(0, rows, norm_row, 0)
    for start in range(0, width, lanes):
        here = slice(start, start + lanes)
        tap = [taps[k : k + 1, here].astype(F32) for k in range(9)]
        found = tuple(jnp.zeros((8, lanes), F32) for _ in range(10))
        for l in range(count):

            def conv_row(r, found, l=l, here=here, tap=tap):
                near = [rimmed[l, r + 2 - a, here.start // lanes] for a in range(3)]
                parts = [sum(tap[3 * a + e] * near[a] for a in range(3)) for e in range(3)]
                normed_grad[l, r, :, here] = row_shift(parts[0], -1) + parts[1] + row_shift(parts[2], 1)
                value = normed[l, r, :, here]
                moved = [row_shift(value, 1), value, row_shift(value, -1)]
                added = [found[3 * a + e] + fold_rows(near[a] * moved[e]) for a in range(3) for e in range(3)]
                return tuple(added) + (found[9] + fold_rows(near[1]),)

            found = lax.fori_loop(0, rows, conv_row, found)
        for k in range(10):
            small[k : k + 1, here] = jnp.sum(found[k], axis=0, keepdims=True)
    sums[...] = jnp.zeros_like(sums)
    for l in range(count):
        scaling = 1.0 + modulation[l : l + 1, width : 2 * width]

        def pull_row(r, carry, l=l, scaling=scaling):
            for h in range(0, cols, 16):
                here = slice(h, h + 16)
                unit, inverse = layer_unit(latents[l, r + 2, here].astype(F32))
                grad = normed_grad[l, r, here]
                sums[l, 0] += fold_rows(grad)
                sums[l, 1] += fold_rows(grad * unit)
                pulled = middle_grad[l, r, here] + unit_pull(unit, inverse, grad * scaling)
                latents_grad[l, r, here] = pulled.astype(BF16)
            return carry

        lax.fori_loop(0, rows, pull_row, 0)


def finish(place, parts, latents_rim, modulation, taps, middle_grad):
    count, rows, cols, width = middle_grad.shape
    return call_whole(
        finish_body,
        (place, *parts, latents_rim, modulation, taps, middle_grad),
        [(middle_grad.shape, BF16), ((count, 2, 8, width), F32), ((16, width), F32)],
        [(chunked(count, rows + 2, cols, width), F32), (middle_grad.shape, F32), (middle_grad.shape, F32)],
    )


def exchange(parts):
    return parts[0], swap_bit(parts[1], BATCH, 0)


def on_device(
    latents,
    cotangent,
    timesteps,
    labels,
    time_weight,
    time_bias,
    label_table,
    ada_weight,
    ada_bias,
    conv_a,
    conv_a_bias,
    qkv_weight,
    qv_bias,
    proj_weight,
    proj_bias,
    fc1_weight,
    fc1_bias,
    conv_f,
    conv_f_bias,
    fc2_weight,
    fc2_bias,
):
    width = latents.shape[3]
    hidden_width = fc1_weight.shape[1]
    devices = lax.axis_size(BATCH) * lax.axis_size(GRP)
    slot = lax.axis_index(BATCH) * lax.axis_size(GRP) + lax.axis_index(GRP)

    strip = lax.axis_index(GRP)
    half = lax.axis_index(BATCH) & 1
    inside = jnp.stack([half == 1, half == 0])
    place = jnp.concatenate([half[None], inside.astype(jnp.int32)])
    numbers = jnp.stack([timesteps.astype(F32), labels.astype(F32)])
    other = swap_bit(numbers, BATCH, 0)
    numbers = jnp.where(half == strip >> 1, numbers, other)
    numbers = jnp.where((strip & 1) == 0, numbers[:, 0], numbers[:, 1])
    latents_rim = with_edges(to_pairs(latents), 2)
    cotangent = to_pairs(cotangent)
    cotangent_rim = with_edges(cotangent, 1)

    frequency_rows = sinusoid(numbers[:1], time_weight.shape[0])
    condition = exact_dot(frequency_rows, time_weight) + time_bias.astype(F32)
    picked = lax.dynamic_slice_in_dim(label_table, numbers[1].astype(jnp.int32), 1, axis=0)
    condition = condition + picked.astype(F32)
    active = condition * jax.nn.sigmoid(condition)
    modulation = exact_dot(active, ada_weight) + ada_bias.astype(F32)
    gate_two = modulation[:, None, None, 5 * width :]

    mixed = exchange(stem(place, latents_rim, modulation, conv_a, conv_a_bias))
    qkv_bias = jnp.concatenate([qv_bias[0:1], jnp.zeros_like(qv_bias[0:1]), qv_bias[1:2]], axis=1)
    *sent, projected, log_totals = attend(place, mixed, qkv_weight, qkv_bias)
    normed_rim, attended, branch_one = middle_part(
        place, exchange(sent), latents_rim, modulation, proj_weight, proj_bias
    )

    branch_two_rim = (gate_two * cotangent_rim.astype(F32)).astype(BF16)
    branch_two, normed_two_grad, fc1_here, fc1_away, fc2_here, fc2_away, ff_small = feed_forward(
        place, normed_rim, branch_two_rim, fc1_weight, fc1_bias, conv_f, conv_f_bias, fc2_weight
    )
    pairs = lax.axis_size(BATCH) // 2
    fc1_sum = halve(fc1_here, fc1_away, BATCH, 0).reshape(pairs, -1, width)
    fc2_sum = halve(fc2_here, fc2_away, BATCH, 0)
    fc1_sum = scatter_rest(fc1_sum, False)
    fc2_sum = scatter_rest(fc2_sum, True)

    output, middle_grad, proj_grad, turn_sums, turn_bias, *sent = turn(
        place,
        branch_two.reshape(cotangent.shape),
        normed_two_grad.reshape(cotangent.shape),
        branch_one,
        attended,
        latents_rim,
        cotangent,
        modulation,
        fc2_bias,
        proj_weight,
    )
    output = from_pairs(output)
    turn_sums = jnp.sum(turn_sums, axis=2)
    turn_bias = jnp.sum(turn_bias, axis=1)

    def slots(vectors):
        return vectors.reshape(len(vectors), devices, -1).transpose(1, 0, 2).reshape(devices, -1)

    small = jnp.concatenate([slots(ff_small[:11]), slots(turn_bias)], axis=1).astype(BF16)
    small_length = small.shape[1]
    small_rows = -(-small_length // width)
    small = jnp.pad(small, ((0, 0), (0, small_rows * width - small_length))).reshape(devices, small_rows, width)
    beside = scatter_sum(
        jnp.concatenate([proj_grad.reshape(devices, -1, width), small], axis=1).reshape(-1, width), False
    )
    proj_sum = beside[:-small_rows]
    small_sum = beside[-small_rows:].reshape(-1)
    wide_length = 11 * (hidden_width // devices)
    wide_sum = small_sum[:wide_length].reshape(11, -1)
    narrow_sum = small_sum[wide_length:small_length].reshape(2, -1)

    qkv_grad, qv_sums, *sent = attend_back(place, exchange(sent), mixed, projected, log_totals, qkv_weight)
    qkv_sum = scatter_sum(qkv_grad, True)
    latents_grad, finish_sums, conv_a_small = finish(
        place, exchange(sent), latents_rim, modulation, conv_a, middle_grad
    )
    latents_grad = from_pairs(latents_grad)
    finish_sums = jnp.sum(finish_sums, axis=2)

    late = jnp.concatenate([conv_a_small[:10], jnp.sum(qv_sums, axis=1)], axis=0)
    modulation_grad = jnp.concatenate([finish_sums, turn_sums], axis=1)[0]
    side = jnp.concatenate(
        [condition, jnp.pad(frequency_rows, ((0, 0), (0, width - frequency_rows.shape[1] - 1))), numbers[1:][None]],
        axis=1,
    )
    every, late_sum = gather_sum(side.reshape(2, width), modulation_grad, late)
    every = every.reshape(-1, 8, width)
    every_grad = every[:, :6].reshape(-1, 6 * width)
    every_condition = every[:, 6]
    every_frequency = every[:, 7, : frequency_rows.shape[1]]
    every_label = every[:, 7, -1].astype(jnp.int32)
    late_sum = lax.dynamic_slice_in_dim(late_sum, slot * (width // devices), width // devices, axis=1)
    sigmoid = jax.nn.sigmoid(every_condition)
    every_active = every_condition * sigmoid
    narrow_width = width // devices
    ada_width = 6 * width // devices
    ada_part = lax.dynamic_slice_in_dim(every_grad, slot * ada_width, ada_width, axis=1)
    ada_grad = lax.dot_general(
        every_active, ada_part, (((0,), (0,)), ((), ())), precision=HIGHEST, preferred_element_type=F32
    )
    ada_bias_grad = jnp.sum(ada_part, axis=0)[None, :]
    ada_rows = lax.dynamic_slice_in_dim(ada_weight, slot * narrow_width, narrow_width, axis=0)
    active_grad = lax.dot_general(
        every_grad, ada_rows.astype(F32), (((1,), (1,)), ((), ())), precision=HIGHEST
    )
    slope_silu = lax.dynamic_slice_in_dim(
        sigmoid * (1.0 + every_condition * (1.0 - sigmoid)), slot * narrow_width, narrow_width, axis=1
    )
    condition_grad = active_grad * slope_silu
    onehot = (every_label[:, None] == jnp.arange(label_table.shape[0], dtype=jnp.int32)[None, :]).astype(F32)
    table_grad = lax.dot_general(onehot, condition_grad, (((0,), (0,)), ((), ())), precision=HIGHEST)
    time_grad = lax.dot_general(
        every_frequency, condition_grad, (((0,), (0,)), ((), ())), precision=HIGHEST
    )
    time_bias_grad = jnp.sum(condition_grad, axis=0)[None, :]

    return (
        output,
        latents_grad,
        time_grad,
        time_bias_grad,
        table_grad,
        ada_grad,
        ada_bias_grad,
        late_sum[0:9],
        late_sum[9:10],
        qkv_sum.T,
        late_sum[10:12],
        proj_sum.T,
        narrow_sum[0:1],
        fc1_sum.T,
        wide_sum[10:11],
        wide_sum[0:9],
        wide_sum[9:10],
        fc2_sum.T,
        narrow_sum[1:2],
    )


def solution(mesh):
    columns = P(None, (BATCH, GRP))
    return jax.shard_map(
        on_device,
        mesh=mesh,
        in_specs=(P(BATCH, GRP, None, None), P(BATCH, GRP, None, None), P(BATCH), P(BATCH)) + (P(),) * 17,
        out_specs=(P(BATCH, GRP, None, None), P(BATCH, GRP, None, None)) + (columns,) * 17,
        check_vma=False,
    )
```

profile of v0, /device:TPU:0, one launch (start us, length us, event | category | flops | bytes accessed | tf_op | source)
XLA Modules:
  0.0 367.0 jit_solution(8293518579805633580)
XLA Ops:
  3.9 2.7 collective-permute-start.6
  14.8 4.0 %fusion.38 = f32[3,4608]{1,0:T(4,128)S(1)} fusion(bf16[768,4608]{1,0:T(8,128)(2,1)} %param.28, bf16[1,768]{1,0:T(2,128)(2,1)S(1)} %get-tuple-element.109, bf16[1,768]{1,0:T(2,128)(2,1)S(1)} %get-tuple-element.108, bf16[1,768]{1,0:T(2,128)(2,1)S(1)} %get-tuple-element.79), kind=kOutput, calls=%fused_computation.129 | convolution fusion | flops 21247488 | bytes 7137792 | tf_op jit(solution)/shard_map/dot_general | solution.py:126
  18.9 4.8 %collective-permute-done = bf16[1,8,32,768]{3,2,1,0:T(8,128)(2,1)S(1)} collective-permute-done((bf16[1,8,32,768]{3,2,1,0:T(8,128)(2,1)}, bf16[1,8,32,768]{3,2,1,0:T(8,128)(2,1)S(1)}, u32[]{:S(2)}, u32[]{:S(2)}) %collective-permute-start) | collective-permute-done | bytes 393248 | tf_op jit(solution)/shard_map/ppermute | solution.py:30
  23.8 19.5 %collective-permute-start.2 = (bf16[1,2,32,768]{3,2,1,0:T(8,128)(2,1)S(1)}, bf16[1,2,32,768]{3,2,1,0:T(8,128)(2,1)S(1)}, u32[]{:S(2)}, u32[]{:S(2)}) collective-permute-start(bf16[1,2,32,768]{3,2,1,0:T(8,128)(2,1)S(1)} %slice_select_fusion), channel_id=1, source_target_pairs={{0,4},{4,0},{8,12},{12,8},{16,20},{20,16},{24,28},{28,24},{1,5},{5... | collective-permute-start | bytes 294920 | tf_op jit(solution)/shard_map/ppermute | solution.py:21
  45.4 7.6 %shard_map.348 = (bf16[2,8,16,768]{3,2,1,0:T(8,128)(2,1)}, bf16[2,8,16,768]{3,2,1,0:T(8,128)(2,1)}) custom-call(s32[3]{0:T(128)} %pad_add_fusion.place, bf16[1,20,32,768]{3,2,1,0:T(8,128)(2,1)} %pad_maximum_fusion.1.latents, f32[1,4608]{1,0:T(1,128)} %copy-done.16, bf16[9,768]{1,0:T(8,128)(2,1)} %taps.5, bf16[1,768]{1,0:T(2,128)(2,1)} %conv_bias.2), custom_call_target="tpu_custom_call" | custom-call | tf_op jit(solution)/shard_map/pallas_call | solution.py:391
  55.6 17.3 %shard_map.349 = (bf16[2,10,16,768]{3,2,1,0:T(8,128)(2,1)}, bf16[2,10,16,768]{3,2,1,0:T(8,128)(2,1)}, bf16[2,256,2304]{2,1,0:T(8,128)(2,1)}, f32[2,256,128]{2,1,0:T(8,128)}) custom-call(s32[3]{0:T(128)} %pad_add_fusion.place, bf16[2,8,16,768]{3,2,1,0:T(8,128)(2,1)} %get-tuple-element.49.part0, bf16[2,8,16,768]{3,2,1,0:T(8,128)(2,1)} %copy-done.11, ...), custom_call_target="tpu_custom_call" | custom-call | tf_op jit(solution)/shard_map/pallas_call | solution.py:391
  75.8 8.6 %shard_map.350 = (bf16[1,20,32,768]{3,2,1,0:T(8,128)(2,1)}, bf16[1,16,32,768]{3,2,1,0:T(8,128)(2,1)}, f32[1,16,32,768]{3,2,1,0:T(8,128)}) custom-call(s32[3]{0:T(128)} %pad_add_fusion.place, bf16[2,10,16,768]{3,2,1,0:T(8,128)(2,1)} %get-tuple-element.51.part0, bf16[2,10,16,768]{3,2,1,0:T(8,128)(2,1)} %copy-done.17, ...), custom_call_target="tpu_custom_call" | custom-call | tf_op jit(solution)/shard_map/pallas_call | solution.py:391
  85.6 50.8 %feed_forward.1 = (f32[512,768]{1,0:T(8,128)S(1)}, f32[512,768]{1,0:T(8,128)S(1)}, bf16[4,1,384,768]{3,2,1,0:T(8,128)(2,1)}, bf16[4,1,384,768]{3,2,1,0:T(8,128)(...) custom-call(s32[3]{0:T(128)S(1)} %copy-done.6, ...), custom_call_target="tpu_custom_call" | custom-call | tf_op jit(solution)/shard_map/feed_forward/pallas_call | solution.py:260
  138.8 12.1 %shard_map.351 = (bf16[1,16,32,768]{3,2,1,0:T(8,128)(2,1)}, f32[1,16,32,768]{3,2,1,0:T(8,128)}, bf16[768,768]{1,0:T(8,128)(2,1)}, f32[1,4,8,768]{3,2,1,0:T(8,128...) custom-call(s32[3]{0:T(128)} %pad_add_fusion.place, ...), custom_call_target="tpu_custom_call" | custom-call | tf_op jit(solution)/shard_map/pallas_call | solution.py:391
  156.1 22.8 %shard_map.352 = (bf16[2304,768]{1,0:T(8,128)(2,1)}, f32[2,8,768]{2,1,0:T(8,128)}, bf16[2,9,16,768]{3,2,1,0:T(8,128)(2,1)}, bf16[2,9,16,768]{3,2,1,0:T(8,128)(2,1)}) custom-call(s32[3]{0:T(128)} %pad_add_fusion.place, bf16[2,8,16,768]{3,2,1,0:T(8,128)(2,1)} %get-tuple-element.59.up0, bf16[2,8,16,768]{3,2,1,0:T(8,128)(2,1)} %copy-done.19, ...), custom_call_target="tpu_custom_call" | custom-call | tf_op jit(solution)/shard_map/pallas_call | solution.py:391
  180.3 4.5 %collective-permute-start.10 = (bf16[1,8,32,768]{3,2,1,0:T(8,128)(2,1)}, bf16[1,8,32,768]{3,2,1,0:T(8,128)(2,1)}, u32[]{:S(2)}, u32[]{:S(2)}) collective-permute-start(bf16[1,8,32,768]{3,2,1,0:T(8,128)(2,1)} %get-tuple-element.89), channel_id=1, source_target_pairs={{0,0},{1,1},{4,2},{5,3},{2,4},{3,5},{6,6},{7,7},{8,8},{9,9},{12,10... | collective-permute-start | bytes 1179656 | tf_op jit(solution)/shard_map/ppermute | solution.py:53
  185.6 2.8 dynamic-slice_bitcast_fusion
  189.4 13.7 %shard_map.353 = (bf16[1,16,32,768]{3,2,1,0:T(8,128)(2,1)}, f32[1,2,8,768]{3,2,1,0:T(8,128)}, f32[16,768]{1,0:T(8,128)}) custom-call(s32[3]{0:T(128)} %pad_add_fusion.place, bf16[2,9,16,768]{3,2,1,0:T(8,128)(2,1)} %get-tuple-element.63.part0, bf16[2,9,16,768]{3,2,1,0:T(8,128)(2,1)} %copy-done.18, bf16[1,20,32,768]{3,2,1,0:T(8,128)(2,1)} %pad_maximum_fusion.1.latents, ...), custom_call_target="tpu_custom_call" | custom-call | tf_op jit(solution)/shard_map/pallas_call | solution.py:391
  211.4 5.1 %collective-permute-done.16 = f32[20,768]{1,0:T(8,128)S(1)} collective-permute-done((f32[20,768]{1,0:T(8,128)S(1)}, f32[20,768]{1,0:T(8,128)S(1)}, u32[]{:S(2)}, u32[]{:S(2)}) %collective-permute-start.16) | collective-permute-done | bytes 61472 | tf_op jit(solution)/shard_map/ppermute | solution.py:21
  219.7 3.0 collective-permute-done.17
  224.8 4.0 %collective-permute-done.27 = bf16[104,768]{1,0:T(8,128)(2,1)S(1)} collective-permute-done((bf16[104,768]{1,0:T(8,128)(2,1)S(1)}, bf16[104,768]{1,0:T(8,128)(2,1)S(1)}, u32[]{:S(2)}, u32[]{:S(2)}) %collective-permute-start.27) | collective-permute-done | bytes 159776 | tf_op jit(solution)/shard_map/ppermute | solution.py:21
  228.8 2.8 collective-permute-start.18
  231.8 3.4 collective-permute-done.18
  240.6 2.7 collective-permute-start.19
  246.9 10.4 %collective-permute-done.29 = bf16[26,768]{1,0:T(8,128)(2,1)S(1)} collective-permute-done((bf16[26,768]{1,0:T(8,128)(2,1)S(1)}, bf16[26,768]{1,0:T(8,128)(2,1)S(1)}, u32[]{:S(2)}, u32[]{:S(2)}) %collective-permute-start.29) | collective-permute-done | bytes 39968 | tf_op jit(solution)/shard_map/ppermute | solution.py:21
  268.7 2.6 fusion
  272.9 2.6 add_convert_fusion
  276.2 17.7 %collective-permute-done.21 = bf16[2,288,768]{2,1,0:T(8,128)(2,1)S(1)} collective-permute-done((bf16[2,288,768]{2,1,0:T(8,128)(2,1)S(1)}, bf16[2,288,768]{2,1,0:T(8,128)(2,1)S(1)}, u32[]{:S(2)}, u32[]{:S(2)}) %collective-permute-start.21) | collective-permute-done | bytes 884768 | tf_op jit(solution)/shard_map/ppermute | solution.py:21
  297.0 10.3 %collective-permute-done.22 = bf16[288,768]{1,0:T(8,128)(2,1)S(1)} collective-permute-done((bf16[288,768]{1,0:T(8,128)(2,1)S(1)}, bf16[288,768]{1,0:T(8,128)(2,1)S(1)}, u32[]{:S(2)}, u32[]{:S(2)}) %collective-permute-start.22) | collective-permute-done | bytes 442400 | tf_op jit(solution)/shard_map/ppermute | solution.py:21
  308.2 9.7 %collective-permute-done.36 = bf16[2,96,3072]{2,1,0:T(8,128)(2,1)S(1)} collective-permute-done((bf16[2,96,3072]{2,1,0:T(8,128)(2,1)S(1)}, bf16[2,96,3072]{2,1,0:T(8,128)(2,1)S(1)}, u32[]{:S(2)}, u32[]{:S(2)}) %collective-permute-start.36) | collective-permute-done | bytes 1179680 | tf_op jit(solution)/shard_map/ppermute | solution.py:21
  319.9 12.7 %collective-permute-done.31 = bf16[2,384,768]{2,1,0:T(8,128)(2,1)S(1)} collective-permute-done((bf16[2,384,768]{2,1,0:T(8,128)(2,1)S(1)}, bf16[2,384,768]{2,1,0:T(8,128)(2,1)S(1)}, u32[]{:S(2)}, u32[]{:S(2)}) %collective-permute-start.31) | collective-permute-done | bytes 1179680 | tf_op jit(solution)/shard_map/ppermute | solution.py:21
  334.7 5.2 %collective-permute-done.24 = bf16[72,768]{1,0:T(8,128)(2,1)S(1)} collective-permute-done((bf16[72,768]{1,0:T(8,128)(2,1)S(1)}, bf16[72,768]{1,0:T(8,128)(2,1)S(1)}, u32[]{:S(2)}, u32[]{:S(2)}) %collective-permute-start.24) | collective-permute-done | bytes 110624 | tf_op jit(solution)/shard_map/ppermute | solution.py:21
  343.7 3.7 %collective-permute-start.33 = (bf16[2,96,768]{2,1,0:T(8,128)(2,1)S(1)}, bf16[2,96,768]{2,1,0:T(8,128)(2,1)S(1)}, u32[]{:S(2)}, u32[]{:S(2)}) collective-permute-start(bf16[2,96,768]{2,1,0:T(8,128)(2,1)S(1)} %dynamic-slice_bitcast_fusion.10), channel_id=1, source_target_pairs={{0,1},{1,0},{2,3},{3,2},{4,5},{5,4},{6,7},{7,6},{8,9},{9,8},{10,11... | collective-permute-start | bytes 884744 | tf_op jit(solution)/shard_map/ppermute | solution.py:21
  347.4 5.4 %collective-permute-done.38 = bf16[2,24,3072]{2,1,0:T(8,128)(2,1)S(1)} collective-permute-done((bf16[2,24,3072]{2,1,0:T(8,128)(2,1)S(1)}, bf16[2,24,3072]{2,1,0:T(8,128)(2,1)S(1)}, u32[]{:S(2)}, u32[]{:S(2)}) %collective-permute-start.38) | collective-permute-done | bytes 294944 | tf_op jit(solution)/shard_map/ppermute | solution.py:21
  353.0 2.8 collective-permute-start.39
  356.1 4.1 %collective-permute-start.34 = (bf16[96,768]{1,0:T(8,128)(2,1)S(1)}, bf16[96,768]{1,0:T(8,128)(2,1)S(1)}, u32[]{:S(2)}, u32[]{:S(2)}) collective-permute-start(bf16[96,768]{1,0:T(8,128)(2,1)S(1)} %dynamic-slice_bitcast_fusion.14), channel_id=1, source_target_pairs={{0,2},{1,3},{2,0},{3,1},{4,6},{5,7},{6,4},{7,5},{8,10},{9,11},{10,... | collective-permute-start | bytes 442376 | tf_op jit(solution)/shard_map/ppermute | solution.py:21
  360.3 4.4 %collective-permute-done.39 = bf16[24,3072]{1,0:T(8,128)(2,1)S(1)} collective-permute-done((bf16[24,3072]{1,0:T(8,128)(2,1)S(1)}, bf16[24,3072]{1,0:T(8,128)(2,1)S(1)}, u32[]{:S(2)}, u32[]{:S(2)}) %collective-permute-start.39) | collective-permute-done | bytes 147488 | tf_op jit(solution)/shard_map/ppermute | solution.py:21
  (241 shorter events, 81.0 us)
Async XLA Ops:
  2.1 9.0 %collective-permute-start.3 = (f32[2,2]{1,0:T(2,128)S(1)}, f32[2,2]{1,0:T(2,128)S(1)}, u32[]{:S(2)}, u32[]{:S(2)}) collective-permute-start(f32[2,2]{1,0:T(2,128)S(1)} %pad_maximum_fusion.8), channel_id=1, source_target_pairs={{0,4},{4,0},{8,12},{12,8},{16,20},{20,16},{24,28},{28,24},{1,5},{5... | collective-permute-start | bytes 56 | tf_op jit(solution)/shard_map/ppermute | solution.py:21
  3.9 49.5 %collective-permute-start.6 = (bf16[1,8,32,768]{3,2,1,0:T(8,128)(2,1)S(1)}, bf16[1,8,32,768]{3,2,1,0:T(8,128)(2,1)S(1)}, u32[]{:S(2)}, u32[]{:S(2)}) collective-permute-start(bf16[1,8,32,768]{3,2,1,0:T(8,128)(2,1)S(1)} %get-tuple-element.92), channel_id=1, source_target_pairs={{0,1},{1,0},{2,5},{3,4},{4,3},{5,2},{6,7},{7,6},{8,9},{9,8},{10,13... | collective-permute-start | bytes 1179656 | tf_op jit(solution)/shard_map/ppermute | solution.py:30
  6.5 46.8 %collective-permute-start.7 = (bf16[1,8,32,768]{3,2,1,0:T(8,128)(2,1)S(1)}, bf16[1,8,32,768]{3,2,1,0:T(8,128)(2,1)S(1)}, u32[]{:S(2)}, u32[]{:S(2)}) collective-permute-start(bf16[1,8,32,768]{3,2,1,0:T(8,128)(2,1)S(1)} %get-tuple-element.93), channel_id=1, source_target_pairs={{0,0},{1,1},{2,4},{3,5},{4,2},{5,3},{6,6},{7,7},{8,8},{9,9},{10,12... | collective-permute-start | bytes 1179656 | tf_op jit(solution)/shard_map/ppermute | solution.py:30
  8.1 15.6 %collective-permute-start = (bf16[1,8,32,768]{3,2,1,0:T(8,128)(2,1)}, bf16[1,8,32,768]{3,2,1,0:T(8,128)(2,1)S(1)}, u32[]{:S(2)}, u32[]{:S(2)}) collective-permute-start(bf16[1,8,32,768]{3,2,1,0:T(8,128)(2,1)} %get-tuple-element.96), channel_id=1, source_target_pairs={{0,1},{1,0},{2,5},{3,4},{4,3},{5,2},{6,7},{7,6},{8,9},{9,8},{10,13... | collective-permute-start | bytes 1179656 | tf_op jit(solution)/shard_map/ppermute | solution.py:30
  8.2 15.6 %collective-permute-start.1 = (bf16[1,8,32,768]{3,2,1,0:T(8,128)(2,1)}, bf16[1,8,32,768]{3,2,1,0:T(8,128)(2,1)S(1)}, u32[]{:S(2)}, u32[]{:S(2)}) collective-permute-start(bf16[1,8,32,768]{3,2,1,0:T(8,128)(2,1)} %get-tuple-element.97), channel_id=1, source_target_pairs={{0,0},{1,1},{2,4},{3,5},{4,2},{5,3},{6,6},{7,7},{8,8},{9,9},{10,12... | collective-permute-start | bytes 1179656 | tf_op jit(solution)/shard_map/ppermute | solution.py:30
  23.8 20.4 %collective-permute-start.2 = (bf16[1,2,32,768]{3,2,1,0:T(8,128)(2,1)S(1)}, bf16[1,2,32,768]{3,2,1,0:T(8,128)(2,1)S(1)}, u32[]{:S(2)}, u32[]{:S(2)}) collective-permute-start(bf16[1,2,32,768]{3,2,1,0:T(8,128)(2,1)S(1)} %slice_select_fusion), channel_id=1, source_target_pairs={{0,4},{4,0},{8,12},{12,8},{16,20},{20,16},{24,28},{28,24},{1,5},{5... | collective-permute-start | bytes 294920 | tf_op jit(solution)/shard_map/ppermute | solution.py:21
  53.4 20.9 %collective-permute-start.8 = (bf16[1,1,32,768]{3,2,1,0:T(8,128)(2,1)S(1)}, bf16[1,1,32,768]{3,2,1,0:T(8,128)(2,1)S(1)}, u32[]{:S(2)}, u32[]{:S(2)}) collective-permute-start(bf16[1,1,32,768]{3,2,1,0:T(8,128)(2,1)S(1)} %slice_select_fusion.1), channel_id=1, source_target_pairs={{0,4},{4,0},{8,12},{12,8},{16,20},{20,16},{24,28},{28,24},{1,5},{5... | collective-permute-start | bytes 147464 | tf_op jit(solution)/shard_map/ppermute | solution.py:21
  153.6 34.8 %collective-permute-start.25 = (bf16[4,104,768]{2,1,0:T(8,128)(2,1)S(1)}, bf16[4,104,768]{2,1,0:T(8,128)(2,1)S(1)}, u32[]{:S(2)}, u32[]{:S(2)}) collective-permute-start(bf16[4,104,768]{2,1,0:T(8,128)(2,1)S(1)} %dynamic-slice_bitcast_fusion.4), channel_id=1, source_target_pairs={{0,4},{4,0},{8,12},{12,8},{16,20},{20,16},{24,28},{28,24},{1,5},{5... | collective-permute-start | bytes 1916936 | tf_op jit(solution)/shard_map/ppermute | solution.py:21
  178.9 9.7 %collective-permute-start.12 = (bf16[2,9,16,768]{3,2,1,0:T(8,128)(2,1)}, bf16[2,9,16,768]{3,2,1,0:T(8,128)(2,1)S(1)}, u32[]{:S(2)}, u32[]{:S(2)}) collective-permute-start(bf16[2,9,16,768]{3,2,1,0:T(8,128)(2,1)} %get-tuple-element.64), channel_id=1, source_target_pairs={{0,4},{4,0},{8,12},{12,8},{16,20},{20,16},{24,28},{28,24},{1,5},{5... | collective-permute-start | bytes 1327112 | tf_op jit(solution)/shard_map/ppermute | solution.py:21
  180.3 59.6 %collective-permute-start.10 = (bf16[1,8,32,768]{3,2,1,0:T(8,128)(2,1)}, bf16[1,8,32,768]{3,2,1,0:T(8,128)(2,1)}, u32[]{:S(2)}, u32[]{:S(2)}) collective-permute-start(bf16[1,8,32,768]{3,2,1,0:T(8,128)(2,1)} %get-tuple-element.89), channel_id=1, source_target_pairs={{0,0},{1,1},{4,2},{5,3},{2,4},{3,5},{6,6},{7,7},{8,8},{9,9},{12,10... | collective-permute-start | bytes 1179656 | tf_op jit(solution)/shard_map/ppermute | solution.py:53
  184.8 55.7 %collective-permute-start.9 = (bf16[1,8,32,768]{3,2,1,0:T(8,128)(2,1)}, bf16[1,8,32,768]{3,2,1,0:T(8,128)(2,1)}, u32[]{:S(2)}, u32[]{:S(2)}) collective-permute-start(bf16[1,8,32,768]{3,2,1,0:T(8,128)(2,1)} %get-tuple-element.88), channel_id=1, source_target_pairs={{1,0},{0,1},{5,2},{4,3},{3,4},{2,5},{7,6},{6,7},{9,8},{8,9},{13,10... | collective-permute-start | bytes 1179656 | tf_op jit(solution)/shard_map/ppermute | solution.py:53
  205.0 13.0 %collective-permute-start.26 = (bf16[2,104,768]{2,1,0:T(8,128)(2,1)S(1)}, bf16[2,104,768]{2,1,0:T(8,128)(2,1)S(1)}, u32[]{:S(2)}, u32[]{:S(2)}) collective-permute-start(bf16[2,104,768]{2,1,0:T(8,128)(2,1)S(1)} %dynamic-slice_bitcast_fusion.8), channel_id=1, source_target_pairs={{0,8},{4,12},{8,0},{12,4},{16,24},{20,28},{24,16},{28,20},{1,9},{5... | collective-permute-start | bytes 958472 | tf_op jit(solution)/shard_map/ppermute | solution.py:21
  207.4 9.1 %collective-permute-start.16 = (f32[20,768]{1,0:T(8,128)S(1)}, f32[20,768]{1,0:T(8,128)S(1)}, u32[]{:S(2)}, u32[]{:S(2)}) collective-permute-start(f32[20,768]{1,0:T(8,128)S(1)} %pad_maximum_fusion.7), channel_id=1, source_target_pairs={{0,8},{4,12},{8,0},{12,4},{16,24},{20,28},{24,16},{28,20},{1,9},{5... | collective-permute-start | bytes 184328 | tf_op jit(solution)/shard_map/ppermute | solution.py:21
  209.4 31.2 %collective-permute-start.13 = (bf16[1,8,32,768]{3,2,1,0:T(8,128)(2,1)}, bf16[1,8,32,768]{3,2,1,0:T(8,128)(2,1)}, u32[]{:S(2)}, u32[]{:S(2)}) collective-permute-start(bf16[1,8,32,768]{3,2,1,0:T(8,128)(2,1)} %get-tuple-element.84), channel_id=1, source_target_pairs={{1,0},{0,1},{5,2},{4,3},{3,4},{2,5},{7,6},{6,7},{9,8},{8,9},{13,10... | collective-permute-start | bytes 1179656 | tf_op jit(solution)/shard_map/ppermute | solution.py:53
  216.5 26.8 %collective-permute-start.14 = (bf16[1,8,32,768]{3,2,1,0:T(8,128)(2,1)S(1)}, bf16[1,8,32,768]{3,2,1,0:T(8,128)(2,1)}, u32[]{:S(2)}, u32[]{:S(2)}) collective-permute-start(bf16[1,8,32,768]{3,2,1,0:T(8,128)(2,1)S(1)} %get-tuple-element.85), channel_id=1, source_target_pairs={{0,0},{1,1},{4,2},{5,3},{2,4},{3,5},{6,6},{7,7},{8,8},{9,9},{12,10... | collective-permute-start | bytes 1179656 | tf_op jit(solution)/shard_map/ppermute | solution.py:53
  239.9 33.1 %collective-permute-start.35 = (bf16[4,96,3072]{2,1,0:T(8,128)(2,1)}, bf16[4,96,3072]{2,1,0:T(8,128)(2,1)}, u32[]{:S(2)}, u32[]{:S(2)}) collective-permute-start(bf16[4,96,3072]{2,1,0:T(8,128)(2,1)} %get-tuple-element.78), channel_id=1, source_target_pairs={{0,4},{4,0},{8,12},{12,8},{16,20},{20,16},{24,28},{28,24},{1,5},{5... | collective-permute-start | bytes 7077896 | tf_op jit(solution)/shard_map/ppermute | solution.py:21
  239.9 55.8 %collective-permute-start.30 = (bf16[4,1,384,768]{3,2,1,0:T(8,128)(2,1)}, bf16[4,1,384,768]{3,2,1,0:T(8,128)(2,1)S(1)}, u32[]{:S(2)}, u32[]{:S(2)}) collective-permute-start(bf16[4,1,384,768]{3,2,1,0:T(8,128)(2,1)} %get-tuple-element.76), channel_id=1, source_target_pairs={{0,4},{4,0},{8,12},{12,8},{16,20},{20,16},{24,28},{28,24},{1,5},{5... | collective-permute-start | bytes 7077896 | tf_op jit(solution)/shard_map/ppermute | solution.py:21
  240.5 28.2 %collective-permute-start.20 = (bf16[4,288,768]{2,1,0:T(8,128)(2,1)}, bf16[4,288,768]{2,1,0:T(8,128)(2,1)}, u32[]{:S(2)}, u32[]{:S(2)}) collective-permute-start(bf16[4,288,768]{2,1,0:T(8,128)(2,1)} %dynamic-slice_bitcast_fusion), channel_id=1, source_target_pairs={{0,4},{4,0},{8,12},{12,8},{16,20},{20,16},{24,28},{28,24},{1,5},{5... | collective-permute-start | bytes 5308424 | tf_op jit(solution)/shard_map/ppermute | solution.py:21
  240.6 19.2 %collective-permute-start.19 = (f32[76,768]{1,0:T(8,128)S(1)}, f32[76,768]{1,0:T(8,128)}, u32[]{:S(2)}, u32[]{:S(2)}) collective-permute-start(f32[76,768]{1,0:T(8,128)S(1)} %concatenate.137), channel_id=1, source_target_pairs={{0,2},{1,3},{2,0},{3,1},{4,6},{5,7},{6,4},{7,5},{8,10},{9,11},{10,... | collective-permute-start | bytes 700424 | tf_op jit(solution)/shard_map/ppermute | solution.py:21
  243.3 13.9 %collective-permute-start.29 = (bf16[26,768]{1,0:T(8,128)(2,1)S(1)}, bf16[26,768]{1,0:T(8,128)(2,1)S(1)}, u32[]{:S(2)}, u32[]{:S(2)}) collective-permute-start(bf16[26,768]{1,0:T(8,128)(2,1)S(1)} %dynamic-slice_bitcast_fusion.17), channel_id=1, source_target_pairs={{0,2},{1,3},{2,0},{3,1},{4,6},{5,7},{6,4},{7,5},{8,10},{9,11},{10,... | collective-permute-start | bytes 119816 | tf_op jit(solution)/shard_map/ppermute | solution.py:21
  271.3 22.6 %collective-permute-start.21 = (bf16[2,288,768]{2,1,0:T(8,128)(2,1)S(1)}, bf16[2,288,768]{2,1,0:T(8,128)(2,1)S(1)}, u32[]{:S(2)}, u32[]{:S(2)}) collective-permute-start(bf16[2,288,768]{2,1,0:T(8,128)(2,1)S(1)} %dynamic-slice_bitcast_fusion.3), channel_id=1, source_target_pairs={{0,16},{4,20},{8,24},{12,28},{16,0},{20,4},{24,8},{28,12},{1,17},{... | collective-permute-start | bytes 2654216 | tf_op jit(solution)/shard_map/ppermute | solution.py:21
  275.6 42.3 %collective-permute-start.36 = (bf16[2,96,3072]{2,1,0:T(8,128)(2,1)S(1)}, bf16[2,96,3072]{2,1,0:T(8,128)(2,1)S(1)}, u32[]{:S(2)}, u32[]{:S(2)}) collective-permute-start(bf16[2,96,3072]{2,1,0:T(8,128)(2,1)S(1)} %dynamic-slice_bitcast_fusion.1), channel_id=1, source_target_pairs={{0,16},{4,20},{8,24},{12,28},{16,0},{20,4},{24,8},{28,12},{1,17},{... | collective-permute-start | bytes 3538952 | tf_op jit(solution)/shard_map/ppermute | solution.py:21
  294.2 13.1 %collective-permute-start.22 = (bf16[288,768]{1,0:T(8,128)(2,1)S(1)}, bf16[288,768]{1,0:T(8,128)(2,1)S(1)}, u32[]{:S(2)}, u32[]{:S(2)}) collective-permute-start(bf16[288,768]{1,0:T(8,128)(2,1)S(1)} %dynamic-slice_bitcast_fusion.7), channel_id=1, source_target_pairs={{0,8},{4,12},{8,0},{12,4},{16,24},{20,28},{24,16},{28,20},{1,9},{5... | collective-permute-start | bytes 1327112 | tf_op jit(solution)/shard_map/ppermute | solution.py:21
  296.4 36.2 %collective-permute-start.31 = (bf16[2,384,768]{2,1,0:T(8,128)(2,1)S(1)}, bf16[2,384,768]{2,1,0:T(8,128)(2,1)S(1)}, u32[]{:S(2)}, u32[]{:S(2)}) collective-permute-start(bf16[2,384,768]{2,1,0:T(8,128)(2,1)S(1)} %dynamic-slice_bitcast_fusion.2), channel_id=1, source_target_pairs={{0,8},{4,12},{8,0},{12,4},{16,24},{20,28},{24,16},{28,20},{1,9},{5... | collective-permute-start | bytes 3538952 | tf_op jit(solution)/shard_map/ppermute | solution.py:21
  307.4 25.4 %collective-permute-start.23 = (bf16[2,72,768]{2,1,0:T(8,128)(2,1)S(1)}, bf16[2,72,768]{2,1,0:T(8,128)(2,1)S(1)}, u32[]{:S(2)}, u32[]{:S(2)}) collective-permute-start(bf16[2,72,768]{2,1,0:T(8,128)(2,1)S(1)} %dynamic-slice_bitcast_fusion.11), channel_id=1, source_target_pairs={{0,1},{1,0},{2,3},{3,2},{4,5},{5,4},{6,7},{7,6},{8,9},{9,8},{10,11... | collective-permute-start | bytes 663560 | tf_op jit(solution)/shard_map/ppermute | solution.py:21
  318.4 23.4 %collective-permute-start.37 = (bf16[96,3072]{1,0:T(8,128)(2,1)S(1)}, bf16[96,3072]{1,0:T(8,128)(2,1)S(1)}, u32[]{:S(2)}, u32[]{:S(2)}) collective-permute-start(bf16[96,3072]{1,0:T(8,128)(2,1)S(1)} %dynamic-slice_bitcast_fusion.5), channel_id=1, source_target_pairs={{0,8},{4,12},{8,0},{12,4},{16,24},{20,28},{24,16},{28,20},{1,9},{5... | collective-permute-start | bytes 1769480 | tf_op jit(solution)/shard_map/ppermute | solution.py:21
  333.0 6.9 %collective-permute-start.24 = (bf16[72,768]{1,0:T(8,128)(2,1)S(1)}, bf16[72,768]{1,0:T(8,128)(2,1)S(1)}, u32[]{:S(2)}, u32[]{:S(2)}) collective-permute-start(bf16[72,768]{1,0:T(8,128)(2,1)S(1)} %dynamic-slice_bitcast_fusion.15), channel_id=1, source_target_pairs={{0,2},{1,3},{2,0},{3,1},{4,6},{5,7},{6,4},{7,5},{8,10},{9,11},{10,... | collective-permute-start | bytes 331784 | tf_op jit(solution)/shard_map/ppermute | solution.py:21
  333.1 10.4 %collective-permute-start.32 = (bf16[384,768]{1,0:T(8,128)(2,1)S(1)}, bf16[384,768]{1,0:T(8,128)(2,1)S(1)}, u32[]{:S(2)}, u32[]{:S(2)}) collective-permute-start(bf16[384,768]{1,0:T(8,128)(2,1)S(1)} %dynamic-slice_bitcast_fusion.6), channel_id=1, source_target_pairs={{0,16},{4,20},{8,24},{12,28},{16,0},{20,4},{24,8},{28,12},{1,17},{... | collective-permute-start | bytes 1769480 | tf_op jit(solution)/shard_map/ppermute | solution.py:21
  341.9 10.9 %collective-permute-start.38 = (bf16[2,24,3072]{2,1,0:T(8,128)(2,1)S(1)}, bf16[2,24,3072]{2,1,0:T(8,128)(2,1)S(1)}, u32[]{:S(2)}, u32[]{:S(2)}) collective-permute-start(bf16[2,24,3072]{2,1,0:T(8,128)(2,1)S(1)} %dynamic-slice_bitcast_fusion.9), channel_id=1, source_target_pairs={{0,1},{1,0},{2,3},{3,2},{4,5},{5,4},{6,7},{7,6},{8,9},{9,8},{10,11... | collective-permute-start | bytes 884744 | tf_op jit(solution)/shard_map/ppermute | solution.py:21
  343.7 12.3 %collective-permute-start.33 = (bf16[2,96,768]{2,1,0:T(8,128)(2,1)S(1)}, bf16[2,96,768]{2,1,0:T(8,128)(2,1)S(1)}, u32[]{:S(2)}, u32[]{:S(2)}) collective-permute-start(bf16[2,96,768]{2,1,0:T(8,128)(2,1)S(1)} %dynamic-slice_bitcast_fusion.10), channel_id=1, source_target_pairs={{0,1},{1,0},{2,3},{3,2},{4,5},{5,4},{6,7},{7,6},{8,9},{9,8},{10,11... | collective-permute-start | bytes 884744 | tf_op jit(solution)/shard_map/ppermute | solution.py:21
  353.0 11.7 %collective-permute-start.39 = (bf16[24,3072]{1,0:T(8,128)(2,1)S(1)}, bf16[24,3072]{1,0:T(8,128)(2,1)S(1)}, u32[]{:S(2)}, u32[]{:S(2)}) collective-permute-start(bf16[24,3072]{1,0:T(8,128)(2,1)S(1)} %dynamic-slice_bitcast_fusion.13), channel_id=1, source_target_pairs={{0,2},{1,3},{2,0},{3,1},{4,6},{5,7},{6,4},{7,5},{8,10},{9,11},{10,... | collective-permute-start | bytes 442376 | tf_op jit(solution)/shard_map/ppermute | solution.py:21
  356.1 10.1 %collective-permute-start.34 = (bf16[96,768]{1,0:T(8,128)(2,1)S(1)}, bf16[96,768]{1,0:T(8,128)(2,1)S(1)}, u32[]{:S(2)}, u32[]{:S(2)}) collective-permute-start(bf16[96,768]{1,0:T(8,128)(2,1)S(1)} %dynamic-slice_bitcast_fusion.14), channel_id=1, source_target_pairs={{0,2},{1,3},{2,0},{3,1},{4,6},{5,7},{6,4},{7,5},{8,10},{9,11},{10,... | collective-permute-start | bytes 442376 | tf_op jit(solution)/shard_map/ppermute | solution.py:21
  (33 other events, 254.4 us)
where the time goes:
time: 368 us; the launch traced here: 367 us
  Pallas kernels  133 us (36%)
  waiting for transfers between devices  104 us (28%)
  starting transfers between devices  69.2 us (19%)
  other arithmetic  26.6 us (7%)
  local copies, waits for them, and re-layouts  23.3 us (6%)
  matrix products  9.11 us (2%)
    ppermute x32, waiting for transfers between devices, swap_bit(): return lax.ppermute(value, axis, [(i, i ^ 1 << bit) for i in range(count)])  98.8 us
    pallas_call x6, Pallas kernels, call_whole(): pl.pallas_call(body, in_specs=[SCALARS] + [WHOLE] * (len(inputs) - 1), ou...  82.1 us
    ppermute x32, starting transfers between devices, swap_bit(): return lax.ppermute(value, axis, [(i, i ^ 1 << bit) for i in range(count)])  56.3 us
    pallas_call x1, Pallas kernels, feed_forward(): pl.pallas_call(feed_forward_body, grid=(steps,), in_specs=[pl.BlockSpec(m...  50.8 us
    ppermute x4, starting transfers between devices, from_pairs(): arrived.append(lax.ppermute(piece, (BATCH, GRP), pair_moves(k, True)))  7.93 us
  transfers between devices with their start and end apart: 40, of which 20 were waited for; matrix products, arithmetic and copies ran while one was open for 13% of the time, Pallas kernels for 17%

commit v1 on v0

--- a/solution.py
+++ b/solution.py
@@ -1,3 +1,4 @@
+from functools import partial
 import math
 
 import jax
@@ -93,21 +94,15 @@
     return block
 
 
-def scatter_sum(block, swapped):
-    pairs = lax.axis_size(BATCH) // 2
-    width = block.shape[-1]
-    block = halve_dim(block.reshape(pairs, 2, -1, width), 1, BATCH, 0)
-    return scatter_rest(block, swapped)
-
-
 def gather_sum(rows, pair_rows, summed):
-    bits = [(BATCH, bit) for bit in range(1, lax.axis_size(BATCH).bit_length() - 1)]
-    bits += [(GRP, bit) for bit in range(lax.axis_size(GRP).bit_length() - 1)]
+    length = pair_rows.shape[0]
+    bits = [(GRP, bit) for bit in range(lax.axis_size(GRP).bit_length() - 1)]
+    bits += [(BATCH, bit) for bit in range(1, lax.axis_size(BATCH).bit_length() - 1)]
     length = pair_rows.shape[0]
     both = jnp.concatenate([pair_rows, summed], axis=0)
     other = swap_bit(both, BATCH, 0)
     both = both + other
-    rows = jnp.concatenate([both[:length], rows], axis=0)
+    rows = both[:length] + rows
     summed = both[length:]
     for axis, bit in bits:
         sent = jnp.concatenate([summed, rows], axis=0)
@@ -451,7 +446,7 @@
             attended[l, :, :, pl.ds(start, lanes)] = both.reshape(len(parts) * halves, cols, lanes)
             return carry
 
-        lax.fori_loop(0, width // lanes, pair, 0)
+        lax.fori_loop(0, width // lanes, pair, 0, unroll=2)
     send_rows(attended, (out0, out1), me, halves, 1, 0)
 
 
@@ -587,7 +582,7 @@
 
 def attend_back_body(
     place, up0, up1, part0, part1, projected, log_totals, weight,
-    weight_grad, bias_sums, out0, out1, gathered, upstream, grads, spread,
+    weight_here, weight_away, bias_sums, out0, out1, gathered, upstream, grads, spread, weight_grad,
 ):
     parts = (part0, part1)
     count, halves, cols, width = part0.shape
@@ -637,11 +632,14 @@
                     bias_sums[k // 2, :, here[0]] += fold_rows(both.astype(F32))
             return carry
 
-        lax.fori_loop(0, width // lanes, pair, 0)
+        lax.fori_loop(0, width // lanes, pair, 0, unroll=2)
     every = grads[...].reshape(count * tokens, 3 * width)
     weight_grad[...] = lax.dot_general(
         every, gathered[...].reshape(count * tokens, width), turned, preferred_element_type=F32
-    ).astype(BF16)
+    ).reshape(weight_grad.shape)
+    for j in range(weight_grad.shape[0]):
+        weight_here[j] = weight_grad[j, me].astype(BF16)
+        weight_away[j] = weight_grad[j, 1 - me].astype(BF16)
     raw = lax.dot_general(every, weight[...], inner, preferred_element_type=F32)
     spread[...] = raw.astype(BF16).reshape(count, len(parts) * halves, cols, width)
     send_rows(spread, (out0, out1), me, halves, me, 0)
@@ -650,15 +648,18 @@
 def attend_back(place, ups, parts, projected, log_totals, weight):
     count, halves, cols, width = parts[0].shape
     tokens = len(parts) * halves * cols
+    batch = lax.axis_size(BATCH)
+    half_grad = (batch // 2, 3 * width // batch, width)
     return call_whole(
         attend_back_body,
         (place, *ups, *parts, projected, log_totals, weight),
-        [((3 * width, width), BF16), ((2, 8, width), F32)] + [((count, halves + 1, cols, width), BF16)] * 2,
+        [(half_grad, BF16), (half_grad, BF16), ((2, 8, width), F32)] + [((count, halves + 1, cols, width), BF16)] * 2,
         [
             ((count, tokens, width), BF16),
             ((count, tokens, width), BF16),
             ((count, tokens, 3 * width), BF16),
             ((count, len(parts) * halves, cols, width), BF16),
+            ((batch // 2, 2, 3 * width // batch, width), F32),
         ],
     )
 
@@ -725,6 +726,62 @@
         [(middle_grad.shape, BF16), ((count, 2, 8, width), F32), ((16, width), F32)],
         [(chunked(count, rows + 2, cols, width), F32), (middle_grad.shape, F32), (middle_grad.shape, F32)],
     )
+
+
+def fold_body(pieces, sources, outputs, *refs):
+    mine = refs[0]
+    heres, aways = refs[1 : 1 + sources], refs[1 + sources : 1 + 2 * sources]
+    kept, sent = refs[1 + 2 * sources :][:outputs], refs[1 + 2 * sources + outputs :][:outputs]
+    scratch = list(refs[1 + 2 * sources + 2 * outputs :])
+    for source, row, rows, lane, lead, bit, out, out_row, out_lane in pieces:
+        here, away = heres[source], aways[source]
+        size = rows // (2 * lead)
+        lanes, out_lanes = slice(lane, lane + FOLD), slice(out_lane, out_lane + FOLD)
+        me = mine[bit]
+        if size % 16:
+            whole = scratch.pop(0)
+            total = here[row : row + rows, lanes].astype(F32) + away[row : row + rows, lanes].astype(F32)
+            whole[...] = total.reshape(lead, 2, size, FOLD)
+            for side, place in ((kept, me), (sent, 1 - me)):
+                picked = whole[:, place].reshape(lead * size, FOLD).astype(BF16)
+                side[out][out_row : out_row + lead * size, out_lanes] = picked
+            continue
+        part = max(p for p in range(16, 97, 16) if size % p == 0)
+
+        def one(n, carry, here=here, away=away, row=row, size=size, part=part, lanes=lanes, out=out,
+                out_row=out_row, out_lanes=out_lanes, me=me):
+            a, k = n // (size // part), n % (size // part)
+            target = pl.ds(pl.multiple_of(out_row + a * size + k * part, 16), part)
+            for side, place in ((kept, me), (sent, 1 - me)):
+                origin = pl.ds(pl.multiple_of(row + (2 * a + place) * size + k * part, 16), part)
+                total = here[origin, lanes].astype(F32) + away[origin, lanes].astype(F32)
+                side[out][target, out_lanes] = total.astype(BF16)
+            return carry
+
+        lax.fori_loop(0, lead * size // part, one, 0)
+
+
+FOLD = 768
+
+
+def fold(pairs, bits, pieces, outs):
+    mine = jnp.stack([(lax.axis_index(axis) >> bit) & 1 for axis, bit in bits]).astype(jnp.int32)
+    scratch = [(p[4], 2, p[2] // (2 * p[4]), FOLD) for p in pieces if p[2] // (2 * p[4]) % 16]
+    found = call_whole(
+        partial(fold_body, pieces, len(pairs), len(outs)),
+        (mine, *[pair[0] for pair in pairs], *[pair[1] for pair in pairs]),
+        [(shape, BF16) for shape in outs] * 2,
+        [(shape, F32) for shape in scratch],
+    )
+    return list(zip(found[: len(outs)], found[len(outs) :]))
+
+
+def swap(pair, axis, bit):
+    return pair[0], swap_bit(pair[1], axis, bit)
+
+
+def quick_sums():
+    return lax.axis_size(BATCH) == 8 and lax.axis_size(GRP) == 4
 
 
 def exchange(parts):
@@ -791,10 +848,28 @@
         place, normed_rim, branch_two_rim, fc1_weight, fc1_bias, conv_f, conv_f_bias, fc2_weight
     )
     pairs = lax.axis_size(BATCH) // 2
-    fc1_sum = halve(fc1_here, fc1_away, BATCH, 0).reshape(pairs, -1, width)
-    fc2_sum = halve(fc2_here, fc2_away, BATCH, 0)
-    fc1_sum = scatter_rest(fc1_sum, False)
-    fc2_sum = scatter_rest(fc2_sum, True)
+    quick = quick_sums()
+    fc1_pair = (fc1_here.reshape(-1, width), fc1_away.reshape(-1, width))
+    fc2_pair = (fc2_here.reshape(-1, hidden_width), fc2_away.reshape(-1, hidden_width))
+    fc1_pair = swap(fc1_pair, BATCH, 0)
+    fc2_pair = swap(fc2_pair, BATCH, 0)
+    lanes = range(0, hidden_width, width)
+    near, far, by_x, by_y = (GRP, 0), (GRP, 1), (BATCH, 1), (BATCH, 2)
+    if quick:
+        fc1_rows, fc2_rows = fc1_pair[0].shape[0], fc2_pair[0].shape[0]
+        fc1_pair, fc2_pair = fold(
+            [fc1_pair, fc2_pair],
+            [by_x, near],
+            [(0, 0, fc1_rows, 0, 2, 0, 0, 0, 0)] + [(1, 0, fc2_rows, c, 8, 1, 1, 0, c) for c in lanes],
+            [(fc1_rows // 2, width), (fc2_rows // 2, hidden_width)],
+        )
+        fc1_pair = swap(fc1_pair, *by_x)
+        fc2_pair = swap(fc2_pair, *near)
+    else:
+        fc1_sum, fc2_sum = (
+            scatter_rest((pair[0].astype(F32) + pair[1].astype(F32)).reshape(pairs, -1, pair[0].shape[1]), flip)
+            for pair, flip in ((fc1_pair, False), (fc2_pair, True))
+        )
 
     output, middle_grad, proj_grad, turn_sums, turn_bias, *sent = turn(
         place,
@@ -817,32 +892,104 @@
 
     small = jnp.concatenate([slots(ff_small[:11]), slots(turn_bias)], axis=1).astype(BF16)
     small_length = small.shape[1]
-    small_rows = -(-small_length // width)
-    small = jnp.pad(small, ((0, 0), (0, small_rows * width - small_length))).reshape(devices, small_rows, width)
-    beside = scatter_sum(
-        jnp.concatenate([proj_grad.reshape(devices, -1, width), small], axis=1).reshape(-1, width), False
-    )
-    proj_sum = beside[:-small_rows]
-    small_sum = beside[-small_rows:].reshape(-1)
+    small_lanes = -(-small_length // 8)
+    small = jnp.pad(small, ((0, 0), (0, small_lanes * 8 - small_length))).reshape(devices, 8, small_lanes)
+    small = jnp.pad(small, ((0, 0), (0, 0), (0, width - small_lanes)))
+    beside = jnp.concatenate([proj_grad.reshape(devices, -1, width), small], axis=1).reshape(pairs, 2, -1, width)
+    beside_pair = tuple(
+        lax.dynamic_index_in_dim(beside, side, 1, keepdims=False).reshape(-1, width) for side in (half, 1 - half)
+    )
+    beside_pair = swap(beside_pair, BATCH, 0)
+
+    qkv_here, qkv_away, qv_sums, *sent = attend_back(
+        place, exchange(sent), mixed, projected, log_totals, qkv_weight
+    )
+    qkv_pair = swap((qkv_here.reshape(-1, width), qkv_away.reshape(-1, width)), BATCH, 0)
+    if quick:
+        beside_rows, qkv_rows = beside_pair[0].shape[0], qkv_pair[0].shape[0]
+        fc1_pair, fc2_pair, beside_pair = fold(
+            [fc1_pair, fc2_pair, beside_pair],
+            [by_y, far, by_x],
+            [(0, 0, fc1_rows // 2, 0, 1, 0, 0, 0, 0)]
+            + [(1, 0, fc2_rows // 2, c, 4, 1, 1, 0, c) for c in lanes]
+            + [(2, 0, beside_rows, 0, 2, 2, 2, 0, 0)],
+            [(fc1_rows // 4, width), (fc2_rows // 4, hidden_width), (beside_rows // 2, width)],
+        )
+        fc1_pair = swap(fc1_pair, *by_y)
+        fc2_pair = swap(fc2_pair, *far)
+        beside_pair = swap(beside_pair, *by_x)
+        (qkv_pair,) = fold([qkv_pair], [by_x], [(0, 0, qkv_rows, 0, 2, 0, 0, 0, 0)], [(qkv_rows // 2, width)])
+        qkv_pair = swap(qkv_pair, *by_x)
+    else:
+        beside, qkv_sum = (
+            scatter_rest((pair[0].astype(F32) + pair[1].astype(F32)).reshape(pairs, -1, width), flip)
+            for pair, flip in ((beside_pair, False), (qkv_pair, True))
+        )
+    latents_grad, finish_sums, conv_a_small = finish(
+        place, exchange(sent), latents_rim, modulation, conv_a, middle_grad
+    )
+    latents_grad = from_pairs(latents_grad)
+    if quick:
+        fc1_rows, fc2_rows, beside_rows, qkv_rows = fc1_rows // 4, fc2_rows // 4, beside_rows // 2, qkv_rows // 2
+        fc1_pair, fc2_pair = fold(
+            [fc1_pair, fc2_pair],
+            [near, by_x],
+            [(0, 0, fc1_rows, 0, 2, 0, 0, 0, 0)]
+            + [(1, 0, fc2_rows, c, 2, 1, 1, k * (fc2_rows // 2), 0) for k, c in enumerate(lanes)],
+            [(fc1_rows // 2, width), (len(lanes) * fc2_rows // 2, width)],
+        )
+        fc1_pair = swap(fc1_pair, *near)
+        fc2_pair = swap(fc2_pair, *by_x)
+        (attention_pair,) = fold(
+            [beside_pair, qkv_pair],
+            [by_y],
+            [(0, 0, beside_rows, 0, 1, 0, 0, 0, 0), (1, 0, qkv_rows, 0, 1, 0, 0, beside_rows // 2, 0)],
+            [((beside_rows + qkv_rows) // 2, width)],
+        )
+        attention_pair = swap(attention_pair, *by_y)
+        fc1_rows, fc2_rows = fc1_rows // 2, len(lanes) * fc2_rows // 2
+        beside_rows, qkv_rows = beside_rows // 2, qkv_rows // 2
+        fc1_pair, fc2_pair, attention_pair = fold(
+            [fc1_pair, fc2_pair, attention_pair],
+            [far, by_y, near],
+            [
+                (0, 0, fc1_rows, 0, 1, 0, 0, 0, 0),
+                (1, 0, fc2_rows, 0, len(lanes), 1, 1, 0, 0),
+                (2, 0, beside_rows, 0, 2, 2, 2, 0, 0),
+                (2, beside_rows, qkv_rows, 0, 2, 2, 2, beside_rows // 2, 0),
+            ],
+            [(fc1_rows // 2, width), (fc2_rows // 2, width), ((beside_rows + qkv_rows) // 2, width)],
+        )
+        fc1_pair = swap(fc1_pair, *far)
+        fc2_pair = swap(fc2_pair, *by_y)
+        attention_pair = swap(attention_pair, *near)
+        beside_rows, qkv_rows = beside_rows // 2, qkv_rows // 2
+        (attention_pair,) = fold(
+            [attention_pair],
+            [far],
+            [(0, 0, beside_rows, 0, 1, 0, 0, 0, 0), (0, beside_rows, qkv_rows, 0, 1, 0, 0, beside_rows // 2, 0)],
+            [((beside_rows + qkv_rows) // 2, width)],
+        )
+        attention_pair = swap(attention_pair, *far)
+        fc1_sum, fc2_sum, attention_sum = (
+            pair[0].astype(F32) + pair[1].astype(F32) for pair in (fc1_pair, fc2_pair, attention_pair)
+        )
+        fc2_sum = fc2_sum.reshape(len(lanes), -1, width).transpose(1, 0, 2).reshape(-1, hidden_width)
+        beside, qkv_sum = attention_sum[: beside_rows // 2], attention_sum[beside_rows // 2 :]
+    proj_sum = beside[:-8]
+    small_sum = beside[-8:, :small_lanes].reshape(-1)
     wide_length = 11 * (hidden_width // devices)
     wide_sum = small_sum[:wide_length].reshape(11, -1)
     narrow_sum = small_sum[wide_length:small_length].reshape(2, -1)
-
-    qkv_grad, qv_sums, *sent = attend_back(place, exchange(sent), mixed, projected, log_totals, qkv_weight)
-    qkv_sum = scatter_sum(qkv_grad, True)
-    latents_grad, finish_sums, conv_a_small = finish(
-        place, exchange(sent), latents_rim, modulation, conv_a, middle_grad
-    )
-    latents_grad = from_pairs(latents_grad)
     finish_sums = jnp.sum(finish_sums, axis=2)
 
-    late = jnp.concatenate([conv_a_small[:10], jnp.sum(qv_sums, axis=1)], axis=0)
-    modulation_grad = jnp.concatenate([finish_sums, turn_sums], axis=1)[0]
+    late = jnp.concatenate([conv_a_small[:10], jnp.sum(qv_sums, axis=1), jnp.zeros((4, width), F32)], axis=0)
+    modulation_grad = jnp.concatenate([finish_sums[0], turn_sums[0], jnp.zeros((2, width), F32)], axis=0)
     side = jnp.concatenate(
         [condition, jnp.pad(frequency_rows, ((0, 0), (0, width - frequency_rows.shape[1] - 1))), numbers[1:][None]],
         axis=1,
     )
-    every, late_sum = gather_sum(side.reshape(2, width), modulation_grad, late)
+    every, late_sum = gather_sum(jnp.pad(side.reshape(2, width), ((6, 0), (0, 0))), modulation_grad, late)
     every = every.reshape(-1, 8, width)
     every_grad = every[:, :6].reshape(-1, 6 * width)
     every_condition = every[:, 6]

time: 368 us -> 348 us (0.946)
  waiting for transfers between devices: 104 us -> 77.1 us
  Pallas kernels: 133 us -> 154 us
  starting transfers between devices: 69.2 us -> 52 us
  local copies, waits for them, and re-layouts: 23.3 us -> 28.1 us
    ppermute x32 -> x29, waiting for transfers between devices: 98.8 us -> 64.6 us  [swap_bit(): return lax.ppermute(value, axis, [(i, i ^ 1 << bit) for i in range(count)])]
    pallas_call x6 -> x13, Pallas kernels: 82.1 us -> 103 us  [call_whole(): pl.pallas_call(body, in_specs=[SCALARS] + [WHOLE] * (len(inputs) - 1), ou...]
    ppermute x32 -> x29, starting transfers between devices: 56.3 us -> 43.6 us  [swap_bit(): return lax.ppermute(value, axis, [(i, i ^ 1 << bit) for i in range(count)])]
    unnamed x53 -> x84, local copies, waits for them, and re-layouts: 6.84 us -> 14.8 us
    convert_element_type x16 -> x0, other arithmetic: 7.56 us -> none  [the longest x8 6.86 us: scatter_rest(): block = halve_dim(block.astype(BF16), left.index(bit), BATCH, bit)]
    ppermute x4, waiting for transfers between devices: 0.01 us -> 7.46 us  [from_pairs(): arrived.append(lax.ppermute(piece, (BATCH, GRP), pair_moves(k, True)))]
  transfers between devices with their start and end apart: 40 -> 37, of which waited for: 20 -> 19; matrix products, arithmetic and copies ran while one was open for 13% -> 12% of each run, Pallas kernels for 17% -> 17%
where the time goes in v1:
time: 348 us; the launch traced here: 347 us
  Pallas kernels  154 us (44%)
  waiting for transfers between devices  77.1 us (22%)
  starting transfers between devices  52 us (15%)
  local copies, waits for them, and re-layouts  28.1 us (8%)
  other arithmetic  24.7 us (7%)
  matrix products  9.12 us (3%)
    pallas_call x13, Pallas kernels, call_whole(): pl.pallas_call(body, in_specs=[SCALARS] + [WHOLE] * (len(inputs) - 1), ou...  103 us
    ppermute x29, waiting for transfers between devices, swap_bit(): return lax.ppermute(value, axis, [(i, i ^ 1 << bit) for i in range(count)])  64.6 us
    pallas_call x1, Pallas kernels, feed_forward(): pl.pallas_call(feed_forward_body, grid=(steps,), in_specs=[pl.BlockSpec(m...  50.8 us
    ppermute x29, starting transfers between devices, swap_bit(): return lax.ppermute(value, axis, [(i, i ^ 1 << bit) for i in range(count)])  43.6 us
    unnamed x84, local copies, waits for them, and re-layouts  14.8 us
    ppermute x4, waiting for transfers between devices, from_pairs(): arrived.append(lax.ppermute(piece, (BATCH, GRP), pair_moves(k, True)))  7.46 us
  transfers between devices with their start and end apart: 37, of which 19 were waited for; matrix products, arithmetic and copies ran while one was open for 12% of the time, Pallas kernels for 17%

profile of v1, /device:TPU:0, one launch (start us, length us, event | category | flops | bytes accessed | tf_op | source)
XLA Modules:
  0.0 346.7 jit_solution(11346804897586038934)
XLA Ops:
  4.3 2.6 collective-permute-start.6
  15.2 4.0 %fusion.16 = f32[3,4608]{1,0:T(4,128)S(1)} fusion(bf16[768,4608]{1,0:T(8,128)(2,1)} %param.28, bf16[1,768]{1,0:T(2,128)(2,1)S(1)} %get-tuple-element.177, bf16[1,768]{1,0:T(2,128)(2,1)S(1)} %get-tuple-element.176, bf16[1,768]{1,0:T(2,128)(2,1)S(1)} %get-tuple-element.137), kind=kOutput, calls=%fused_computation.72 | convolution fusion | flops 21247488 | bytes 7137792 | tf_op jit(solution)/shard_map/dot_general | solution.py:121
  19.3 5.0 %collective-permute-done = bf16[1,8,32,768]{3,2,1,0:T(8,128)(2,1)S(1)} collective-permute-done((bf16[1,8,32,768]{3,2,1,0:T(8,128)(2,1)S(1)}, bf16[1,8,32,768]{3,2,1,0:T(8,128)(2,1)S(1)}, u32[]{:S(2)}, u32[]{:S(2)}) %collective-permute-start) | collective-permute-done | bytes 393248 | tf_op jit(solution)/shard_map/ppermute | solution.py:31
  24.3 19.4 %collective-permute-start.2 = (bf16[1,2,32,768]{3,2,1,0:T(8,128)(2,1)S(1)}, bf16[1,2,32,768]{3,2,1,0:T(8,128)(2,1)S(1)}, u32[]{:S(2)}, u32[]{:S(2)}) collective-permute-start(bf16[1,2,32,768]{3,2,1,0:T(8,128)(2,1)S(1)} %slice_select_fusion), channel_id=1, source_target_pairs={{0,4},{4,0},{8,12},{12,8},{16,20},{20,16},{24,28},{28,24},{1,5},{5... | collective-permute-start | bytes 294920 | tf_op jit(solution)/shard_map/ppermute | solution.py:22
  45.8 7.6 %shard_map.348 = (bf16[2,8,16,768]{3,2,1,0:T(8,128)(2,1)}, bf16[2,8,16,768]{3,2,1,0:T(8,128)(2,1)}) custom-call(s32[3]{0:T(128)} %pad_add_fusion.place, bf16[1,20,32,768]{3,2,1,0:T(8,128)(2,1)} %pad_maximum_fusion.latents, f32[1,4608]{1,0:T(1,128)} %copy-done.22, bf16[9,768]{1,0:T(8,128)(2,1)} %taps.5, bf16[1,768]{1,0:T(2,128)(2,1)} %conv_bias.2), custom_call_target="tpu_custom_call" | custom-call | tf_op jit(solution)/shard_map/pallas_call | solution.py:386
  56.1 13.0 %shard_map.349 = (bf16[2,10,16,768]{3,2,1,0:T(8,128)(2,1)}, bf16[2,10,16,768]{3,2,1,0:T(8,128)(2,1)}, bf16[2,256,2304]{2,1,0:T(8,128)(2,1)}, f32[2,256,128]{2,1,0:T(8,128)}) custom-call(s32[3]{0:T(128)} %pad_add_fusion.place, bf16[2,8,16,768]{3,2,1,0:T(8,128)(2,1)} %get-tuple-element.76.part0, bf16[2,8,16,768]{3,2,1,0:T(8,128)(2,1)} %copy-done.11, ...), custom_call_target="tpu_custom_call" | custom-call | tf_op jit(solution)/shard_map/pallas_call | solution.py:386
  72.0 8.6 %shard_map.350 = (bf16[1,20,32,768]{3,2,1,0:T(8,128)(2,1)}, bf16[1,16,32,768]{3,2,1,0:T(8,128)(2,1)}, f32[1,16,32,768]{3,2,1,0:T(8,128)}) custom-call(s32[3]{0:T(128)} %pad_add_fusion.place, bf16[2,10,16,768]{3,2,1,0:T(8,128)(2,1)} %get-tuple-element.78.part0, bf16[2,10,16,768]{3,2,1,0:T(8,128)(2,1)} %copy-done.23, ...), custom_call_target="tpu_custom_call" | custom-call | tf_op jit(solution)/shard_map/pallas_call | solution.py:386
  81.8 50.8 %feed_forward.1 = (f32[512,768]{1,0:T(8,128)S(1)}, f32[512,768]{1,0:T(8,128)S(1)}, bf16[4,1,384,768]{3,2,1,0:T(8,128)(2,1)}, bf16[4,1,384,768]{3,2,1,0:T(8,128)(...) custom-call(s32[3]{0:T(128)S(1)} %copy-done.6, ...), custom_call_target="tpu_custom_call" | custom-call | tf_op jit(solution)/shard_map/feed_forward/pallas_call | solution.py:255
  134.9 12.1 %shard_map.351 = (bf16[1,16,32,768]{3,2,1,0:T(8,128)(2,1)}, f32[1,16,32,768]{3,2,1,0:T(8,128)}, bf16[768,768]{1,0:T(8,128)(2,1)}, f32[1,4,8,768]{3,2,1,0:T(8,128...) custom-call(s32[3]{0:T(128)} %pad_add_fusion.place, ...), custom_call_target="tpu_custom_call" | custom-call | tf_op jit(solution)/shard_map/pallas_call | solution.py:386
  149.7 20.7 %shard_map.352 = (bf16[4,288,768]{2,1,0:T(8,128)(2,1)}, bf16[4,288,768]{2,1,0:T(8,128)(2,1)}, f32[2,8,768]{2,1,0:T(8,128)}, bf16[2,9,16,768]{3,2,1,0:T(8,128)(2,1)}, bf16[2,9,16,768]{3,2,1,0:T(8,128)(2,1)}) custom-call(s32[3]{0:T(128)} %pad_add_fusion.place, bf16[2,8,16,768]{3,2,1,0:T(8,128)(2,1)} %get-tuple-element.86.up0, ...), custom_call_target="tpu_custom_call" | custom-call | tf_op jit(solution)/shard_map/pallas_call | solution.py:386
  176.3 13.8 %shard_map.353 = (bf16[1,16,32,768]{3,2,1,0:T(8,128)(2,1)}, f32[1,2,8,768]{3,2,1,0:T(8,128)}, f32[16,768]{1,0:T(8,128)}) custom-call(s32[3]{0:T(128)} %pad_add_fusion.place, bf16[2,9,16,768]{3,2,1,0:T(8,128)(2,1)} %get-tuple-element.90.part0, bf16[2,9,16,768]{3,2,1,0:T(8,128)(2,1)} %copy-done.24, bf16[1,20,32,768]{3,2,1,0:T(8,128)(2,1)} %pad_maximum_fusion.latents, ...), custom_call_target="tpu_custom_call" | custom-call | tf_op jit(solution)/shard_map/pallas_call | solution.py:386
  201.6 12.6 %collective-permute-done.17 = f32[32,768]{1,0:T(8,128)S(1)} collective-permute-done((f32[32,768]{1,0:T(8,128)S(1)}, f32[32,768]{1,0:T(8,128)S(1)}, u32[]{:S(2)}, u32[]{:S(2)}) %collective-permute-start.17) | collective-permute-done | bytes 98336 | tf_op jit(solution)/shard_map/ppermute | solution.py:22
  217.1 2.3 collective-permute-done.18
  221.3 2.0 collective-permute-start.13
  224.1 7.3 %shard_map.354 = (bf16[768,768]{1,0:T(8,128)(2,1)}, bf16[192,3072]{1,0:T(8,128)(2,1)}, bf16[768,768]{1,0:T(8,128)(2,1)}, bf16[192,3072]{1,0:T(8,128)(2,1)}) custom-call(s32[2]{0:T(128)} %pad_add_fusion.4.refs_0_, bf16[1536,768]{1,0:T(8,128)(2,1)} %bitcast.88, bf16[384,3072]{1,0:T(8,128)(2,1)} %bitcast.89, bf16[1536,768]{1,0:T(8,128)(2,1)} %copy-done.9, ...), custom_call_target="tpu_custom_call" | custom-call | tf_op jit(solution)/shard_map/pallas_call | solution.py:386
  235.0 7.5 %collective-permute-done.13 = bf16[1,8,32,768]{3,2,1,0:T(8,128)(2,1)S(1)} collective-permute-done((bf16[1,8,32,768]{3,2,1,0:T(8,128)(2,1)S(1)}, bf16[1,8,32,768]{3,2,1,0:T(8,128)(2,1)S(1)}, u32[]{:S(2)}, u32[]{:S(2)}) %collective-permute-start.13) | collective-permute-done | bytes 393248 | tf_op jit(solution)/shard_map/ppermute | solution.py:54
  246.5 3.7 %shard_map.357 = (bf16[576,768]{1,0:T(8,128)(2,1)}, bf16[576,768]{1,0:T(8,128)(2,1)}) custom-call(s32[1]{0:T(128)} %bitcast.19.refs_0_, bf16[1152,768]{1,0:T(8,128)(2,1)} %bitcast.90, bf16[1152,768]{1,0:T(8,128)(2,1)} %copy-done.10), custom_call_target="tpu_custom_call" | custom-call | tf_op jit(solution)/shard_map/pallas_call | solution.py:386
  250.1 2.4 collective-permute-start.29
  255.5 5.0 %collective-permute-done.22.refs_4_ = bf16[768,768]{1,0:T(8,128)(2,1)S(1)} collective-permute-done((bf16[768,768]{1,0:T(8,128)(2,1)}, bf16[768,768]{1,0:T(8,128)(2,1)S(1)}, u32[]{:S(2)}, u32[]{:S(2)}) %collective-permute-start.22) | collective-permute-done | bytes 1179680 | tf_op jit(solution)/shard_map/ppermute | solution.py:22
  260.5 7.3 %collective-permute-done.23.refs_5_ = bf16[192,3072]{1,0:T(8,128)(2,1)S(1)} collective-permute-done((bf16[192,3072]{1,0:T(8,128)(2,1)}, bf16[192,3072]{1,0:T(8,128)(2,1)S(1)}, u32[]{:S(2)}, u32[]{:S(2)}) %collective-permute-start.23) | collective-permute-done | bytes 1179680 | tf_op jit(solution)/shard_map/ppermute | solution.py:22
  268.9 5.4 %shard_map.355 = (bf16[384,768]{1,0:T(8,128)(2,1)}, bf16[96,3072]{1,0:T(8,128)(2,1)}, bf16[256,768]{1,0:T(8,128)(2,1)}, bf16[384,768]{1,0:T(8,128)(2,1)}, bf16[9...) custom-call(s32[3]{0:T(128)} %pad_add_fusion.3.refs_0_, bf16[768,768]{1,0:T(8,128)(2,1)} %get-tuple-element.102.refs_1_, ...), custom_call_target="tpu_custom_call" | custom-call | tf_op jit(solution)/shard_map/pallas_call | solution.py:386
  279.6 8.0 %collective-permute-done.28.refs_3_ = bf16[256,768]{1,0:T(8,128)(2,1)S(1)} collective-permute-done((bf16[256,768]{1,0:T(8,128)(2,1)}, bf16[256,768]{1,0:T(8,128)(2,1)S(1)}, u32[]{:S(2)}, u32[]{:S(2)}) %collective-permute-start.28) | collective-permute-done | bytes 393248 | tf_op jit(solution)/shard_map/ppermute | solution.py:22
  288.3 3.1 shard_map.358
  292.9 11.0 %collective-permute-done.26.refs_4_ = bf16[96,3072]{1,0:T(8,128)(2,1)S(1)} collective-permute-done((bf16[96,3072]{1,0:T(8,128)(2,1)}, bf16[96,3072]{1,0:T(8,128)(2,1)S(1)}, u32[]{:S(2)}, u32[]{:S(2)}) %collective-permute-start.26) | collective-permute-done | bytes 589856 | tf_op jit(solution)/shard_map/ppermute | solution.py:22
  304.7 2.9 shard_map.356
  311.6 3.2 collective-permute-done.30.refs_4_
  317.1 2.9 shard_map.359
  324.3 3.3 collective-permute-start.35
  329.3 3.2 collective-permute-done.33.refs_2_
  333.2 1.9 shard_map.360
  335.1 2.1 collective-permute-start.34
  337.9 4.5 %collective-permute-done.34 = bf16[104,768]{1,0:T(8,128)(2,1)S(1)} collective-permute-done((bf16[104,768]{1,0:T(8,128)(2,1)}, bf16[104,768]{1,0:T(8,128)(2,1)S(1)}, u32[]{:S(2)}, u32[]{:S(2)}) %collective-permute-start.34) | collective-permute-done | bytes 159776 | tf_op jit(solution)/shard_map/ppermute | solution.py:22
  (243 shorter events, 85.6 us)
Async XLA Ops:
  2.7 7.2 %collective-permute-start.3 = (f32[2,2]{1,0:T(2,128)}, f32[2,2]{1,0:T(2,128)}, u32[]{:S(2)}, u32[]{:S(2)}) collective-permute-start(f32[2,2]{1,0:T(2,128)} %pad_maximum_fusion.8), channel_id=1, source_target_pairs={{0,4},{4,0},{8,12},{12,8},{16,20},{20,16},{24,28},{28,24},{1,5},{5... | collective-permute-start | bytes 56 | tf_op jit(solution)/shard_map/ppermute | solution.py:22
  4.3 49.4 %collective-permute-start.6 = (bf16[1,8,32,768]{3,2,1,0:T(8,128)(2,1)S(1)}, bf16[1,8,32,768]{3,2,1,0:T(8,128)(2,1)S(1)}, u32[]{:S(2)}, u32[]{:S(2)}) collective-permute-start(bf16[1,8,32,768]{3,2,1,0:T(8,128)(2,1)S(1)} %get-tuple-element.152), channel_id=1, source_target_pairs={{0,1},{1,0},{2,5},{3,4},{4,3},{5,2},{6,7},{7,6},{8,9},{9,8},{10,13... | collective-permute-start | bytes 1179656 | tf_op jit(solution)/shard_map/ppermute | solution.py:31
  7.0 46.8 %collective-permute-start.7 = (bf16[1,8,32,768]{3,2,1,0:T(8,128)(2,1)S(1)}, bf16[1,8,32,768]{3,2,1,0:T(8,128)(2,1)S(1)}, u32[]{:S(2)}, u32[]{:S(2)}) collective-permute-start(bf16[1,8,32,768]{3,2,1,0:T(8,128)(2,1)S(1)} %get-tuple-element.153), channel_id=1, source_target_pairs={{0,0},{1,1},{2,4},{3,5},{4,2},{5,3},{6,6},{7,7},{8,8},{9,9},{10,12... | collective-permute-start | bytes 1179656 | tf_op jit(solution)/shard_map/ppermute | solution.py:31
  7.7 16.5 %collective-permute-start = (bf16[1,8,32,768]{3,2,1,0:T(8,128)(2,1)S(1)}, bf16[1,8,32,768]{3,2,1,0:T(8,128)(2,1)S(1)}, u32[]{:S(2)}, u32[]{:S(2)}) collective-permute-start(bf16[1,8,32,768]{3,2,1,0:T(8,128)(2,1)S(1)} %get-tuple-element.156), channel_id=1, source_target_pairs={{0,1},{1,0},{2,5},{3,4},{4,3},{5,2},{6,7},{7,6},{8,9},{9,8},{10,13... | collective-permute-start | bytes 1179656 | tf_op jit(solution)/shard_map/ppermute | solution.py:31
  7.8 16.4 %collective-permute-start.1 = (bf16[1,8,32,768]{3,2,1,0:T(8,128)(2,1)S(1)}, bf16[1,8,32,768]{3,2,1,0:T(8,128)(2,1)S(1)}, u32[]{:S(2)}, u32[]{:S(2)}) collective-permute-start(bf16[1,8,32,768]{3,2,1,0:T(8,128)(2,1)S(1)} %get-tuple-element.157), channel_id=1, source_target_pairs={{0,0},{1,1},{2,4},{3,5},{4,2},{5,3},{6,6},{7,7},{8,8},{9,9},{10,12... | collective-permute-start | bytes 1179656 | tf_op jit(solution)/shard_map/ppermute | solution.py:31
  24.3 20.4 %collective-permute-start.2 = (bf16[1,2,32,768]{3,2,1,0:T(8,128)(2,1)S(1)}, bf16[1,2,32,768]{3,2,1,0:T(8,128)(2,1)S(1)}, u32[]{:S(2)}, u32[]{:S(2)}) collective-permute-start(bf16[1,2,32,768]{3,2,1,0:T(8,128)(2,1)S(1)} %slice_select_fusion), channel_id=1, source_target_pairs={{0,4},{4,0},{8,12},{12,8},{16,20},{20,16},{24,28},{28,24},{1,5},{5... | collective-permute-start | bytes 294920 | tf_op jit(solution)/shard_map/ppermute | solution.py:22
  53.8 16.6 %collective-permute-start.8 = (bf16[1,1,32,768]{3,2,1,0:T(8,128)(2,1)S(1)}, bf16[1,1,32,768]{3,2,1,0:T(8,128)(2,1)S(1)}, u32[]{:S(2)}, u32[]{:S(2)}) collective-permute-start(bf16[1,1,32,768]{3,2,1,0:T(8,128)(2,1)S(1)} %slice_select_fusion.1), channel_id=1, source_target_pairs={{0,4},{4,0},{8,12},{12,8},{16,20},{20,16},{24,28},{28,24},{1,5},{5... | collective-permute-start | bytes 147464 | tf_op jit(solution)/shard_map/ppermute | solution.py:22
  170.4 5.2 %collective-permute-start.12 = (bf16[2,9,16,768]{3,2,1,0:T(8,128)(2,1)}, bf16[2,9,16,768]{3,2,1,0:T(8,128)(2,1)S(1)}, u32[]{:S(2)}, u32[]{:S(2)}) collective-permute-start(bf16[2,9,16,768]{3,2,1,0:T(8,128)(2,1)} %get-tuple-element.91), channel_id=1, source_target_pairs={{0,4},{4,0},{8,12},{12,8},{16,20},{20,16},{24,28},{28,24},{1,5},{5... | collective-permute-start | bytes 1327112 | tf_op jit(solution)/shard_map/ppermute | solution.py:22
  174.1 47.2 %collective-permute-start.20 = (bf16[1536,768]{1,0:T(8,128)(2,1)}, bf16[1536,768]{1,0:T(8,128)(2,1)S(1)}, u32[]{:S(2)}, u32[]{:S(2)}) collective-permute-start(bf16[1536,768]{1,0:T(8,128)(2,1)} %bitcast.110), channel_id=1, source_target_pairs={{0,4},{4,0},{8,12},{12,8},{16,20},{20,16},{24,28},{28,24},{1,5},{5... | collective-permute-start | bytes 7077896 | tf_op jit(solution)/shard_map/ppermute | solution.py:22
  174.3 49.0 %collective-permute-start.21 = (bf16[384,3072]{1,0:T(8,128)(2,1)}, bf16[384,3072]{1,0:T(8,128)(2,1)}, u32[]{:S(2)}, u32[]{:S(2)}) collective-permute-start(bf16[384,3072]{1,0:T(8,128)(2,1)} %bitcast.109), channel_id=1, source_target_pairs={{0,4},{4,0},{8,12},{12,8},{16,20},{20,16},{24,28},{28,24},{1,5},{5... | collective-permute-start | bytes 7077896 | tf_op jit(solution)/shard_map/ppermute | solution.py:22
  195.2 36.2 %collective-permute-start.10 = (bf16[1,8,32,768]{3,2,1,0:T(8,128)(2,1)}, bf16[1,8,32,768]{3,2,1,0:T(8,128)(2,1)S(1)}, u32[]{:S(2)}, u32[]{:S(2)}) collective-permute-start(bf16[1,8,32,768]{3,2,1,0:T(8,128)(2,1)} %get-tuple-element.149), channel_id=1, source_target_pairs={{0,0},{1,1},{4,2},{5,3},{2,4},{3,5},{6,6},{7,7},{8,8},{9,9},{12,10... | collective-permute-start | bytes 1179656 | tf_op jit(solution)/shard_map/ppermute | solution.py:54
  198.7 15.6 %collective-permute-start.17 = (f32[32,768]{1,0:T(8,128)S(1)}, f32[32,768]{1,0:T(8,128)S(1)}, u32[]{:S(2)}, u32[]{:S(2)}) collective-permute-start(f32[32,768]{1,0:T(8,128)S(1)} %pad_maximum_fusion.5), channel_id=1, source_target_pairs={{0,2},{1,3},{2,0},{3,1},{4,6},{5,7},{6,4},{7,5},{8,10},{9,11},{10,... | collective-permute-start | bytes 294920 | tf_op jit(solution)/shard_map/ppermute | solution.py:22
  201.4 43.8 %collective-permute-start.27 = (bf16[1152,768]{1,0:T(8,128)(2,1)}, bf16[1152,768]{1,0:T(8,128)(2,1)S(1)}, u32[]{:S(2)}, u32[]{:S(2)}) collective-permute-start(bf16[1152,768]{1,0:T(8,128)(2,1)} %bitcast.32), channel_id=1, source_target_pairs={{0,4},{4,0},{8,12},{12,8},{16,20},{20,16},{24,28},{28,24},{1,5},{5... | collective-permute-start | bytes 5308424 | tf_op jit(solution)/shard_map/ppermute | solution.py:22
  214.3 5.2 %collective-permute-start.18 = (f32[48,768]{1,0:T(8,128)S(1)}, f32[48,768]{1,0:T(8,128)S(1)}, u32[]{:S(2)}, u32[]{:S(2)}) collective-permute-start(f32[48,768]{1,0:T(8,128)S(1)} %pad_maximum_fusion.4), channel_id=1, source_target_pairs={{0,8},{4,12},{8,0},{12,4},{16,24},{20,28},{24,16},{28,20},{1,9},{5... | collective-permute-start | bytes 442376 | tf_op jit(solution)/shard_map/ppermute | solution.py:22
  219.5 13.5 %collective-permute-start.9 = (bf16[1,8,32,768]{3,2,1,0:T(8,128)(2,1)}, bf16[1,8,32,768]{3,2,1,0:T(8,128)(2,1)S(1)}, u32[]{:S(2)}, u32[]{:S(2)}) collective-permute-start(bf16[1,8,32,768]{3,2,1,0:T(8,128)(2,1)} %get-tuple-element.148), channel_id=1, source_target_pairs={{1,0},{0,1},{5,2},{4,3},{3,4},{2,5},{7,6},{6,7},{9,8},{8,9},{13,10... | collective-permute-start | bytes 1179656 | tf_op jit(solution)/shard_map/ppermute | solution.py:54
  221.3 21.2 %collective-permute-start.13 = (bf16[1,8,32,768]{3,2,1,0:T(8,128)(2,1)S(1)}, bf16[1,8,32,768]{3,2,1,0:T(8,128)(2,1)S(1)}, u32[]{:S(2)}, u32[]{:S(2)}) collective-permute-start(bf16[1,8,32,768]{3,2,1,0:T(8,128)(2,1)S(1)} %get-tuple-element.144), channel_id=1, source_target_pairs={{1,0},{0,1},{5,2},{4,3},{3,4},{2,5},{7,6},{6,7},{9,8},{8,9},{13,10... | collective-permute-start | bytes 1179656 | tf_op jit(solution)/shard_map/ppermute | solution.py:54
  223.4 19.1 %collective-permute-start.14 = (bf16[1,8,32,768]{3,2,1,0:T(8,128)(2,1)S(1)}, bf16[1,8,32,768]{3,2,1,0:T(8,128)(2,1)S(1)}, u32[]{:S(2)}, u32[]{:S(2)}) collective-permute-start(bf16[1,8,32,768]{3,2,1,0:T(8,128)(2,1)S(1)} %get-tuple-element.145), channel_id=1, source_target_pairs={{0,0},{1,1},{4,2},{5,3},{2,4},{3,5},{6,6},{7,7},{8,8},{9,9},{12,10... | collective-permute-start | bytes 1179656 | tf_op jit(solution)/shard_map/ppermute | solution.py:54
  231.4 29.1 %collective-permute-start.22 = (bf16[768,768]{1,0:T(8,128)(2,1)}, bf16[768,768]{1,0:T(8,128)(2,1)S(1)}, u32[]{:S(2)}, u32[]{:S(2)}) collective-permute-start(bf16[768,768]{1,0:T(8,128)(2,1)} %get-tuple-element.107), channel_id=1, source_target_pairs={{0,8},{4,12},{8,0},{12,4},{16,24},{20,28},{24,16},{28,20},{1,9},{5... | collective-permute-start | bytes 3538952 | tf_op jit(solution)/shard_map/ppermute | solution.py:22
  233.0 34.9 %collective-permute-start.23 = (bf16[192,3072]{1,0:T(8,128)(2,1)}, bf16[192,3072]{1,0:T(8,128)(2,1)S(1)}, u32[]{:S(2)}, u32[]{:S(2)}) collective-permute-start(bf16[192,3072]{1,0:T(8,128)(2,1)} %get-tuple-element.108), channel_id=1, source_target_pairs={{0,1},{1,0},{2,3},{3,2},{4,5},{5,4},{6,7},{7,6},{8,9},{9,8},{10,11... | collective-permute-start | bytes 3538952 | tf_op jit(solution)/shard_map/ppermute | solution.py:22
  242.5 13.0 %collective-permute-start.24 = (bf16[512,768]{1,0:T(8,128)(2,1)}, bf16[512,768]{1,0:T(8,128)(2,1)S(1)}, u32[]{:S(2)}, u32[]{:S(2)}) collective-permute-start(bf16[512,768]{1,0:T(8,128)(2,1)} %bitcast.30), channel_id=1, source_target_pairs={{0,4},{4,0},{8,12},{12,8},{16,20},{20,16},{24,28},{28,24},{1,5},{5... | collective-permute-start | bytes 2359304 | tf_op jit(solution)/shard_map/ppermute | solution.py:22
  242.5 12.0 %collective-permute-start.19 = (f32[80,768]{1,0:T(8,128)}, f32[80,768]{1,0:T(8,128)S(1)}, u32[]{:S(2)}, u32[]{:S(2)}) collective-permute-start(f32[80,768]{1,0:T(8,128)} %get-tuple-element.158), channel_id=1, source_target_pairs={{0,16},{4,20},{8,24},{12,28},{16,0},{20,4},{24,8},{28,12},{1,17},{... | collective-permute-start | bytes 737288 | tf_op jit(solution)/shard_map/ppermute | solution.py:22
  250.1 29.4 %collective-permute-start.29 = (bf16[576,768]{1,0:T(8,128)(2,1)}, bf16[576,768]{1,0:T(8,128)(2,1)}, u32[]{:S(2)}, u32[]{:S(2)}) collective-permute-start(bf16[576,768]{1,0:T(8,128)(2,1)} %get-tuple-element.120), channel_id=1, source_target_pairs={{0,8},{4,12},{8,0},{12,4},{16,24},{20,28},{24,16},{28,20},{1,9},{5... | collective-permute-start | bytes 2654216 | tf_op jit(solution)/shard_map/ppermute | solution.py:22
  274.3 13.2 %collective-permute-start.28 = (bf16[256,768]{1,0:T(8,128)(2,1)}, bf16[256,768]{1,0:T(8,128)(2,1)S(1)}, u32[]{:S(2)}, u32[]{:S(2)}) collective-permute-start(bf16[256,768]{1,0:T(8,128)(2,1)} %get-tuple-element.119), channel_id=1, source_target_pairs={{0,8},{4,12},{8,0},{12,4},{16,24},{20,28},{24,16},{28,20},{1,9},{5... | collective-permute-start | bytes 1179656 | tf_op jit(solution)/shard_map/ppermute | solution.py:22
  275.8 17.1 %collective-permute-start.25 = (bf16[384,768]{1,0:T(8,128)(2,1)}, bf16[384,768]{1,0:T(8,128)(2,1)S(1)}, u32[]{:S(2)}, u32[]{:S(2)}) collective-permute-start(bf16[384,768]{1,0:T(8,128)(2,1)} %get-tuple-element.111), channel_id=1, source_target_pairs={{0,16},{4,20},{8,24},{12,28},{16,0},{20,4},{24,8},{28,12},{1,17},{... | collective-permute-start | bytes 1769480 | tf_op jit(solution)/shard_map/ppermute | solution.py:22
  277.3 26.5 %collective-permute-start.26 = (bf16[96,3072]{1,0:T(8,128)(2,1)}, bf16[96,3072]{1,0:T(8,128)(2,1)S(1)}, u32[]{:S(2)}, u32[]{:S(2)}) collective-permute-start(bf16[96,3072]{1,0:T(8,128)(2,1)} %get-tuple-element.112), channel_id=1, source_target_pairs={{0,2},{1,3},{2,0},{3,1},{4,6},{5,7},{6,4},{7,5},{8,10},{9,11},{10,... | collective-permute-start | bytes 1769480 | tf_op jit(solution)/shard_map/ppermute | solution.py:22
  291.4 24.8 %collective-permute-start.32 = (bf16[416,768]{1,0:T(8,128)(2,1)}, bf16[416,768]{1,0:T(8,128)(2,1)S(1)}, u32[]{:S(2)}, u32[]{:S(2)}) collective-permute-start(bf16[416,768]{1,0:T(8,128)(2,1)} %get-tuple-element.124), channel_id=1, source_target_pairs={{0,16},{4,20},{8,24},{12,28},{16,0},{20,4},{24,8},{28,12},{1,17},{... | collective-permute-start | bytes 1916936 | tf_op jit(solution)/shard_map/ppermute | solution.py:22
  307.5 7.2 %collective-permute-start.30 = (bf16[192,768]{1,0:T(8,128)(2,1)}, bf16[192,768]{1,0:T(8,128)(2,1)S(1)}, u32[]{:S(2)}, u32[]{:S(2)}) collective-permute-start(bf16[192,768]{1,0:T(8,128)(2,1)} %get-tuple-element.122), channel_id=1, source_target_pairs={{0,1},{1,0},{2,3},{3,2},{4,5},{5,4},{6,7},{7,6},{8,9},{9,8},{10,11... | collective-permute-start | bytes 884744 | tf_op jit(solution)/shard_map/ppermute | solution.py:22
  307.5 8.6 %collective-permute-start.31 = (bf16[192,768]{1,0:T(8,128)(2,1)}, bf16[192,768]{1,0:T(8,128)(2,1)S(1)}, u32[]{:S(2)}, u32[]{:S(2)}) collective-permute-start(bf16[192,768]{1,0:T(8,128)(2,1)} %get-tuple-element.123), channel_id=1, source_target_pairs={{0,8},{4,12},{8,0},{12,4},{16,24},{20,28},{24,16},{28,20},{1,9},{5... | collective-permute-start | bytes 884744 | tf_op jit(solution)/shard_map/ppermute | solution.py:22
  320.0 7.5 %collective-permute-start.36 = (bf16[96,768]{1,0:T(8,128)(2,1)}, bf16[96,768]{1,0:T(8,128)(2,1)S(1)}, u32[]{:S(2)}, u32[]{:S(2)}) collective-permute-start(bf16[96,768]{1,0:T(8,128)(2,1)} %get-tuple-element.132), channel_id=1, source_target_pairs={{0,16},{4,20},{8,24},{12,28},{16,0},{20,4},{24,8},{28,12},{1,17},{... | collective-permute-start | bytes 442376 | tf_op jit(solution)/shard_map/ppermute | solution.py:22
  321.4 11.1 %collective-permute-start.33 = (bf16[208,768]{1,0:T(8,128)(2,1)}, bf16[208,768]{1,0:T(8,128)(2,1)S(1)}, u32[]{:S(2)}, u32[]{:S(2)}) collective-permute-start(bf16[208,768]{1,0:T(8,128)(2,1)} %get-tuple-element.126), channel_id=1, source_target_pairs={{0,1},{1,0},{2,3},{3,2},{4,5},{5,4},{6,7},{7,6},{8,9},{9,8},{10,11... | collective-permute-start | bytes 958472 | tf_op jit(solution)/shard_map/ppermute | solution.py:22
  324.3 12.9 %collective-permute-start.35 = (bf16[96,768]{1,0:T(8,128)(2,1)}, bf16[96,768]{1,0:T(8,128)(2,1)S(1)}, u32[]{:S(2)}, u32[]{:S(2)}) collective-permute-start(bf16[96,768]{1,0:T(8,128)(2,1)} %get-tuple-element.130), channel_id=1, source_target_pairs={{0,2},{1,3},{2,0},{3,1},{4,6},{5,7},{6,4},{7,5},{8,10},{9,11},{10,... | collective-permute-start | bytes 442376 | tf_op jit(solution)/shard_map/ppermute | solution.py:22
  335.1 7.4 %collective-permute-start.34 = (bf16[104,768]{1,0:T(8,128)(2,1)}, bf16[104,768]{1,0:T(8,128)(2,1)S(1)}, u32[]{:S(2)}, u32[]{:S(2)}) collective-permute-start(bf16[104,768]{1,0:T(8,128)(2,1)} %get-tuple-element.128), channel_id=1, source_target_pairs={{0,2},{1,3},{2,0},{3,1},{4,6},{5,7},{6,4},{7,5},{8,10},{9,11},{10,... | collective-permute-start | bytes 479240 | tf_op jit(solution)/shard_map/ppermute | solution.py:22
  (45 other events, 324.0 us)

commit v2 on v1

--- a/solution.py
+++ b/solution.py
@@ -198,7 +198,7 @@
         for l in range(count):
             forward_row(l, 0, None)
             forward_row(l, rows + 1, None)
-            sums = lax.fori_loop(1, rows + 1, lambda r, sums, l=l: forward_row(l, r, sums), sums)
+            sums = lax.fori_loop(1, rows + 1, lambda r, sums, l=l: forward_row(l, r, sums), sums, unroll=2)
 
             def backward_row(r, bias_sum, l=l):
                 near = [convolved_grad[l, r + 2 - a, :, here] for a in range(3)]
@@ -208,7 +208,7 @@
                 hidden_grad[l, r, :, here] = rounded
                 return bias_sum + fold_rows(rounded.astype(F32))
 
-            bias_sum = lax.fori_loop(0, rows, backward_row, bias_sum)
+            bias_sum = lax.fori_loop(0, rows, backward_row, bias_sum, unroll=2)
         for k in range(10):
             small_out[k : k + 1, here] = jnp.sum(sums[k], axis=0, keepdims=True)
         small_out[10:11, here] = jnp.sum(bias_sum, axis=0, keepdims=True)
@@ -358,7 +358,7 @@
                 normed[l, r, h : h + 16] = (unit * scaling + offset).astype(BF16).astype(F32)
             return carry
 
-        lax.fori_loop(0, rim_rows, norm_row, 0)
+        lax.fori_loop(0, rim_rows, norm_row, 0, unroll=2)
         normed[l, 0] = normed[l, 0] * place[1].astype(F32)
         normed[l, rows + 1] = normed[l, rows + 1] * place[2].astype(F32)
     for start in range(0, width, lanes):
@@ -374,7 +374,7 @@
                 mixed[l, r, here.start // lanes] = total
                 return carry
 
-            lax.fori_loop(0, rows, conv_row, 0)
+            lax.fori_loop(0, rows, conv_row, 0, unroll=2)
     pack_strips(mixed, (out0, out1), place[0])
 
 
@@ -446,7 +446,7 @@
             attended[l, :, :, pl.ds(start, lanes)] = both.reshape(len(parts) * halves, cols, lanes)
             return carry
 
-        lax.fori_loop(0, width // lanes, pair, 0, unroll=2)
+        lax.fori_loop(0, width // lanes, pair, 0, unroll=3)
     send_rows(attended, (out0, out1), me, halves, 1, 0)
 
 
@@ -498,7 +498,7 @@
                 normed[l, r, h : h + 16] = (unit * scaling + offset).astype(BF16)
             return carry
 
-        lax.fori_loop(0, rim_rows, norm_row, 0)
+        lax.fori_loop(0, rim_rows, norm_row, 0, unroll=2)
 
 
 def middle_part(place, parts, latents_rim, modulation, weight, bias):
@@ -551,7 +551,7 @@
                 bias_sums[1] += fold_rows((gate_two * upstream).astype(BF16).astype(F32))
             return carry
 
-        lax.fori_loop(0, rows, one_row, 0)
+        lax.fori_loop(0, rows, one_row, 0, unroll=2)
     tokens = count * rows * cols
     back = branch_grad[...].reshape(tokens, width)
     weight_grad[...] = lax.dot_general(
@@ -632,7 +632,7 @@
                     bias_sums[k // 2, :, here[0]] += fold_rows(both.astype(F32))
             return carry
 
-        lax.fori_loop(0, width // lanes, pair, 0, unroll=2)
+        lax.fori_loop(0, width // lanes, pair, 0, unroll=3)
     every = grads[...].reshape(count * tokens, 3 * width)
     weight_grad[...] = lax.dot_general(
         every, gathered[...].reshape(count * tokens, width), turned, preferred_element_type=F32
@@ -681,7 +681,7 @@
                 normed[l, r, h : h + 16] = (unit * scaling + offset).astype(BF16).astype(F32)
             return carry
 
-        lax.fori_loop(0, rows, norm_row, 0)
+        lax.fori_loop(0, rows, norm_row, 0, unroll=2)
     for start in range(0, width, lanes):
         here = slice(start, start + lanes)
         tap = [taps[k : k + 1, here].astype(F32) for k in range(9)]
@@ -697,7 +697,7 @@
                 added = [found[3 * a + e] + fold_rows(near[a] * moved[e]) for a in range(3) for e in range(3)]
                 return tuple(added) + (found[9] + fold_rows(near[1]),)
 
-            found = lax.fori_loop(0, rows, conv_row, found)
+            found = lax.fori_loop(0, rows, conv_row, found, unroll=2)
         for k in range(10):
             small[k : k + 1, here] = jnp.sum(found[k], axis=0, keepdims=True)
     sums[...] = jnp.zeros_like(sums)
@@ -715,7 +715,7 @@
                 latents_grad[l, r, here] = pulled.astype(BF16)
             return carry
 
-        lax.fori_loop(0, rows, pull_row, 0)
+        lax.fori_loop(0, rows, pull_row, 0, unroll=2)
 
 
 def finish(place, parts, latents_rim, modulation, taps, middle_grad):

time: 348 us -> 331 us (0.951)
  Pallas kernels: 154 us -> 137 us
    pallas_call x13, Pallas kernels: 103 us -> 90.8 us  [call_whole(): pl.pallas_call(body, in_specs=[SCALARS] + [WHOLE] * (len(inputs) - 1), ou...]
    pallas_call x1, Pallas kernels: 50.8 us -> 46 us  [feed_forward(): pl.pallas_call(feed_forward_body, grid=(steps,), in_specs=[pl.BlockSpec(m...]
  transfers between devices with their start and end apart: 37 -> 37, of which waited for: 19 -> 19; matrix products, arithmetic and copies ran while one was open for 12% -> 13% of each run, Pallas kernels for 17% -> 16%
where the time goes in v2:
time: 331 us; the launch traced here: 330 us
  Pallas kernels  137 us (41%)
  waiting for transfers between devices  77.2 us (23%)
  starting transfers between devices  52.1 us (16%)
  local copies, waits for them, and re-layouts  28.1 us (8%)
  other arithmetic  24.7 us (7%)
  matrix products  9.12 us (3%)
    pallas_call x13, Pallas kernels, call_whole(): pl.pallas_call(body, in_specs=[SCALARS] + [WHOLE] * (len(inputs) - 1), ou...  90.8 us
    ppermute x29, waiting for transfers between devices, swap_bit(): return lax.ppermute(value, axis, [(i, i ^ 1 << bit) for i in range(count)])  64.3 us
    pallas_call x1, Pallas kernels, feed_forward(): pl.pallas_call(feed_forward_body, grid=(steps,), in_specs=[pl.BlockSpec(m...  46 us
    ppermute x29, starting transfers between devices, swap_bit(): return lax.ppermute(value, axis, [(i, i ^ 1 << bit) for i in range(count)])  43.7 us
    unnamed x84, local copies, waits for them, and re-layouts  14.8 us
    ppermute x4, waiting for transfers between devices, from_pairs(): arrived.append(lax.ppermute(piece, (BATCH, GRP), pair_moves(k, True)))  7.91 us
  transfers between devices with their start and end apart: 37, of which 19 were waited for; matrix products, arithmetic and copies ran while one was open for 13% of the time, Pallas kernels for 16%

profile of v2, /device:TPU:0, one launch (start us, length us, event | category | flops | bytes accessed | tf_op | source)
XLA Modules:
  0.0 330.0 jit_solution(11147923787437721331)
XLA Ops:
  4.3 2.6 collective-permute-start.6
  15.2 4.0 %fusion.16 = f32[3,4608]{1,0:T(4,128)S(1)} fusion(bf16[768,4608]{1,0:T(8,128)(2,1)} %param.28, bf16[1,768]{1,0:T(2,128)(2,1)S(1)} %get-tuple-element.177, bf16[1,768]{1,0:T(2,128)(2,1)S(1)} %get-tuple-element.176, bf16[1,768]{1,0:T(2,128)(2,1)S(1)} %get-tuple-element.137), kind=kOutput, calls=%fused_computation.72 | convolution fusion | flops 21247488 | bytes 7137792 | tf_op jit(solution)/shard_map/dot_general | solution.py:121
  19.3 5.0 %collective-permute-done = bf16[1,8,32,768]{3,2,1,0:T(8,128)(2,1)S(1)} collective-permute-done((bf16[1,8,32,768]{3,2,1,0:T(8,128)(2,1)S(1)}, bf16[1,8,32,768]{3,2,1,0:T(8,128)(2,1)S(1)}, u32[]{:S(2)}, u32[]{:S(2)}) %collective-permute-start) | collective-permute-done | bytes 393248 | tf_op jit(solution)/shard_map/ppermute | solution.py:31
  24.3 19.4 %collective-permute-start.2 = (bf16[1,2,32,768]{3,2,1,0:T(8,128)(2,1)S(1)}, bf16[1,2,32,768]{3,2,1,0:T(8,128)(2,1)S(1)}, u32[]{:S(2)}, u32[]{:S(2)}) collective-permute-start(bf16[1,2,32,768]{3,2,1,0:T(8,128)(2,1)S(1)} %slice_select_fusion), channel_id=1, source_target_pairs={{0,4},{4,0},{8,12},{12,8},{16,20},{20,16},{24,28},{28,24},{1,5},{5... | collective-permute-start | bytes 294920 | tf_op jit(solution)/shard_map/ppermute | solution.py:22
  45.8 5.6 %shard_map.348 = (bf16[2,8,16,768]{3,2,1,0:T(8,128)(2,1)}, bf16[2,8,16,768]{3,2,1,0:T(8,128)(2,1)}) custom-call(s32[3]{0:T(128)} %pad_add_fusion.place, bf16[1,20,32,768]{3,2,1,0:T(8,128)(2,1)} %pad_maximum_fusion.latents, f32[1,4608]{1,0:T(1,128)} %copy-done.22, bf16[9,768]{1,0:T(8,128)(2,1)} %taps.5, bf16[1,768]{1,0:T(2,128)(2,1)} %conv_bias.2), custom_call_target="tpu_custom_call" | custom-call | tf_op jit(solution)/shard_map/pallas_call | solution.py:386
  54.1 11.6 %shard_map.349 = (bf16[2,10,16,768]{3,2,1,0:T(8,128)(2,1)}, bf16[2,10,16,768]{3,2,1,0:T(8,128)(2,1)}, bf16[2,256,2304]{2,1,0:T(8,128)(2,1)}, f32[2,256,128]{2,1,0:T(8,128)}) custom-call(s32[3]{0:T(128)} %pad_add_fusion.place, bf16[2,8,16,768]{3,2,1,0:T(8,128)(2,1)} %get-tuple-element.76.part0, bf16[2,8,16,768]{3,2,1,0:T(8,128)(2,1)} %copy-done.11, ...), custom_call_target="tpu_custom_call" | custom-call | tf_op jit(solution)/shard_map/pallas_call | solution.py:386
  68.6 6.8 %shard_map.350 = (bf16[1,20,32,768]{3,2,1,0:T(8,128)(2,1)}, bf16[1,16,32,768]{3,2,1,0:T(8,128)(2,1)}, f32[1,16,32,768]{3,2,1,0:T(8,128)}) custom-call(s32[3]{0:T(128)} %pad_add_fusion.place, bf16[2,10,16,768]{3,2,1,0:T(8,128)(2,1)} %get-tuple-element.78.part0, bf16[2,10,16,768]{3,2,1,0:T(8,128)(2,1)} %copy-done.23, ...), custom_call_target="tpu_custom_call" | custom-call | tf_op jit(solution)/shard_map/pallas_call | solution.py:386
  76.6 46.0 %feed_forward.1 = (f32[512,768]{1,0:T(8,128)S(1)}, f32[512,768]{1,0:T(8,128)S(1)}, bf16[4,1,384,768]{3,2,1,0:T(8,128)(2,1)}, bf16[4,1,384,768]{3,2,1,0:T(8,128)(...) custom-call(s32[3]{0:T(128)S(1)} %copy-done.6, ...), custom_call_target="tpu_custom_call" | custom-call | tf_op jit(solution)/shard_map/feed_forward/pallas_call | solution.py:255
  124.9 10.2 %shard_map.351 = (bf16[1,16,32,768]{3,2,1,0:T(8,128)(2,1)}, f32[1,16,32,768]{3,2,1,0:T(8,128)}, bf16[768,768]{1,0:T(8,128)(2,1)}, f32[1,4,8,768]{3,2,1,0:T(8,128...) custom-call(s32[3]{0:T(128)} %pad_add_fusion.place, ...), custom_call_target="tpu_custom_call" | custom-call | tf_op jit(solution)/shard_map/pallas_call | solution.py:386
  137.8 19.6 %shard_map.352 = (bf16[4,288,768]{2,1,0:T(8,128)(2,1)}, bf16[4,288,768]{2,1,0:T(8,128)(2,1)}, f32[2,8,768]{2,1,0:T(8,128)}, bf16[2,9,16,768]{3,2,1,0:T(8,128)(2,1)}, bf16[2,9,16,768]{3,2,1,0:T(8,128)(2,1)}) custom-call(s32[3]{0:T(128)} %pad_add_fusion.place, bf16[2,8,16,768]{3,2,1,0:T(8,128)(2,1)} %get-tuple-element.86.up0, ...), custom_call_target="tpu_custom_call" | custom-call | tf_op jit(solution)/shard_map/pallas_call | solution.py:386
  163.4 10.0 %shard_map.353 = (bf16[1,16,32,768]{3,2,1,0:T(8,128)(2,1)}, f32[1,2,8,768]{3,2,1,0:T(8,128)}, f32[16,768]{1,0:T(8,128)}) custom-call(s32[3]{0:T(128)} %pad_add_fusion.place, bf16[2,9,16,768]{3,2,1,0:T(8,128)(2,1)} %get-tuple-element.90.part0, bf16[2,9,16,768]{3,2,1,0:T(8,128)(2,1)} %copy-done.24, bf16[1,20,32,768]{3,2,1,0:T(8,128)(2,1)} %pad_maximum_fusion.latents, ...), custom_call_target="tpu_custom_call" | custom-call | tf_op jit(solution)/shard_map/pallas_call | solution.py:386
  185.1 12.4 %collective-permute-done.17 = f32[32,768]{1,0:T(8,128)S(1)} collective-permute-done((f32[32,768]{1,0:T(8,128)S(1)}, f32[32,768]{1,0:T(8,128)S(1)}, u32[]{:S(2)}, u32[]{:S(2)}) %collective-permute-start.17) | collective-permute-done | bytes 98336 | tf_op jit(solution)/shard_map/ppermute | solution.py:22
  200.4 2.3 collective-permute-done.18
  204.6 2.0 collective-permute-start.13
  207.3 7.1 %shard_map.354 = (bf16[768,768]{1,0:T(8,128)(2,1)}, bf16[192,3072]{1,0:T(8,128)(2,1)}, bf16[768,768]{1,0:T(8,128)(2,1)}, bf16[192,3072]{1,0:T(8,128)(2,1)}) custom-call(s32[2]{0:T(128)} %pad_add_fusion.4.refs_0_, bf16[1536,768]{1,0:T(8,128)(2,1)} %bitcast.88, bf16[384,3072]{1,0:T(8,128)(2,1)} %bitcast.89, bf16[1536,768]{1,0:T(8,128)(2,1)} %copy-done.9, ...), custom_call_target="tpu_custom_call" | custom-call | tf_op jit(solution)/shard_map/pallas_call | solution.py:386
  218.1 7.9 %collective-permute-done.13 = bf16[1,8,32,768]{3,2,1,0:T(8,128)(2,1)S(1)} collective-permute-done((bf16[1,8,32,768]{3,2,1,0:T(8,128)(2,1)S(1)}, bf16[1,8,32,768]{3,2,1,0:T(8,128)(2,1)S(1)}, u32[]{:S(2)}, u32[]{:S(2)}) %collective-permute-start.13) | collective-permute-done | bytes 393248 | tf_op jit(solution)/shard_map/ppermute | solution.py:54
  229.9 3.7 %shard_map.357 = (bf16[576,768]{1,0:T(8,128)(2,1)}, bf16[576,768]{1,0:T(8,128)(2,1)}) custom-call(s32[1]{0:T(128)} %bitcast.19.refs_0_, bf16[1152,768]{1,0:T(8,128)(2,1)} %bitcast.90, bf16[1152,768]{1,0:T(8,128)(2,1)} %copy-done.10), custom_call_target="tpu_custom_call" | custom-call | tf_op jit(solution)/shard_map/pallas_call | solution.py:386
  233.6 2.4 collective-permute-start.29
  239.0 4.6 %collective-permute-done.22.refs_4_ = bf16[768,768]{1,0:T(8,128)(2,1)S(1)} collective-permute-done((bf16[768,768]{1,0:T(8,128)(2,1)}, bf16[768,768]{1,0:T(8,128)(2,1)S(1)}, u32[]{:S(2)}, u32[]{:S(2)}) %collective-permute-start.22) | collective-permute-done | bytes 1179680 | tf_op jit(solution)/shard_map/ppermute | solution.py:22
  243.6 7.5 %collective-permute-done.23.refs_5_ = bf16[192,3072]{1,0:T(8,128)(2,1)S(1)} collective-permute-done((bf16[192,3072]{1,0:T(8,128)(2,1)}, bf16[192,3072]{1,0:T(8,128)(2,1)S(1)}, u32[]{:S(2)}, u32[]{:S(2)}) %collective-permute-start.23) | collective-permute-done | bytes 1179680 | tf_op jit(solution)/shard_map/ppermute | solution.py:22
  252.1 5.4 %shard_map.355 = (bf16[384,768]{1,0:T(8,128)(2,1)}, bf16[96,3072]{1,0:T(8,128)(2,1)}, bf16[256,768]{1,0:T(8,128)(2,1)}, bf16[384,768]{1,0:T(8,128)(2,1)}, bf16[9...) custom-call(s32[3]{0:T(128)} %pad_add_fusion.3.refs_0_, bf16[768,768]{1,0:T(8,128)(2,1)} %get-tuple-element.102.refs_1_, ...), custom_call_target="tpu_custom_call" | custom-call | tf_op jit(solution)/shard_map/pallas_call | solution.py:386
  262.6 8.0 %collective-permute-done.28.refs_3_ = bf16[256,768]{1,0:T(8,128)(2,1)S(1)} collective-permute-done((bf16[256,768]{1,0:T(8,128)(2,1)}, bf16[256,768]{1,0:T(8,128)(2,1)S(1)}, u32[]{:S(2)}, u32[]{:S(2)}) %collective-permute-start.28) | collective-permute-done | bytes 393248 | tf_op jit(solution)/shard_map/ppermute | solution.py:22
  271.3 3.1 shard_map.358
  276.0 11.2 %collective-permute-done.26.refs_4_ = bf16[96,3072]{1,0:T(8,128)(2,1)S(1)} collective-permute-done((bf16[96,3072]{1,0:T(8,128)(2,1)}, bf16[96,3072]{1,0:T(8,128)(2,1)S(1)}, u32[]{:S(2)}, u32[]{:S(2)}) %collective-permute-start.26) | collective-permute-done | bytes 589856 | tf_op jit(solution)/shard_map/ppermute | solution.py:22
  288.0 2.9 shard_map.356
  294.7 3.3 %collective-permute-done.30.refs_4_ = bf16[192,768]{1,0:T(8,128)(2,1)S(1)} collective-permute-done((bf16[192,768]{1,0:T(8,128)(2,1)}, bf16[192,768]{1,0:T(8,128)(2,1)S(1)}, u32[]{:S(2)}, u32[]{:S(2)}) %collective-permute-start.30) | collective-permute-done | bytes 294944 | tf_op jit(solution)/shard_map/ppermute | solution.py:22
  300.4 2.9 shard_map.359
  307.6 3.3 collective-permute-start.35
  312.6 3.2 collective-permute-done.33.refs_2_
  316.5 1.9 shard_map.360
  318.4 2.1 collective-permute-start.34
  321.2 4.5 %collective-permute-done.34 = bf16[104,768]{1,0:T(8,128)(2,1)S(1)} collective-permute-done((bf16[104,768]{1,0:T(8,128)(2,1)}, bf16[104,768]{1,0:T(8,128)(2,1)S(1)}, u32[]{:S(2)}, u32[]{:S(2)}) %collective-permute-start.34) | collective-permute-done | bytes 159776 | tf_op jit(solution)/shard_map/ppermute | solution.py:22
  (243 shorter events, 85.5 us)
Async XLA Ops:
  2.7 7.2 %collective-permute-start.3 = (f32[2,2]{1,0:T(2,128)}, f32[2,2]{1,0:T(2,128)}, u32[]{:S(2)}, u32[]{:S(2)}) collective-permute-start(f32[2,2]{1,0:T(2,128)} %pad_maximum_fusion.8), channel_id=1, source_target_pairs={{0,4},{4,0},{8,12},{12,8},{16,20},{20,16},{24,28},{28,24},{1,5},{5... | collective-permute-start | bytes 56 | tf_op jit(solution)/shard_map/ppermute | solution.py:22
  4.3 47.4 %collective-permute-start.6 = (bf16[1,8,32,768]{3,2,1,0:T(8,128)(2,1)S(1)}, bf16[1,8,32,768]{3,2,1,0:T(8,128)(2,1)S(1)}, u32[]{:S(2)}, u32[]{:S(2)}) collective-permute-start(bf16[1,8,32,768]{3,2,1,0:T(8,128)(2,1)S(1)} %get-tuple-element.152), channel_id=1, source_target_pairs={{0,1},{1,0},{2,5},{3,4},{4,3},{5,2},{6,7},{7,6},{8,9},{9,8},{10,13... | collective-permute-start | bytes 1179656 | tf_op jit(solution)/shard_map/ppermute | solution.py:31
  7.0 44.8 %collective-permute-start.7 = (bf16[1,8,32,768]{3,2,1,0:T(8,128)(2,1)S(1)}, bf16[1,8,32,768]{3,2,1,0:T(8,128)(2,1)S(1)}, u32[]{:S(2)}, u32[]{:S(2)}) collective-permute-start(bf16[1,8,32,768]{3,2,1,0:T(8,128)(2,1)S(1)} %get-tuple-element.153), channel_id=1, source_target_pairs={{0,0},{1,1},{2,4},{3,5},{4,2},{5,3},{6,6},{7,7},{8,8},{9,9},{10,12... | collective-permute-start | bytes 1179656 | tf_op jit(solution)/shard_map/ppermute | solution.py:31
  7.7 16.5 %collective-permute-start = (bf16[1,8,32,768]{3,2,1,0:T(8,128)(2,1)S(1)}, bf16[1,8,32,768]{3,2,1,0:T(8,128)(2,1)S(1)}, u32[]{:S(2)}, u32[]{:S(2)}) collective-permute-start(bf16[1,8,32,768]{3,2,1,0:T(8,128)(2,1)S(1)} %get-tuple-element.156), channel_id=1, source_target_pairs={{0,1},{1,0},{2,5},{3,4},{4,3},{5,2},{6,7},{7,6},{8,9},{9,8},{10,13... | collective-permute-start | bytes 1179656 | tf_op jit(solution)/shard_map/ppermute | solution.py:31
  7.8 16.4 %collective-permute-start.1 = (bf16[1,8,32,768]{3,2,1,0:T(8,128)(2,1)S(1)}, bf16[1,8,32,768]{3,2,1,0:T(8,128)(2,1)S(1)}, u32[]{:S(2)}, u32[]{:S(2)}) collective-permute-start(bf16[1,8,32,768]{3,2,1,0:T(8,128)(2,1)S(1)} %get-tuple-element.157), channel_id=1, source_target_pairs={{0,0},{1,1},{2,4},{3,5},{4,2},{5,3},{6,6},{7,7},{8,8},{9,9},{10,12... | collective-permute-start | bytes 1179656 | tf_op jit(solution)/shard_map/ppermute | solution.py:31
  24.3 20.4 %collective-permute-start.2 = (bf16[1,2,32,768]{3,2,1,0:T(8,128)(2,1)S(1)}, bf16[1,2,32,768]{3,2,1,0:T(8,128)(2,1)S(1)}, u32[]{:S(2)}, u32[]{:S(2)}) collective-permute-start(bf16[1,2,32,768]{3,2,1,0:T(8,128)(2,1)S(1)} %slice_select_fusion), channel_id=1, source_target_pairs={{0,4},{4,0},{8,12},{12,8},{16,20},{20,16},{24,28},{28,24},{1,5},{5... | collective-permute-start | bytes 294920 | tf_op jit(solution)/shard_map/ppermute | solution.py:22
  51.9 15.2 %collective-permute-start.8 = (bf16[1,1,32,768]{3,2,1,0:T(8,128)(2,1)S(1)}, bf16[1,1,32,768]{3,2,1,0:T(8,128)(2,1)S(1)}, u32[]{:S(2)}, u32[]{:S(2)}) collective-permute-start(bf16[1,1,32,768]{3,2,1,0:T(8,128)(2,1)S(1)} %slice_select_fusion.1), channel_id=1, source_target_pairs={{0,4},{4,0},{8,12},{12,8},{16,20},{20,16},{24,28},{28,24},{1,5},{5... | collective-permute-start | bytes 147464 | tf_op jit(solution)/shard_map/ppermute | solution.py:22
  157.4 5.2 %collective-permute-start.12 = (bf16[2,9,16,768]{3,2,1,0:T(8,128)(2,1)}, bf16[2,9,16,768]{3,2,1,0:T(8,128)(2,1)S(1)}, u32[]{:S(2)}, u32[]{:S(2)}) collective-permute-start(bf16[2,9,16,768]{3,2,1,0:T(8,128)(2,1)} %get-tuple-element.91), channel_id=1, source_target_pairs={{0,4},{4,0},{8,12},{12,8},{16,20},{20,16},{24,28},{28,24},{1,5},{5... | collective-permute-start | bytes 1327112 | tf_op jit(solution)/shard_map/ppermute | solution.py:22
  161.2 43.4 %collective-permute-start.20 = (bf16[1536,768]{1,0:T(8,128)(2,1)}, bf16[1536,768]{1,0:T(8,128)(2,1)S(1)}, u32[]{:S(2)}, u32[]{:S(2)}) collective-permute-start(bf16[1536,768]{1,0:T(8,128)(2,1)} %bitcast.110), channel_id=1, source_target_pairs={{0,4},{4,0},{8,12},{12,8},{16,20},{20,16},{24,28},{28,24},{1,5},{5... | collective-permute-start | bytes 7077896 | tf_op jit(solution)/shard_map/ppermute | solution.py:22
  161.4 45.3 %collective-permute-start.21 = (bf16[384,3072]{1,0:T(8,128)(2,1)}, bf16[384,3072]{1,0:T(8,128)(2,1)}, u32[]{:S(2)}, u32[]{:S(2)}) collective-permute-start(bf16[384,3072]{1,0:T(8,128)(2,1)} %bitcast.109), channel_id=1, source_target_pairs={{0,4},{4,0},{8,12},{12,8},{16,20},{20,16},{24,28},{28,24},{1,5},{5... | collective-permute-start | bytes 7077896 | tf_op jit(solution)/shard_map/ppermute | solution.py:22
  178.5 35.9 %collective-permute-start.10 = (bf16[1,8,32,768]{3,2,1,0:T(8,128)(2,1)}, bf16[1,8,32,768]{3,2,1,0:T(8,128)(2,1)S(1)}, u32[]{:S(2)}, u32[]{:S(2)}) collective-permute-start(bf16[1,8,32,768]{3,2,1,0:T(8,128)(2,1)} %get-tuple-element.149), channel_id=1, source_target_pairs={{0,0},{1,1},{4,2},{5,3},{2,4},{3,5},{6,6},{7,7},{8,8},{9,9},{12,10... | collective-permute-start | bytes 1179656 | tf_op jit(solution)/shard_map/ppermute | solution.py:54
  181.9 15.6 %collective-permute-start.17 = (f32[32,768]{1,0:T(8,128)S(1)}, f32[32,768]{1,0:T(8,128)S(1)}, u32[]{:S(2)}, u32[]{:S(2)}) collective-permute-start(f32[32,768]{1,0:T(8,128)S(1)} %pad_maximum_fusion.5), channel_id=1, source_target_pairs={{0,2},{1,3},{2,0},{3,1},{4,6},{5,7},{6,4},{7,5},{8,10},{9,11},{10,... | collective-permute-start | bytes 294920 | tf_op jit(solution)/shard_map/ppermute | solution.py:22
  184.9 43.8 %collective-permute-start.27 = (bf16[1152,768]{1,0:T(8,128)(2,1)}, bf16[1152,768]{1,0:T(8,128)(2,1)S(1)}, u32[]{:S(2)}, u32[]{:S(2)}) collective-permute-start(bf16[1152,768]{1,0:T(8,128)(2,1)} %bitcast.32), channel_id=1, source_target_pairs={{0,4},{4,0},{8,12},{12,8},{16,20},{20,16},{24,28},{28,24},{1,5},{5... | collective-permute-start | bytes 5308424 | tf_op jit(solution)/shard_map/ppermute | solution.py:22
  197.5 5.2 %collective-permute-start.18 = (f32[48,768]{1,0:T(8,128)S(1)}, f32[48,768]{1,0:T(8,128)S(1)}, u32[]{:S(2)}, u32[]{:S(2)}) collective-permute-start(f32[48,768]{1,0:T(8,128)S(1)} %pad_maximum_fusion.4), channel_id=1, source_target_pairs={{0,8},{4,12},{8,0},{12,4},{16,24},{20,28},{24,16},{28,20},{1,9},{5... | collective-permute-start | bytes 442376 | tf_op jit(solution)/shard_map/ppermute | solution.py:22
  202.7 13.3 %collective-permute-start.9 = (bf16[1,8,32,768]{3,2,1,0:T(8,128)(2,1)}, bf16[1,8,32,768]{3,2,1,0:T(8,128)(2,1)S(1)}, u32[]{:S(2)}, u32[]{:S(2)}) collective-permute-start(bf16[1,8,32,768]{3,2,1,0:T(8,128)(2,1)} %get-tuple-element.148), channel_id=1, source_target_pairs={{1,0},{0,1},{5,2},{4,3},{3,4},{2,5},{7,6},{6,7},{9,8},{8,9},{13,10... | collective-permute-start | bytes 1179656 | tf_op jit(solution)/shard_map/ppermute | solution.py:54
  204.6 21.4 %collective-permute-start.13 = (bf16[1,8,32,768]{3,2,1,0:T(8,128)(2,1)S(1)}, bf16[1,8,32,768]{3,2,1,0:T(8,128)(2,1)S(1)}, u32[]{:S(2)}, u32[]{:S(2)}) collective-permute-start(bf16[1,8,32,768]{3,2,1,0:T(8,128)(2,1)S(1)} %get-tuple-element.144), channel_id=1, source_target_pairs={{1,0},{0,1},{5,2},{4,3},{3,4},{2,5},{7,6},{6,7},{9,8},{8,9},{13,10... | collective-permute-start | bytes 1179656 | tf_op jit(solution)/shard_map/ppermute | solution.py:54
  206.6 19.4 %collective-permute-start.14 = (bf16[1,8,32,768]{3,2,1,0:T(8,128)(2,1)S(1)}, bf16[1,8,32,768]{3,2,1,0:T(8,128)(2,1)S(1)}, u32[]{:S(2)}, u32[]{:S(2)}) collective-permute-start(bf16[1,8,32,768]{3,2,1,0:T(8,128)(2,1)S(1)} %get-tuple-element.145), channel_id=1, source_target_pairs={{0,0},{1,1},{4,2},{5,3},{2,4},{3,5},{6,6},{7,7},{8,8},{9,9},{12,10... | collective-permute-start | bytes 1179656 | tf_op jit(solution)/shard_map/ppermute | solution.py:54
  214.4 29.1 %collective-permute-start.22 = (bf16[768,768]{1,0:T(8,128)(2,1)}, bf16[768,768]{1,0:T(8,128)(2,1)S(1)}, u32[]{:S(2)}, u32[]{:S(2)}) collective-permute-start(bf16[768,768]{1,0:T(8,128)(2,1)} %get-tuple-element.107), channel_id=1, source_target_pairs={{0,8},{4,12},{8,0},{12,4},{16,24},{20,28},{24,16},{28,20},{1,9},{5... | collective-permute-start | bytes 3538952 | tf_op jit(solution)/shard_map/ppermute | solution.py:22
  216.0 35.1 %collective-permute-start.23 = (bf16[192,3072]{1,0:T(8,128)(2,1)}, bf16[192,3072]{1,0:T(8,128)(2,1)S(1)}, u32[]{:S(2)}, u32[]{:S(2)}) collective-permute-start(bf16[192,3072]{1,0:T(8,128)(2,1)} %get-tuple-element.108), channel_id=1, source_target_pairs={{0,1},{1,0},{2,3},{3,2},{4,5},{5,4},{6,7},{7,6},{8,9},{9,8},{10,11... | collective-permute-start | bytes 3538952 | tf_op jit(solution)/shard_map/ppermute | solution.py:22
  226.0 13.0 %collective-permute-start.24 = (bf16[512,768]{1,0:T(8,128)(2,1)}, bf16[512,768]{1,0:T(8,128)(2,1)S(1)}, u32[]{:S(2)}, u32[]{:S(2)}) collective-permute-start(bf16[512,768]{1,0:T(8,128)(2,1)} %bitcast.30), channel_id=1, source_target_pairs={{0,4},{4,0},{8,12},{12,8},{16,20},{20,16},{24,28},{28,24},{1,5},{5... | collective-permute-start | bytes 2359304 | tf_op jit(solution)/shard_map/ppermute | solution.py:22
  226.0 12.0 %collective-permute-start.19 = (f32[80,768]{1,0:T(8,128)}, f32[80,768]{1,0:T(8,128)S(1)}, u32[]{:S(2)}, u32[]{:S(2)}) collective-permute-start(f32[80,768]{1,0:T(8,128)} %get-tuple-element.158), channel_id=1, source_target_pairs={{0,16},{4,20},{8,24},{12,28},{16,0},{20,4},{24,8},{28,12},{1,17},{... | collective-permute-start | bytes 737288 | tf_op jit(solution)/shard_map/ppermute | solution.py:22
  233.6 29.0 %collective-permute-start.29 = (bf16[576,768]{1,0:T(8,128)(2,1)}, bf16[576,768]{1,0:T(8,128)(2,1)}, u32[]{:S(2)}, u32[]{:S(2)}) collective-permute-start(bf16[576,768]{1,0:T(8,128)(2,1)} %get-tuple-element.120), channel_id=1, source_target_pairs={{0,8},{4,12},{8,0},{12,4},{16,24},{20,28},{24,16},{28,20},{1,9},{5... | collective-permute-start | bytes 2654216 | tf_op jit(solution)/shard_map/ppermute | solution.py:22
  257.6 13.0 %collective-permute-start.28 = (bf16[256,768]{1,0:T(8,128)(2,1)}, bf16[256,768]{1,0:T(8,128)(2,1)S(1)}, u32[]{:S(2)}, u32[]{:S(2)}) collective-permute-start(bf16[256,768]{1,0:T(8,128)(2,1)} %get-tuple-element.119), channel_id=1, source_target_pairs={{0,8},{4,12},{8,0},{12,4},{16,24},{20,28},{24,16},{28,20},{1,9},{5... | collective-permute-start | bytes 1179656 | tf_op jit(solution)/shard_map/ppermute | solution.py:22
  259.1 16.9 %collective-permute-start.25 = (bf16[384,768]{1,0:T(8,128)(2,1)}, bf16[384,768]{1,0:T(8,128)(2,1)S(1)}, u32[]{:S(2)}, u32[]{:S(2)}) collective-permute-start(bf16[384,768]{1,0:T(8,128)(2,1)} %get-tuple-element.111), channel_id=1, source_target_pairs={{0,16},{4,20},{8,24},{12,28},{16,0},{20,4},{24,8},{28,12},{1,17},{... | collective-permute-start | bytes 1769480 | tf_op jit(solution)/shard_map/ppermute | solution.py:22
  260.6 26.5 %collective-permute-start.26 = (bf16[96,3072]{1,0:T(8,128)(2,1)}, bf16[96,3072]{1,0:T(8,128)(2,1)S(1)}, u32[]{:S(2)}, u32[]{:S(2)}) collective-permute-start(bf16[96,3072]{1,0:T(8,128)(2,1)} %get-tuple-element.112), channel_id=1, source_target_pairs={{0,2},{1,3},{2,0},{3,1},{4,6},{5,7},{6,4},{7,5},{8,10},{9,11},{10,... | collective-permute-start | bytes 1769480 | tf_op jit(solution)/shard_map/ppermute | solution.py:22
  274.4 25.0 %collective-permute-start.32 = (bf16[416,768]{1,0:T(8,128)(2,1)}, bf16[416,768]{1,0:T(8,128)(2,1)S(1)}, u32[]{:S(2)}, u32[]{:S(2)}) collective-permute-start(bf16[416,768]{1,0:T(8,128)(2,1)} %get-tuple-element.124), channel_id=1, source_target_pairs={{0,16},{4,20},{8,24},{12,28},{16,0},{20,4},{24,8},{28,12},{1,17},{... | collective-permute-start | bytes 1916936 | tf_op jit(solution)/shard_map/ppermute | solution.py:22
  290.8 7.2 %collective-permute-start.30 = (bf16[192,768]{1,0:T(8,128)(2,1)}, bf16[192,768]{1,0:T(8,128)(2,1)S(1)}, u32[]{:S(2)}, u32[]{:S(2)}) collective-permute-start(bf16[192,768]{1,0:T(8,128)(2,1)} %get-tuple-element.122), channel_id=1, source_target_pairs={{0,1},{1,0},{2,3},{3,2},{4,5},{5,4},{6,7},{7,6},{8,9},{9,8},{10,11... | collective-permute-start | bytes 884744 | tf_op jit(solution)/shard_map/ppermute | solution.py:22
  290.8 8.6 %collective-permute-start.31 = (bf16[192,768]{1,0:T(8,128)(2,1)}, bf16[192,768]{1,0:T(8,128)(2,1)S(1)}, u32[]{:S(2)}, u32[]{:S(2)}) collective-permute-start(bf16[192,768]{1,0:T(8,128)(2,1)} %get-tuple-element.123), channel_id=1, source_target_pairs={{0,8},{4,12},{8,0},{12,4},{16,24},{20,28},{24,16},{28,20},{1,9},{5... | collective-permute-start | bytes 884744 | tf_op jit(solution)/shard_map/ppermute | solution.py:22
  303.3 7.5 %collective-permute-start.36 = (bf16[96,768]{1,0:T(8,128)(2,1)}, bf16[96,768]{1,0:T(8,128)(2,1)S(1)}, u32[]{:S(2)}, u32[]{:S(2)}) collective-permute-start(bf16[96,768]{1,0:T(8,128)(2,1)} %get-tuple-element.132), channel_id=1, source_target_pairs={{0,16},{4,20},{8,24},{12,28},{16,0},{20,4},{24,8},{28,12},{1,17},{... | collective-permute-start | bytes 442376 | tf_op jit(solution)/shard_map/ppermute | solution.py:22
  304.6 11.1 %collective-permute-start.33 = (bf16[208,768]{1,0:T(8,128)(2,1)}, bf16[208,768]{1,0:T(8,128)(2,1)S(1)}, u32[]{:S(2)}, u32[]{:S(2)}) collective-permute-start(bf16[208,768]{1,0:T(8,128)(2,1)} %get-tuple-element.126), channel_id=1, source_target_pairs={{0,1},{1,0},{2,3},{3,2},{4,5},{5,4},{6,7},{7,6},{8,9},{9,8},{10,11... | collective-permute-start | bytes 958472 | tf_op jit(solution)/shard_map/ppermute | solution.py:22
  307.6 12.9 %collective-permute-start.35 = (bf16[96,768]{1,0:T(8,128)(2,1)}, bf16[96,768]{1,0:T(8,128)(2,1)S(1)}, u32[]{:S(2)}, u32[]{:S(2)}) collective-permute-start(bf16[96,768]{1,0:T(8,128)(2,1)} %get-tuple-element.130), channel_id=1, source_target_pairs={{0,2},{1,3},{2,0},{3,1},{4,6},{5,7},{6,4},{7,5},{8,10},{9,11},{10,... | collective-permute-start | bytes 442376 | tf_op jit(solution)/shard_map/ppermute | solution.py:22
  318.4 7.4 %collective-permute-start.34 = (bf16[104,768]{1,0:T(8,128)(2,1)}, bf16[104,768]{1,0:T(8,128)(2,1)S(1)}, u32[]{:S(2)}, u32[]{:S(2)}) collective-permute-start(bf16[104,768]{1,0:T(8,128)(2,1)} %get-tuple-element.128), channel_id=1, source_target_pairs={{0,2},{1,3},{2,0},{3,1},{4,6},{5,7},{6,4},{7,5},{8,10},{9,11},{10,... | collective-permute-start | bytes 479240 | tf_op jit(solution)/shard_map/ppermute | solution.py:22
  (45 other events, 311.5 us)

commit v3 on v2

--- a/solution.py
+++ b/solution.py
@@ -208,7 +208,7 @@
                 hidden_grad[l, r, :, here] = rounded
                 return bias_sum + fold_rows(rounded.astype(F32))
 
-            bias_sum = lax.fori_loop(0, rows, backward_row, bias_sum, unroll=2)
+            bias_sum = lax.fori_loop(0, rows, backward_row, bias_sum, unroll=4)
         for k in range(10):
             small_out[k : k + 1, here] = jnp.sum(sums[k], axis=0, keepdims=True)
         small_out[10:11, here] = jnp.sum(bias_sum, axis=0, keepdims=True)
@@ -374,7 +374,7 @@
                 mixed[l, r, here.start // lanes] = total
                 return carry
 
-            lax.fori_loop(0, rows, conv_row, 0, unroll=2)
+            lax.fori_loop(0, rows, conv_row, 0, unroll=4)
     pack_strips(mixed, (out0, out1), place[0])
 
 
@@ -715,7 +715,7 @@
                 latents_grad[l, r, here] = pulled.astype(BF16)
             return carry
 
-        lax.fori_loop(0, rows, pull_row, 0, unroll=2)
+        lax.fori_loop(0, rows, pull_row, 0, unroll=4)
 
 
 def finish(place, parts, latents_rim, modulation, taps, middle_grad):

time: 331 us -> 329 us (level)
  transfers between devices with their start and end apart: 37 -> 37, of which waited for: 19 -> 19; matrix products, arithmetic and copies ran while one was open for 13% -> 13% of each run, Pallas kernels for 16% -> 15%
where the time goes in v3:
time: 329 us; the launch traced here: 328 us
  Pallas kernels  135 us (41%)
  waiting for transfers between devices  77.2 us (23%)
  starting transfers between devices  52.1 us (16%)
  local copies, waits for them, and re-layouts  28.1 us (9%)
  other arithmetic  24.7 us (8%)
  matrix products  9.12 us (3%)
    pallas_call x13, Pallas kernels, call_whole(): pl.pallas_call(body, in_specs=[SCALARS] + [WHOLE] * (len(inputs) - 1), ou...  89.6 us
    ppermute x29, waiting for transfers between devices, swap_bit(): return lax.ppermute(value, axis, [(i, i ^ 1 << bit) for i in range(count)])  64.3 us
    pallas_call x1, Pallas kernels, feed_forward(): pl.pallas_call(feed_forward_body, grid=(steps,), in_specs=[pl.BlockSpec(m...  45.2 us
    ppermute x29, starting transfers between devices, swap_bit(): return lax.ppermute(value, axis, [(i, i ^ 1 << bit) for i in range(count)])  43.6 us
    unnamed x84, local copies, waits for them, and re-layouts  14.8 us
    ppermute x4, waiting for transfers between devices, from_pairs(): arrived.append(lax.ppermute(piece, (BATCH, GRP), pair_moves(k, True)))  7.91 us
  transfers between devices with their start and end apart: 37, of which 19 were waited for; matrix products, arithmetic and copies ran while one was open for 13% of the time, Pallas kernels for 15%

profile of v3, /device:TPU:0, one launch (start us, length us, event | category | flops | bytes accessed | tf_op | source)
XLA Modules:
  0.0 328.0 jit_solution(3220331070509968350)
XLA Ops:
  4.3 2.6 collective-permute-start.6
  15.2 4.0 %fusion.16 = f32[3,4608]{1,0:T(4,128)S(1)} fusion(bf16[768,4608]{1,0:T(8,128)(2,1)} %param.28, bf16[1,768]{1,0:T(2,128)(2,1)S(1)} %get-tuple-element.177, bf16[1,768]{1,0:T(2,128)(2,1)S(1)} %get-tuple-element.176, bf16[1,768]{1,0:T(2,128)(2,1)S(1)} %get-tuple-element.137), kind=kOutput, calls=%fused_computation.72 | convolution fusion | flops 21247488 | bytes 7137792 | tf_op jit(solution)/shard_map/dot_general | solution.py:121
  19.3 5.0 %collective-permute-done = bf16[1,8,32,768]{3,2,1,0:T(8,128)(2,1)S(1)} collective-permute-done((bf16[1,8,32,768]{3,2,1,0:T(8,128)(2,1)S(1)}, bf16[1,8,32,768]{3,2,1,0:T(8,128)(2,1)S(1)}, u32[]{:S(2)}, u32[]{:S(2)}) %collective-permute-start) | collective-permute-done | bytes 393248 | tf_op jit(solution)/shard_map/ppermute | solution.py:31
  24.3 19.4 %collective-permute-start.2 = (bf16[1,2,32,768]{3,2,1,0:T(8,128)(2,1)S(1)}, bf16[1,2,32,768]{3,2,1,0:T(8,128)(2,1)S(1)}, u32[]{:S(2)}, u32[]{:S(2)}) collective-permute-start(bf16[1,2,32,768]{3,2,1,0:T(8,128)(2,1)S(1)} %slice_select_fusion), channel_id=1, source_target_pairs={{0,4},{4,0},{8,12},{12,8},{16,20},{20,16},{24,28},{28,24},{1,5},{5... | collective-permute-start | bytes 294920 | tf_op jit(solution)/shard_map/ppermute | solution.py:22
  45.8 5.5 %shard_map.348 = (bf16[2,8,16,768]{3,2,1,0:T(8,128)(2,1)}, bf16[2,8,16,768]{3,2,1,0:T(8,128)(2,1)}) custom-call(s32[3]{0:T(128)} %pad_add_fusion.place, bf16[1,20,32,768]{3,2,1,0:T(8,128)(2,1)} %pad_maximum_fusion.latents, f32[1,4608]{1,0:T(1,128)} %copy-done.22, bf16[9,768]{1,0:T(8,128)(2,1)} %taps.5, bf16[1,768]{1,0:T(2,128)(2,1)} %conv_bias.2), custom_call_target="tpu_custom_call" | custom-call | tf_op jit(solution)/shard_map/pallas_call | solution.py:386
  54.0 11.6 %shard_map.349 = (bf16[2,10,16,768]{3,2,1,0:T(8,128)(2,1)}, bf16[2,10,16,768]{3,2,1,0:T(8,128)(2,1)}, bf16[2,256,2304]{2,1,0:T(8,128)(2,1)}, f32[2,256,128]{2,1,0:T(8,128)}) custom-call(s32[3]{0:T(128)} %pad_add_fusion.place, bf16[2,8,16,768]{3,2,1,0:T(8,128)(2,1)} %get-tuple-element.76.part0, bf16[2,8,16,768]{3,2,1,0:T(8,128)(2,1)} %copy-done.11, ...), custom_call_target="tpu_custom_call" | custom-call | tf_op jit(solution)/shard_map/pallas_call | solution.py:386
  68.5 6.8 %shard_map.350 = (bf16[1,20,32,768]{3,2,1,0:T(8,128)(2,1)}, bf16[1,16,32,768]{3,2,1,0:T(8,128)(2,1)}, f32[1,16,32,768]{3,2,1,0:T(8,128)}) custom-call(s32[3]{0:T(128)} %pad_add_fusion.place, bf16[2,10,16,768]{3,2,1,0:T(8,128)(2,1)} %get-tuple-element.78.part0, bf16[2,10,16,768]{3,2,1,0:T(8,128)(2,1)} %copy-done.23, ...), custom_call_target="tpu_custom_call" | custom-call | tf_op jit(solution)/shard_map/pallas_call | solution.py:386
  76.5 45.2 %feed_forward.1 = (f32[512,768]{1,0:T(8,128)S(1)}, f32[512,768]{1,0:T(8,128)S(1)}, bf16[4,1,384,768]{3,2,1,0:T(8,128)(2,1)}, bf16[4,1,384,768]{3,2,1,0:T(8,128)(...) custom-call(s32[3]{0:T(128)S(1)} %copy-done.6, ...), custom_call_target="tpu_custom_call" | custom-call | tf_op jit(solution)/shard_map/feed_forward/pallas_call | solution.py:255
  124.0 10.2 %shard_map.351 = (bf16[1,16,32,768]{3,2,1,0:T(8,128)(2,1)}, f32[1,16,32,768]{3,2,1,0:T(8,128)}, bf16[768,768]{1,0:T(8,128)(2,1)}, f32[1,4,8,768]{3,2,1,0:T(8,128...) custom-call(s32[3]{0:T(128)} %pad_add_fusion.place, ...), custom_call_target="tpu_custom_call" | custom-call | tf_op jit(solution)/shard_map/pallas_call | solution.py:386
  136.9 19.6 %shard_map.352 = (bf16[4,288,768]{2,1,0:T(8,128)(2,1)}, bf16[4,288,768]{2,1,0:T(8,128)(2,1)}, f32[2,8,768]{2,1,0:T(8,128)}, bf16[2,9,16,768]{3,2,1,0:T(8,128)(2,1)}, bf16[2,9,16,768]{3,2,1,0:T(8,128)(2,1)}) custom-call(s32[3]{0:T(128)} %pad_add_fusion.place, bf16[2,8,16,768]{3,2,1,0:T(8,128)(2,1)} %get-tuple-element.86.up0, ...), custom_call_target="tpu_custom_call" | custom-call | tf_op jit(solution)/shard_map/pallas_call | solution.py:386
  162.4 9.0 %shard_map.353 = (bf16[1,16,32,768]{3,2,1,0:T(8,128)(2,1)}, f32[1,2,8,768]{3,2,1,0:T(8,128)}, f32[16,768]{1,0:T(8,128)}) custom-call(s32[3]{0:T(128)} %pad_add_fusion.place, bf16[2,9,16,768]{3,2,1,0:T(8,128)(2,1)} %get-tuple-element.90.part0, bf16[2,9,16,768]{3,2,1,0:T(8,128)(2,1)} %copy-done.24, bf16[1,20,32,768]{3,2,1,0:T(8,128)(2,1)} %pad_maximum_fusion.latents, ...), custom_call_target="tpu_custom_call" | custom-call | tf_op jit(solution)/shard_map/pallas_call | solution.py:386
  183.2 12.4 %collective-permute-done.17 = f32[32,768]{1,0:T(8,128)S(1)} collective-permute-done((f32[32,768]{1,0:T(8,128)S(1)}, f32[32,768]{1,0:T(8,128)S(1)}, u32[]{:S(2)}, u32[]{:S(2)}) %collective-permute-start.17) | collective-permute-done | bytes 98336 | tf_op jit(solution)/shard_map/ppermute | solution.py:22
  198.5 2.3 collective-permute-done.18
  202.7 2.0 collective-permute-start.13
  205.4 7.1 %shard_map.354 = (bf16[768,768]{1,0:T(8,128)(2,1)}, bf16[192,3072]{1,0:T(8,128)(2,1)}, bf16[768,768]{1,0:T(8,128)(2,1)}, bf16[192,3072]{1,0:T(8,128)(2,1)}) custom-call(s32[2]{0:T(128)} %pad_add_fusion.4.refs_0_, bf16[1536,768]{1,0:T(8,128)(2,1)} %bitcast.88, bf16[384,3072]{1,0:T(8,128)(2,1)} %bitcast.89, bf16[1536,768]{1,0:T(8,128)(2,1)} %copy-done.9, ...), custom_call_target="tpu_custom_call" | custom-call | tf_op jit(solution)/shard_map/pallas_call | solution.py:386
  216.2 7.9 %collective-permute-done.13 = bf16[1,8,32,768]{3,2,1,0:T(8,128)(2,1)S(1)} collective-permute-done((bf16[1,8,32,768]{3,2,1,0:T(8,128)(2,1)S(1)}, bf16[1,8,32,768]{3,2,1,0:T(8,128)(2,1)S(1)}, u32[]{:S(2)}, u32[]{:S(2)}) %collective-permute-start.13) | collective-permute-done | bytes 393248 | tf_op jit(solution)/shard_map/ppermute | solution.py:54
  228.0 3.7 %shard_map.357 = (bf16[576,768]{1,0:T(8,128)(2,1)}, bf16[576,768]{1,0:T(8,128)(2,1)}) custom-call(s32[1]{0:T(128)} %bitcast.19.refs_0_, bf16[1152,768]{1,0:T(8,128)(2,1)} %bitcast.90, bf16[1152,768]{1,0:T(8,128)(2,1)} %copy-done.10), custom_call_target="tpu_custom_call" | custom-call | tf_op jit(solution)/shard_map/pallas_call | solution.py:386
  231.7 2.4 collective-permute-start.29
  237.1 4.6 %collective-permute-done.22.refs_4_ = bf16[768,768]{1,0:T(8,128)(2,1)S(1)} collective-permute-done((bf16[768,768]{1,0:T(8,128)(2,1)}, bf16[768,768]{1,0:T(8,128)(2,1)S(1)}, u32[]{:S(2)}, u32[]{:S(2)}) %collective-permute-start.22) | collective-permute-done | bytes 1179680 | tf_op jit(solution)/shard_map/ppermute | solution.py:22
  241.6 7.5 %collective-permute-done.23.refs_5_ = bf16[192,3072]{1,0:T(8,128)(2,1)S(1)} collective-permute-done((bf16[192,3072]{1,0:T(8,128)(2,1)}, bf16[192,3072]{1,0:T(8,128)(2,1)S(1)}, u32[]{:S(2)}, u32[]{:S(2)}) %collective-permute-start.23) | collective-permute-done | bytes 1179680 | tf_op jit(solution)/shard_map/ppermute | solution.py:22
  250.2 5.4 %shard_map.355 = (bf16[384,768]{1,0:T(8,128)(2,1)}, bf16[96,3072]{1,0:T(8,128)(2,1)}, bf16[256,768]{1,0:T(8,128)(2,1)}, bf16[384,768]{1,0:T(8,128)(2,1)}, bf16[9...) custom-call(s32[3]{0:T(128)} %pad_add_fusion.3.refs_0_, bf16[768,768]{1,0:T(8,128)(2,1)} %get-tuple-element.102.refs_1_, ...), custom_call_target="tpu_custom_call" | custom-call | tf_op jit(solution)/shard_map/pallas_call | solution.py:386
  260.7 8.0 %collective-permute-done.28.refs_3_ = bf16[256,768]{1,0:T(8,128)(2,1)S(1)} collective-permute-done((bf16[256,768]{1,0:T(8,128)(2,1)}, bf16[256,768]{1,0:T(8,128)(2,1)S(1)}, u32[]{:S(2)}, u32[]{:S(2)}) %collective-permute-start.28) | collective-permute-done | bytes 393248 | tf_op jit(solution)/shard_map/ppermute | solution.py:22
  269.4 3.1 shard_map.358
  274.0 11.2 %collective-permute-done.26.refs_4_ = bf16[96,3072]{1,0:T(8,128)(2,1)S(1)} collective-permute-done((bf16[96,3072]{1,0:T(8,128)(2,1)}, bf16[96,3072]{1,0:T(8,128)(2,1)S(1)}, u32[]{:S(2)}, u32[]{:S(2)}) %collective-permute-start.26) | collective-permute-done | bytes 589856 | tf_op jit(solution)/shard_map/ppermute | solution.py:22
  286.0 2.9 shard_map.356
  292.8 3.3 %collective-permute-done.30.refs_4_ = bf16[192,768]{1,0:T(8,128)(2,1)S(1)} collective-permute-done((bf16[192,768]{1,0:T(8,128)(2,1)}, bf16[192,768]{1,0:T(8,128)(2,1)S(1)}, u32[]{:S(2)}, u32[]{:S(2)}) %collective-permute-start.30) | collective-permute-done | bytes 294944 | tf_op jit(solution)/shard_map/ppermute | solution.py:22
  298.5 2.9 shard_map.359
  305.6 3.3 collective-permute-start.35
  310.6 3.2 collective-permute-done.33.refs_2_
  314.5 1.9 shard_map.360
  316.4 2.1 collective-permute-start.34
  319.3 4.5 %collective-permute-done.34 = bf16[104,768]{1,0:T(8,128)(2,1)S(1)} collective-permute-done((bf16[104,768]{1,0:T(8,128)(2,1)}, bf16[104,768]{1,0:T(8,128)(2,1)S(1)}, u32[]{:S(2)}, u32[]{:S(2)}) %collective-permute-start.34) | collective-permute-done | bytes 159776 | tf_op jit(solution)/shard_map/ppermute | solution.py:22
  (243 shorter events, 85.5 us)
Async XLA Ops:
  2.7 7.2 %collective-permute-start.3 = (f32[2,2]{1,0:T(2,128)}, f32[2,2]{1,0:T(2,128)}, u32[]{:S(2)}, u32[]{:S(2)}) collective-permute-start(f32[2,2]{1,0:T(2,128)} %pad_maximum_fusion.8), channel_id=1, source_target_pairs={{0,4},{4,0},{8,12},{12,8},{16,20},{20,16},{24,28},{28,24},{1,5},{5... | collective-permute-start | bytes 56 | tf_op jit(solution)/shard_map/ppermute | solution.py:22
  4.3 47.3 %collective-permute-start.6 = (bf16[1,8,32,768]{3,2,1,0:T(8,128)(2,1)S(1)}, bf16[1,8,32,768]{3,2,1,0:T(8,128)(2,1)S(1)}, u32[]{:S(2)}, u32[]{:S(2)}) collective-permute-start(bf16[1,8,32,768]{3,2,1,0:T(8,128)(2,1)S(1)} %get-tuple-element.152), channel_id=1, source_target_pairs={{0,1},{1,0},{2,5},{3,4},{4,3},{5,2},{6,7},{7,6},{8,9},{9,8},{10,13... | collective-permute-start | bytes 1179656 | tf_op jit(solution)/shard_map/ppermute | solution.py:31
  7.0 44.7 %collective-permute-start.7 = (bf16[1,8,32,768]{3,2,1,0:T(8,128)(2,1)S(1)}, bf16[1,8,32,768]{3,2,1,0:T(8,128)(2,1)S(1)}, u32[]{:S(2)}, u32[]{:S(2)}) collective-permute-start(bf16[1,8,32,768]{3,2,1,0:T(8,128)(2,1)S(1)} %get-tuple-element.153), channel_id=1, source_target_pairs={{0,0},{1,1},{2,4},{3,5},{4,2},{5,3},{6,6},{7,7},{8,8},{9,9},{10,12... | collective-permute-start | bytes 1179656 | tf_op jit(solution)/shard_map/ppermute | solution.py:31
  7.7 16.5 %collective-permute-start = (bf16[1,8,32,768]{3,2,1,0:T(8,128)(2,1)S(1)}, bf16[1,8,32,768]{3,2,1,0:T(8,128)(2,1)S(1)}, u32[]{:S(2)}, u32[]{:S(2)}) collective-permute-start(bf16[1,8,32,768]{3,2,1,0:T(8,128)(2,1)S(1)} %get-tuple-element.156), channel_id=1, source_target_pairs={{0,1},{1,0},{2,5},{3,4},{4,3},{5,2},{6,7},{7,6},{8,9},{9,8},{10,13... | collective-permute-start | bytes 1179656 | tf_op jit(solution)/shard_map/ppermute | solution.py:31
  7.8 16.4 %collective-permute-start.1 = (bf16[1,8,32,768]{3,2,1,0:T(8,128)(2,1)S(1)}, bf16[1,8,32,768]{3,2,1,0:T(8,128)(2,1)S(1)}, u32[]{:S(2)}, u32[]{:S(2)}) collective-permute-start(bf16[1,8,32,768]{3,2,1,0:T(8,128)(2,1)S(1)} %get-tuple-element.157), channel_id=1, source_target_pairs={{0,0},{1,1},{2,4},{3,5},{4,2},{5,3},{6,6},{7,7},{8,8},{9,9},{10,12... | collective-permute-start | bytes 1179656 | tf_op jit(solution)/shard_map/ppermute | solution.py:31
  24.3 20.4 %collective-permute-start.2 = (bf16[1,2,32,768]{3,2,1,0:T(8,128)(2,1)S(1)}, bf16[1,2,32,768]{3,2,1,0:T(8,128)(2,1)S(1)}, u32[]{:S(2)}, u32[]{:S(2)}) collective-permute-start(bf16[1,2,32,768]{3,2,1,0:T(8,128)(2,1)S(1)} %slice_select_fusion), channel_id=1, source_target_pairs={{0,4},{4,0},{8,12},{12,8},{16,20},{20,16},{24,28},{28,24},{1,5},{5... | collective-permute-start | bytes 294920 | tf_op jit(solution)/shard_map/ppermute | solution.py:22
  51.7 15.2 %collective-permute-start.8 = (bf16[1,1,32,768]{3,2,1,0:T(8,128)(2,1)S(1)}, bf16[1,1,32,768]{3,2,1,0:T(8,128)(2,1)S(1)}, u32[]{:S(2)}, u32[]{:S(2)}) collective-permute-start(bf16[1,1,32,768]{3,2,1,0:T(8,128)(2,1)S(1)} %slice_select_fusion.1), channel_id=1, source_target_pairs={{0,4},{4,0},{8,12},{12,8},{16,20},{20,16},{24,28},{28,24},{1,5},{5... | collective-permute-start | bytes 147464 | tf_op jit(solution)/shard_map/ppermute | solution.py:22
  156.5 5.2 %collective-permute-start.12 = (bf16[2,9,16,768]{3,2,1,0:T(8,128)(2,1)}, bf16[2,9,16,768]{3,2,1,0:T(8,128)(2,1)S(1)}, u32[]{:S(2)}, u32[]{:S(2)}) collective-permute-start(bf16[2,9,16,768]{3,2,1,0:T(8,128)(2,1)} %get-tuple-element.91), channel_id=1, source_target_pairs={{0,4},{4,0},{8,12},{12,8},{16,20},{20,16},{24,28},{28,24},{1,5},{5... | collective-permute-start | bytes 1327112 | tf_op jit(solution)/shard_map/ppermute | solution.py:22
  160.2 42.5 %collective-permute-start.20 = (bf16[1536,768]{1,0:T(8,128)(2,1)}, bf16[1536,768]{1,0:T(8,128)(2,1)S(1)}, u32[]{:S(2)}, u32[]{:S(2)}) collective-permute-start(bf16[1536,768]{1,0:T(8,128)(2,1)} %bitcast.110), channel_id=1, source_target_pairs={{0,4},{4,0},{8,12},{12,8},{16,20},{20,16},{24,28},{28,24},{1,5},{5... | collective-permute-start | bytes 7077896 | tf_op jit(solution)/shard_map/ppermute | solution.py:22
  160.4 44.3 %collective-permute-start.21 = (bf16[384,3072]{1,0:T(8,128)(2,1)}, bf16[384,3072]{1,0:T(8,128)(2,1)}, u32[]{:S(2)}, u32[]{:S(2)}) collective-permute-start(bf16[384,3072]{1,0:T(8,128)(2,1)} %bitcast.109), channel_id=1, source_target_pairs={{0,4},{4,0},{8,12},{12,8},{16,20},{20,16},{24,28},{28,24},{1,5},{5... | collective-permute-start | bytes 7077896 | tf_op jit(solution)/shard_map/ppermute | solution.py:22
  176.6 35.9 %collective-permute-start.10 = (bf16[1,8,32,768]{3,2,1,0:T(8,128)(2,1)}, bf16[1,8,32,768]{3,2,1,0:T(8,128)(2,1)S(1)}, u32[]{:S(2)}, u32[]{:S(2)}) collective-permute-start(bf16[1,8,32,768]{3,2,1,0:T(8,128)(2,1)} %get-tuple-element.149), channel_id=1, source_target_pairs={{0,0},{1,1},{4,2},{5,3},{2,4},{3,5},{6,6},{7,7},{8,8},{9,9},{12,10... | collective-permute-start | bytes 1179656 | tf_op jit(solution)/shard_map/ppermute | solution.py:54
  180.0 15.6 %collective-permute-start.17 = (f32[32,768]{1,0:T(8,128)S(1)}, f32[32,768]{1,0:T(8,128)S(1)}, u32[]{:S(2)}, u32[]{:S(2)}) collective-permute-start(f32[32,768]{1,0:T(8,128)S(1)} %pad_maximum_fusion.5), channel_id=1, source_target_pairs={{0,2},{1,3},{2,0},{3,1},{4,6},{5,7},{6,4},{7,5},{8,10},{9,11},{10,... | collective-permute-start | bytes 294920 | tf_op jit(solution)/shard_map/ppermute | solution.py:22
  183.0 43.8 %collective-permute-start.27 = (bf16[1152,768]{1,0:T(8,128)(2,1)}, bf16[1152,768]{1,0:T(8,128)(2,1)S(1)}, u32[]{:S(2)}, u32[]{:S(2)}) collective-permute-start(bf16[1152,768]{1,0:T(8,128)(2,1)} %bitcast.32), channel_id=1, source_target_pairs={{0,4},{4,0},{8,12},{12,8},{16,20},{20,16},{24,28},{28,24},{1,5},{5... | collective-permute-start | bytes 5308424 | tf_op jit(solution)/shard_map/ppermute | solution.py:22
  195.6 5.2 %collective-permute-start.18 = (f32[48,768]{1,0:T(8,128)S(1)}, f32[48,768]{1,0:T(8,128)S(1)}, u32[]{:S(2)}, u32[]{:S(2)}) collective-permute-start(f32[48,768]{1,0:T(8,128)S(1)} %pad_maximum_fusion.4), channel_id=1, source_target_pairs={{0,8},{4,12},{8,0},{12,4},{16,24},{20,28},{24,16},{28,20},{1,9},{5... | collective-permute-start | bytes 442376 | tf_op jit(solution)/shard_map/ppermute | solution.py:22
  200.8 13.3 %collective-permute-start.9 = (bf16[1,8,32,768]{3,2,1,0:T(8,128)(2,1)}, bf16[1,8,32,768]{3,2,1,0:T(8,128)(2,1)S(1)}, u32[]{:S(2)}, u32[]{:S(2)}) collective-permute-start(bf16[1,8,32,768]{3,2,1,0:T(8,128)(2,1)} %get-tuple-element.148), channel_id=1, source_target_pairs={{1,0},{0,1},{5,2},{4,3},{3,4},{2,5},{7,6},{6,7},{9,8},{8,9},{13,10... | collective-permute-start | bytes 1179656 | tf_op jit(solution)/shard_map/ppermute | solution.py:54
  202.7 21.4 %collective-permute-start.13 = (bf16[1,8,32,768]{3,2,1,0:T(8,128)(2,1)S(1)}, bf16[1,8,32,768]{3,2,1,0:T(8,128)(2,1)S(1)}, u32[]{:S(2)}, u32[]{:S(2)}) collective-permute-start(bf16[1,8,32,768]{3,2,1,0:T(8,128)(2,1)S(1)} %get-tuple-element.144), channel_id=1, source_target_pairs={{1,0},{0,1},{5,2},{4,3},{3,4},{2,5},{7,6},{6,7},{9,8},{8,9},{13,10... | collective-permute-start | bytes 1179656 | tf_op jit(solution)/shard_map/ppermute | solution.py:54
  204.7 19.4 %collective-permute-start.14 = (bf16[1,8,32,768]{3,2,1,0:T(8,128)(2,1)S(1)}, bf16[1,8,32,768]{3,2,1,0:T(8,128)(2,1)S(1)}, u32[]{:S(2)}, u32[]{:S(2)}) collective-permute-start(bf16[1,8,32,768]{3,2,1,0:T(8,128)(2,1)S(1)} %get-tuple-element.145), channel_id=1, source_target_pairs={{0,0},{1,1},{4,2},{5,3},{2,4},{3,5},{6,6},{7,7},{8,8},{9,9},{12,10... | collective-permute-start | bytes 1179656 | tf_op jit(solution)/shard_map/ppermute | solution.py:54
  212.5 29.1 %collective-permute-start.22 = (bf16[768,768]{1,0:T(8,128)(2,1)}, bf16[768,768]{1,0:T(8,128)(2,1)S(1)}, u32[]{:S(2)}, u32[]{:S(2)}) collective-permute-start(bf16[768,768]{1,0:T(8,128)(2,1)} %get-tuple-element.107), channel_id=1, source_target_pairs={{0,8},{4,12},{8,0},{12,4},{16,24},{20,28},{24,16},{28,20},{1,9},{5... | collective-permute-start | bytes 3538952 | tf_op jit(solution)/shard_map/ppermute | solution.py:22
  214.1 35.1 %collective-permute-start.23 = (bf16[192,3072]{1,0:T(8,128)(2,1)}, bf16[192,3072]{1,0:T(8,128)(2,1)S(1)}, u32[]{:S(2)}, u32[]{:S(2)}) collective-permute-start(bf16[192,3072]{1,0:T(8,128)(2,1)} %get-tuple-element.108), channel_id=1, source_target_pairs={{0,1},{1,0},{2,3},{3,2},{4,5},{5,4},{6,7},{7,6},{8,9},{9,8},{10,11... | collective-permute-start | bytes 3538952 | tf_op jit(solution)/shard_map/ppermute | solution.py:22
  224.1 13.0 %collective-permute-start.24 = (bf16[512,768]{1,0:T(8,128)(2,1)}, bf16[512,768]{1,0:T(8,128)(2,1)S(1)}, u32[]{:S(2)}, u32[]{:S(2)}) collective-permute-start(bf16[512,768]{1,0:T(8,128)(2,1)} %bitcast.30), channel_id=1, source_target_pairs={{0,4},{4,0},{8,12},{12,8},{16,20},{20,16},{24,28},{28,24},{1,5},{5... | collective-permute-start | bytes 2359304 | tf_op jit(solution)/shard_map/ppermute | solution.py:22
  224.1 12.0 %collective-permute-start.19 = (f32[80,768]{1,0:T(8,128)}, f32[80,768]{1,0:T(8,128)S(1)}, u32[]{:S(2)}, u32[]{:S(2)}) collective-permute-start(f32[80,768]{1,0:T(8,128)} %get-tuple-element.158), channel_id=1, source_target_pairs={{0,16},{4,20},{8,24},{12,28},{16,0},{20,4},{24,8},{28,12},{1,17},{... | collective-permute-start | bytes 737288 | tf_op jit(solution)/shard_map/ppermute | solution.py:22
  231.7 29.0 %collective-permute-start.29 = (bf16[576,768]{1,0:T(8,128)(2,1)}, bf16[576,768]{1,0:T(8,128)(2,1)}, u32[]{:S(2)}, u32[]{:S(2)}) collective-permute-start(bf16[576,768]{1,0:T(8,128)(2,1)} %get-tuple-element.120), channel_id=1, source_target_pairs={{0,8},{4,12},{8,0},{12,4},{16,24},{20,28},{24,16},{28,20},{1,9},{5... | collective-permute-start | bytes 2654216 | tf_op jit(solution)/shard_map/ppermute | solution.py:22
  255.6 13.0 %collective-permute-start.28 = (bf16[256,768]{1,0:T(8,128)(2,1)}, bf16[256,768]{1,0:T(8,128)(2,1)S(1)}, u32[]{:S(2)}, u32[]{:S(2)}) collective-permute-start(bf16[256,768]{1,0:T(8,128)(2,1)} %get-tuple-element.119), channel_id=1, source_target_pairs={{0,8},{4,12},{8,0},{12,4},{16,24},{20,28},{24,16},{28,20},{1,9},{5... | collective-permute-start | bytes 1179656 | tf_op jit(solution)/shard_map/ppermute | solution.py:22
  257.1 16.9 %collective-permute-start.25 = (bf16[384,768]{1,0:T(8,128)(2,1)}, bf16[384,768]{1,0:T(8,128)(2,1)S(1)}, u32[]{:S(2)}, u32[]{:S(2)}) collective-permute-start(bf16[384,768]{1,0:T(8,128)(2,1)} %get-tuple-element.111), channel_id=1, source_target_pairs={{0,16},{4,20},{8,24},{12,28},{16,0},{20,4},{24,8},{28,12},{1,17},{... | collective-permute-start | bytes 1769480 | tf_op jit(solution)/shard_map/ppermute | solution.py:22
  258.7 26.6 %collective-permute-start.26 = (bf16[96,3072]{1,0:T(8,128)(2,1)}, bf16[96,3072]{1,0:T(8,128)(2,1)S(1)}, u32[]{:S(2)}, u32[]{:S(2)}) collective-permute-start(bf16[96,3072]{1,0:T(8,128)(2,1)} %get-tuple-element.112), channel_id=1, source_target_pairs={{0,2},{1,3},{2,0},{3,1},{4,6},{5,7},{6,4},{7,5},{8,10},{9,11},{10,... | collective-permute-start | bytes 1769480 | tf_op jit(solution)/shard_map/ppermute | solution.py:22
  272.5 25.0 %collective-permute-start.32 = (bf16[416,768]{1,0:T(8,128)(2,1)}, bf16[416,768]{1,0:T(8,128)(2,1)S(1)}, u32[]{:S(2)}, u32[]{:S(2)}) collective-permute-start(bf16[416,768]{1,0:T(8,128)(2,1)} %get-tuple-element.124), channel_id=1, source_target_pairs={{0,16},{4,20},{8,24},{12,28},{16,0},{20,4},{24,8},{28,12},{1,17},{... | collective-permute-start | bytes 1916936 | tf_op jit(solution)/shard_map/ppermute | solution.py:22
  288.9 7.2 %collective-permute-start.30 = (bf16[192,768]{1,0:T(8,128)(2,1)}, bf16[192,768]{1,0:T(8,128)(2,1)S(1)}, u32[]{:S(2)}, u32[]{:S(2)}) collective-permute-start(bf16[192,768]{1,0:T(8,128)(2,1)} %get-tuple-element.122), channel_id=1, source_target_pairs={{0,1},{1,0},{2,3},{3,2},{4,5},{5,4},{6,7},{7,6},{8,9},{9,8},{10,11... | collective-permute-start | bytes 884744 | tf_op jit(solution)/shard_map/ppermute | solution.py:22
  288.9 8.6 %collective-permute-start.31 = (bf16[192,768]{1,0:T(8,128)(2,1)}, bf16[192,768]{1,0:T(8,128)(2,1)S(1)}, u32[]{:S(2)}, u32[]{:S(2)}) collective-permute-start(bf16[192,768]{1,0:T(8,128)(2,1)} %get-tuple-element.123), channel_id=1, source_target_pairs={{0,8},{4,12},{8,0},{12,4},{16,24},{20,28},{24,16},{28,20},{1,9},{5... | collective-permute-start | bytes 884744 | tf_op jit(solution)/shard_map/ppermute | solution.py:22
  301.4 7.5 %collective-permute-start.36 = (bf16[96,768]{1,0:T(8,128)(2,1)}, bf16[96,768]{1,0:T(8,128)(2,1)S(1)}, u32[]{:S(2)}, u32[]{:S(2)}) collective-permute-start(bf16[96,768]{1,0:T(8,128)(2,1)} %get-tuple-element.132), channel_id=1, source_target_pairs={{0,16},{4,20},{8,24},{12,28},{16,0},{20,4},{24,8},{28,12},{1,17},{... | collective-permute-start | bytes 442376 | tf_op jit(solution)/shard_map/ppermute | solution.py:22
  302.7 11.1 %collective-permute-start.33 = (bf16[208,768]{1,0:T(8,128)(2,1)}, bf16[208,768]{1,0:T(8,128)(2,1)S(1)}, u32[]{:S(2)}, u32[]{:S(2)}) collective-permute-start(bf16[208,768]{1,0:T(8,128)(2,1)} %get-tuple-element.126), channel_id=1, source_target_pairs={{0,1},{1,0},{2,3},{3,2},{4,5},{5,4},{6,7},{7,6},{8,9},{9,8},{10,11... | collective-permute-start | bytes 958472 | tf_op jit(solution)/shard_map/ppermute | solution.py:22
  305.6 12.9 %collective-permute-start.35 = (bf16[96,768]{1,0:T(8,128)(2,1)}, bf16[96,768]{1,0:T(8,128)(2,1)S(1)}, u32[]{:S(2)}, u32[]{:S(2)}) collective-permute-start(bf16[96,768]{1,0:T(8,128)(2,1)} %get-tuple-element.130), channel_id=1, source_target_pairs={{0,2},{1,3},{2,0},{3,1},{4,6},{5,7},{6,4},{7,5},{8,10},{9,11},{10,... | collective-permute-start | bytes 442376 | tf_op jit(solution)/shard_map/ppermute | solution.py:22
  316.4 7.4 %collective-permute-start.34 = (bf16[104,768]{1,0:T(8,128)(2,1)}, bf16[104,768]{1,0:T(8,128)(2,1)S(1)}, u32[]{:S(2)}, u32[]{:S(2)}) collective-permute-start(bf16[104,768]{1,0:T(8,128)(2,1)} %get-tuple-element.128), channel_id=1, source_target_pairs={{0,2},{1,3},{2,0},{3,1},{4,6},{5,7},{6,4},{7,5},{8,10},{9,11},{10,... | collective-permute-start | bytes 479240 | tf_op jit(solution)/shard_map/ppermute | solution.py:22
  (45 other events, 310.5 us)
